TPU v7x, 32 devices: a whole 2x2x4 slice. The times are simulated.
32 devices in a mesh: dp: 16 (over z, y, x), tensor: 2 (over core).
Axes of the slice: x: 2, y: 2, z: 4, core: 2. Of those that a mesh axis runs over, the one named last changes fastest.
Arguments:
- layer_input: bfloat16 [16, 1024, 768], P('dp', 'tensor'), may hold values from -6 to 6
- cotangent: bfloat16 [16, 1024, 768], P('dp', 'tensor'), may hold values from -6 to 6
- lengths: int32 [16], P('dp'), may hold values from 256 to 1024, as said below
- w_qkv: bfloat16 [2, 768, 3, 768], P(None, 'dp', None, 'tensor'), may hold values from -0.21875 to 0.21875
- w_out: bfloat16 [2, 768, 768], P(None, 'tensor', 'dp'), may hold values from -0.625 to 0.625
- w_up: bfloat16 [2, 768, 3072], P(None, 'dp', 'tensor'), may hold values from -0.21875 to 0.21875
- w_down: bfloat16 [2, 3072, 768], P(None, 'tensor', 'dp'), may hold values from -0.109375 to 0.109375
- vec_bias: float32 [2, 6, 768], P(None, None, ('dp', 'tensor')), may hold values from -2 to 2
- norm_gain: float32 [2, 2, 768], P(None, None, ('dp', 'tensor')), may hold values from 0.5 to 1.5
- bias_up: float32 [2, 3072], P(None, ('dp', 'tensor')), may hold values from -2 to 2
- seg_pos: float32 [8, 768], P(None, ('dp', 'tensor')), may hold values from -3 to 3
Outputs:
- output: bfloat16 [16, 1024, 768], P('dp', 'tensor')
- grad_input: float32 [16, 1024, 768], P('dp', 'tensor')
- grad_w_qkv: float32 [2, 768, 3, 768], P(None, 'dp', None, 'tensor')
- grad_w_out: float32 [2, 768, 768], P(None, 'tensor', 'dp')
- grad_w_up: float32 [2, 768, 3072], P(None, 'dp', 'tensor')
- grad_w_down: float32 [2, 3072, 768], P(None, 'tensor', 'dp')
- grad_vec_bias: float32 [2, 6, 768], P(None, None, ('dp', 'tensor'))
- grad_norm_gain: float32 [2, 2, 768], P(None, None, ('dp', 'tensor'))
- grad_bias_up: float32 [2, 3072], P(None, ('dp', 'tensor'))
- grad_seg_pos: float32 [8, 768], P(None, ('dp', 'tensor'))
Inputs may be any that keep to these rules, and one draw needn't show every extreme that they name: `lengths`: valid slots are the first ones of a sequence; every draw holds a sequence of 1024 valid slots and one of 256.
All inputs are finite; a program needn't handle non-finite values.
Results may differ from a plain program's by a relative error of at most 0.02.
Values may be sent and summed in bfloat16 or wider, within the bound.
No kernel may reach another device: no remote copies, remote signals or barrier semaphores. Data moves between devices by JAX's collectives and lax.ppermute only.
A program may use at most 192 MiB of HBM per device.

v0:
```python
import math

import jax
import jax.numpy as jnp
from jax import lax
from jax.sharding import PartitionSpec as P

HD = 64
SEG = 128


NEG_FILL = -1000000000.0
EPS_NORM = 1e-06


def layer_norm(values, gain_vec, shift_vec):
    centred = values - jnp.mean(values, axis=-1, keepdims=True)
    spread_sq = jnp.mean(centred * centred, axis=-1, keepdims=True)
    return centred * lax.rsqrt(spread_sq + EPS_NORM) * gain_vec + shift_vec


def gelu_exact(values):
    return jax.nn.gelu(values, approximate=False)


def gather_rows(values):
    return lax.all_gather(values, "tensor", axis=1, tiled=True)


def sum_rows(values):
    return lax.psum_scatter(values, "tensor", scatter_dimension=1, tiled=True)


def block_weights(index, mats, vec_full, gain_full, up_full, part_index):
    w_qkv_b, w_out_b, w_up_b, w_down_b = mats
    local_width = w_qkv_b.shape[2]
    hidden_local = w_up_b.shape[1]
    bias_query = lax.dynamic_slice_in_dim(vec_full[index, 0], part_index * local_width, local_width)
    bias_value = lax.dynamic_slice_in_dim(vec_full[index, 1], part_index * local_width, local_width)
    bias_hidden = lax.dynamic_slice_in_dim(up_full[index], part_index * hidden_local, hidden_local)
    return (
        w_qkv_b,
        w_out_b,
        w_up_b,
        w_down_b,
        bias_query,
        bias_value,
        vec_full[index, 2],
        vec_full[index, 3],
        vec_full[index, 4],
        vec_full[index, 5],
        gain_full[index, 0],
        gain_full[index, 1],
        bias_hidden,
    )


def masked_scores(query_b, key_b, key_valid, shape_four):
    raw_scores = jnp.einsum(
        "grhe,gshe->ghrs",
        query_b.reshape(shape_four),
        key_b.reshape(shape_four),
        preferred_element_type=jnp.float32,
    ) * HD ** (-0.5)
    return jnp.where(key_valid[:, None, None, :], raw_scores, NEG_FILL)


def block_forward(inputs, key_valid, groups, width_rows, weights):
    (
        w_qkv_b,
        w_out_b,
        w_up_b,
        w_down_b,
        bias_query,
        bias_value,
        bias_attn,
        bias_mlp,
        shift_one,
        shift_two,
        gain_one,
        gain_two,
        bias_hidden,
    ) = weights
    model_dim = inputs.shape[2]
    gathered = gather_rows(inputs.astype(jnp.bfloat16))
    full_shape = gathered.shape
    flat_rows = gathered.reshape(-1, model_dim)
    total_rows = flat_rows.shape[0]
    projected = jnp.einsum("nd,dke->nke", flat_rows, w_qkv_b, preferred_element_type=jnp.float32)
    local_width = projected.shape[2]
    shape_four = (groups, width_rows, local_width // HD, HD)
    query_b = (projected[:, 0] + bias_query).astype(jnp.bfloat16)
    key_b = projected[:, 1].astype(jnp.bfloat16)
    value_b = (projected[:, 2] + bias_value).astype(jnp.bfloat16)
    scores = masked_scores(query_b, key_b, key_valid, shape_four)
    peak_val = jnp.max(scores, axis=-1, keepdims=True)
    expo_val = jnp.exp(scores - peak_val)
    row_total = jnp.sum(expo_val, axis=-1, keepdims=True)
    probs_low = (expo_val / row_total).astype(jnp.bfloat16)
    log_total = peak_val + jnp.log(row_total)
    attended = (
        jnp.einsum(
            "ghrs,gshe->grhe",
            probs_low,
            value_b.reshape(shape_four),
            preferred_element_type=jnp.float32,
        )
        .astype(jnp.bfloat16)
        .reshape(total_rows, local_width)
    )
    partial_attn = jnp.dot(attended, w_out_b, preferred_element_type=jnp.float32).reshape(
        full_shape
    )
    first_sum = sum_rows(partial_attn) + bias_attn + inputs
    first = layer_norm(first_sum, gain_one, shift_one)
    hidden_rows = gather_rows(first.astype(jnp.bfloat16)).reshape(total_rows, model_dim)
    pre_act = jnp.dot(hidden_rows, w_up_b, preferred_element_type=jnp.float32) + bias_hidden
    act_low = gelu_exact(pre_act).astype(jnp.bfloat16)
    partial_mlp = jnp.dot(act_low, w_down_b, preferred_element_type=jnp.float32).reshape(full_shape)
    second_sum = sum_rows(partial_mlp) + bias_mlp + first
    result = layer_norm(second_sum, gain_two, shift_two)
    saved = (
        first_sum,
        second_sum,
        flat_rows,
        query_b,
        key_b,
        value_b,
        log_total,
        attended,
        hidden_rows,
        pre_act,
        act_low,
    )
    return (result, saved)


def block_backward(grad_out, saved, key_valid, groups, width_rows, weights):
    (
        w_qkv_b,
        w_out_b,
        w_up_b,
        w_down_b,
        bias_query,
        bias_value,
        bias_attn,
        bias_mlp,
        shift_one,
        shift_two,
        gain_one,
        gain_two,
        bias_hidden,
    ) = weights
    (
        first_sum,
        second_sum,
        flat_rows,
        query_b,
        key_b,
        value_b,
        log_total,
        attended,
        hidden_rows,
        pre_act,
        act_low,
    ) = saved
    model_dim = grad_out.shape[2]
    total_rows = flat_rows.shape[0]
    local_width = query_b.shape[1]
    shape_four = (groups, width_rows, local_width // HD, HD)
    unused_second, second_pull = jax.vjp(layer_norm, second_sum, gain_two, shift_two)
    grad_second, grad_gain_two, grad_shift_two = second_pull(grad_out)
    grad_bias_mlp = jnp.sum(grad_second, axis=(0, 1))
    grad_mlp_full = gather_rows(grad_second.astype(jnp.bfloat16))
    full_shape = grad_mlp_full.shape
    grad_mlp_rows = grad_mlp_full.reshape(total_rows, model_dim)
    grad_w_down = jnp.einsum(
        "nf,nd->fd", act_low, grad_mlp_rows, preferred_element_type=jnp.float32
    )
    grad_act = jnp.einsum("nd,fd->nf", grad_mlp_rows, w_down_b, preferred_element_type=jnp.float32)
    unused_gelu, gelu_pull = jax.vjp(gelu_exact, pre_act)
    grad_pre = gelu_pull(grad_act)[0].astype(jnp.bfloat16)
    grad_bias_hidden = jnp.sum(grad_pre.astype(jnp.float32), axis=0)
    grad_w_up = jnp.einsum("nd,nf->df", hidden_rows, grad_pre, preferred_element_type=jnp.float32)
    grad_hidden = jnp.einsum(
        "nf,df->nd", grad_pre, w_up_b, preferred_element_type=jnp.float32
    ).reshape(full_shape)
    grad_first = sum_rows(grad_hidden) + grad_second
    unused_first, first_pull = jax.vjp(layer_norm, first_sum, gain_one, shift_one)
    grad_first_sum, grad_gain_one, grad_shift_one = first_pull(grad_first)
    grad_bias_attn = jnp.sum(grad_first_sum, axis=(0, 1))
    grad_attn_rows = gather_rows(grad_first_sum.astype(jnp.bfloat16)).reshape(total_rows, model_dim)
    grad_w_out = jnp.einsum(
        "nh,nd->hd", attended, grad_attn_rows, preferred_element_type=jnp.float32
    )
    grad_attended = (
        jnp.einsum("nd,hd->nh", grad_attn_rows, w_out_b, preferred_element_type=jnp.float32)
        .astype(jnp.bfloat16)
        .reshape(shape_four)
    )
    scores = masked_scores(query_b, key_b, key_valid, shape_four)
    probs = jnp.exp(scores - log_total)
    probs_low = probs.astype(jnp.bfloat16)
    grad_value = jnp.einsum(
        "ghrs,grhe->gshe", probs_low, grad_attended, preferred_element_type=jnp.float32
    )
    grad_probs = jnp.einsum(
        "grhe,gshe->ghrs",
        grad_attended,
        value_b.reshape(shape_four),
        preferred_element_type=jnp.float32,
    )
    inner_sum = jnp.sum(grad_probs * probs, axis=-1, keepdims=True)
    grad_scores = jnp.where(
        key_valid[:, None, None, :], probs * (grad_probs - inner_sum), 0.0
    ).astype(jnp.bfloat16)
    grad_query = jnp.einsum(
        "ghrs,gshe->grhe",
        grad_scores,
        key_b.reshape(shape_four),
        preferred_element_type=jnp.float32,
    ) * HD ** (-0.5)
    grad_key = jnp.einsum(
        "ghrs,grhe->gshe",
        grad_scores,
        query_b.reshape(shape_four),
        preferred_element_type=jnp.float32,
    ) * HD ** (-0.5)
    grad_proj = jnp.stack(
        [
            grad_query.reshape(total_rows, local_width),
            grad_key.reshape(total_rows, local_width),
            grad_value.reshape(total_rows, local_width),
        ],
        axis=1,
    ).astype(jnp.bfloat16)
    grad_bias_query = jnp.sum(grad_proj[:, 0].astype(jnp.float32), axis=0)
    grad_bias_value = jnp.sum(grad_proj[:, 2].astype(jnp.float32), axis=0)
    grad_w_qkv = jnp.einsum("nd,nke->dke", flat_rows, grad_proj, preferred_element_type=jnp.float32)
    grad_rows = jnp.einsum(
        "nke,dke->nd", grad_proj, w_qkv_b, preferred_element_type=jnp.float32
    ).reshape(full_shape)
    grad_inputs = sum_rows(grad_rows) + grad_first_sum
    mats_grad = (grad_w_qkv, grad_w_out, grad_w_up, grad_w_down)
    vecs_grad = (
        grad_bias_query,
        grad_bias_value,
        grad_bias_attn,
        grad_bias_mlp,
        grad_shift_one,
        grad_shift_two,
        grad_gain_one,
        grad_gain_two,
        grad_bias_hidden,
    )
    return (grad_inputs, mats_grad, vecs_grad)


def place_slice(values, width, part_index):
    return lax.dynamic_update_slice(
        jnp.zeros((width,), jnp.float32), values, (part_index * values.shape[0],)
    )


def vector_rows(vecs_grad, model_dim, hidden_width, part_index, factor):
    (
        grad_bias_query,
        grad_bias_value,
        grad_bias_attn,
        grad_bias_mlp,
        grad_shift_one,
        grad_shift_two,
        grad_gain_one,
        grad_gain_two,
        grad_bias_hidden,
    ) = vecs_grad
    bias_rows = (
        jnp.stack(
            [
                place_slice(grad_bias_query, model_dim, part_index),
                place_slice(grad_bias_value, model_dim, part_index),
                grad_bias_attn,
                grad_bias_mlp,
                grad_shift_one,
                grad_shift_two,
            ]
        )
        * factor
    )
    gain_rows = jnp.stack([grad_gain_one, grad_gain_two]) * factor
    hidden_row = place_slice(grad_bias_hidden, hidden_width, part_index) * factor
    return (bias_rows, gain_rows, hidden_row)


def local(
    layer_input,
    cotangent,
    lengths,
    w_qkv,
    w_out,
    w_up,
    w_down,
    vec_bias,
    norm_gain,
    bias_up,
    seg_pos,
):
    tensor_count = lax.axis_size("tensor")
    tensor_index = lax.axis_index("tensor")
    data_count = lax.axis_size("dp")
    seqs_here, half_rows, model_dim = layer_input.shape
    full_len = half_rows * tensor_count
    segment_count = full_len // SEG
    seg_here = half_rows // SEG
    vec_full, gain_full, up_full, segpos_full = (
        lax.all_gather(vec_bias, ("dp", "tensor"), axis=2, tiled=True),
        lax.all_gather(norm_gain, ("dp", "tensor"), axis=2, tiled=True),
        lax.all_gather(bias_up, ("dp", "tensor"), axis=1, tiled=True),
        lax.all_gather(seg_pos, ("dp", "tensor"), axis=1, tiled=True),
    )
    hidden_width = up_full.shape[1]
    whole_set = (
        lax.all_gather(w_qkv, "dp", axis=1, tiled=True),
        lax.all_gather(w_out, "dp", axis=2, tiled=True),
        lax.all_gather(w_up, "dp", axis=1, tiled=True),
        lax.all_gather(w_down, "dp", axis=2, tiled=True),
    )
    mats_one = tuple((piece[0] for piece in whole_set))
    positions = jnp.arange(full_len, dtype=jnp.int32)
    valid_full = positions[None, :] < lengths[:, None]
    key_valid_two = valid_full[:, ::SEG]
    local_valid = lax.dynamic_slice_in_dim(valid_full, tensor_index * half_rows, half_rows, axis=1)
    local_mask = local_valid.astype(jnp.float32)[..., None]
    key_valid_one = valid_full.reshape(seqs_here * segment_count, SEG)
    groups_one = seqs_here * segment_count
    weights_one = block_weights(0, mats_one, vec_full, gain_full, up_full, tensor_index)
    first_out, saved_one = block_forward(
        layer_input.astype(jnp.float32), key_valid_one, groups_one, SEG, weights_one
    )
    mats_two = tuple((piece[1] for piece in whole_set))
    weights_two = block_weights(1, mats_two, vec_full, gain_full, up_full, tensor_index)
    seg_local = lax.dynamic_slice_in_dim(segpos_full, tensor_index * seg_here, seg_here, axis=0)
    cls_in = first_out[:, ::SEG, :] + seg_local[None]
    cls_out, saved_two = block_forward(cls_in, key_valid_two, seqs_here, segment_count, weights_two)
    combined = first_out.at[:, ::SEG, :].set(cls_out) * local_mask
    output = combined.astype(jnp.bfloat16)
    scale_one = 1.0 / math.sqrt(seqs_here * data_count * full_len)
    scale_two = 1.0 / math.sqrt(seqs_here * data_count * segment_count)
    grad_out = cotangent.astype(jnp.float32) * local_mask
    grad_cls_in, mats_grad_two, vecs_grad_two = block_backward(
        grad_out[:, ::SEG, :], saved_two, key_valid_two, seqs_here, segment_count, weights_two
    )
    grad_seg_local = jnp.sum(grad_cls_in, axis=0)
    grad_first_out = grad_out.at[:, ::SEG, :].set(grad_cls_in)
    grad_input, mats_grad_one, vecs_grad_one = block_backward(
        grad_first_out, saved_one, key_valid_one, groups_one, SEG, weights_one
    )
    scaled_one = tuple((piece * scale_one for piece in mats_grad_one))
    reduced = (
        lax.psum_scatter(
            jnp.stack([scaled_one[0], mats_grad_two[0] * scale_two]),
            "dp",
            scatter_dimension=1,
            tiled=True,
        ),
        lax.psum_scatter(
            jnp.stack([scaled_one[1], mats_grad_two[1] * scale_two]),
            "dp",
            scatter_dimension=2,
            tiled=True,
        ),
        lax.psum_scatter(
            jnp.stack([scaled_one[2], mats_grad_two[2] * scale_two]),
            "dp",
            scatter_dimension=1,
            tiled=True,
        ),
        lax.psum_scatter(
            jnp.stack([scaled_one[3], mats_grad_two[3] * scale_two]),
            "dp",
            scatter_dimension=2,
            tiled=True,
        ),
    )
    bias_one, gains_one, hidden_one = vector_rows(
        vecs_grad_one, model_dim, hidden_width, tensor_index, scale_one
    )
    bias_two, gains_two, hidden_two = vector_rows(
        vecs_grad_two, model_dim, hidden_width, tensor_index, scale_two
    )
    grad_seg_full = (
        lax.dynamic_update_slice(
            jnp.zeros((segment_count, model_dim), jnp.float32),
            grad_seg_local,
            (tensor_index * seg_here, 0),
        )
        * scale_two
    )
    grad_vec, grad_gain, grad_up_vec, grad_segment = (
        lax.psum_scatter(
            jnp.stack([bias_one, bias_two]), ("dp", "tensor"), scatter_dimension=2, tiled=True
        ),
        lax.psum_scatter(
            jnp.stack([gains_one, gains_two]), ("dp", "tensor"), scatter_dimension=2, tiled=True
        ),
        lax.psum_scatter(
            jnp.stack([hidden_one, hidden_two]), ("dp", "tensor"), scatter_dimension=1, tiled=True
        ),
        lax.psum_scatter(grad_seg_full, ("dp", "tensor"), scatter_dimension=1, tiled=True),
    )
    return (
        output,
        grad_input,
        reduced[0],
        reduced[1],
        reduced[2],
        reduced[3],
        grad_vec,
        grad_gain,
        grad_up_vec,
        grad_segment,
    )


def solution(mesh):
    return jax.shard_map(
        local,
        mesh=mesh,
        in_specs=(
            P("dp", "tensor", None),
            P("dp", "tensor", None),
            P("dp"),
            P(None, "dp", None, "tensor"),
            P(None, "tensor", "dp"),
            P(None, "dp", "tensor"),
            P(None, "tensor", "dp"),
            P(None, None, ("dp", "tensor")),
            P(None, None, ("dp", "tensor")),
            P(None, ("dp", "tensor")),
            P(None, ("dp", "tensor")),
        ),
        out_specs=(
            P("dp", "tensor", None),
            P("dp", "tensor", None),
            P(None, "dp", None, "tensor"),
            P(None, "tensor", "dp"),
            P(None, "dp", "tensor"),
            P(None, "tensor", "dp"),
            P(None, None, ("dp", "tensor")),
            P(None, None, ("dp", "tensor")),
            P(None, ("dp", "tensor")),
            P(None, ("dp", "tensor")),
        ),
        check_vma=False,
    )
```

profile of v0, /device:TPU:0, one launch (start us, length us, event | category | flops | bytes accessed | tf_op | source)
XLA Modules:
  0.0 1453.2 jit_solution(11749735560862111781)
XLA Ops:
  11.4 45.7 %all_gather.50 = f32[2,6,768]{1,0,2:T(2,128)S(1)} all-gather(f32[2,6,24]{1,0,2:T(2,128)S(1)} %copy.143), channel_id=1, replica_groups=mesh['dp'=16,'tensor'=2] {'dp','tensor'}, dimensions={2}, use_global_device_ids=true | all-gather | bytes 38016 | tf_op jit(solution)/shard_map/all_gather | solution.py:316
  57.1 20.8 %fusion.200 = (f32[1,1,768]{1,0,2:T(1,128)S(1)}, f32[1,1,768]{1,0,2:T(1,128)}, f32[768]{0:T(1024)S(1)}, f32[768]{0:T(1024)}, f32[768]{0:T(1024)}, /*index=5*/f32...) fusion(f32[2,6,768]{1,0,2:T(2,128)S(1)} %all_gather.50), kind=kLoop, calls=%fused_computation.358 | loop fusion | bytes 73728 | tf_op jit(solution)/shard_map/slice | solution.py:39
  79.6 18.1 %all-gather.13.cloned.1.call-done = bf16[2,768,3,384]{3,1,2,0:T(8,128)(2,1)} async-done(((bf16[2,48,3,384]{3,1,2,0:T(8,128)(2,1)}), bf16[2,768,3,384]{3,1,2,0:T(8,128)(2,1)}) %all-gather.13.cloned.1.call-update) | async-done | bytes 3538960 | tf_op jit(solution)/shard_map/all_gather | solution.py:323
  97.6 4.2 fusion.41
  114.7 40.2 %all-gather.15.cloned.1.call-done = bf16[2,384,768]{1,2,0:T(8,128)(2,1)} async-done(((bf16[2,384,48]{1,2,0:T(8,128)(2,1)}), bf16[2,384,768]{1,2,0:T(8,128)(2,1)}) %all-gather.15.cloned.1.call-update) | async-done | bytes 1179664 | tf_op jit(solution)/shard_map/all_gather | solution.py:324
  154.8 3.8 convolution_bitcast_fusion.1
  159.4 42.2 %all_gather.52 = f32[2,2,768]{1,0,2:T(2,128)S(1)} all-gather(f32[2,2,24]{1,0,2:T(2,128)S(1)} %copy.151), channel_id=1, replica_groups=mesh['dp'=16,'tensor'=2] {'dp','tensor'}, dimensions={2}, use_global_device_ids=true | all-gather | bytes 12672 | tf_op jit(solution)/shard_map/all_gather | solution.py:317
  201.6 9.7 slice_reduce_fusion.1
  215.5 38.0 %all-gather = f32[32,96,2]{1,2,0:T(2,128)S(1)} all-gather(f32[1,96,2]{1,2,0:T(2,128)S(1)} %bitcast.321), channel_id=1, replica_groups=mesh['dp'=16,'tensor'=2] {'dp','tensor'}, dimensions={0}, use_global_device_ids=true | all-gather | bytes 25344 | tf_op jit(solution)/shard_map/all_gather | solution.py:318
  253.6 9.8 all-gather.17.cloned.1.call-done
  263.4 20.0 %multiply_convert_fusion = (bf16[1024,1536]{1,0:T(8,128)(2,1)}, f32[1024,1536]{1,0:T(8,128)}, f32[1024,1536]{1,0:T(8,128)}) fusion(f32[1536]{0:T(1024)S(1)} %dynamic-slice_reduce_fusion.5, bf16[2,768,1536]{2,1,0:T(8,128)(2,1)} %all-gather.19.cloned.1.call-done, bf16[1,1024,768]{2,1,0:T(8,128)(2,1)} %all-gather.17.cloned.1.call-done), kind=kOutput, calls=%fused_computation.11 | convolution fusion | flops 2519728128 | bytes 19666944 | tf_op jit(solution)/shard_map/dot_general | solution.py:117
  283.4 63.6 %all-gather.21.cloned.1.call-done = bf16[2,1536,768]{1,2,0:T(8,128)(2,1)} async-done(((bf16[2,1536,48]{1,2,0:T(8,128)(2,1)}), bf16[2,1536,768]{1,2,0:T(8,128)(2,1)}) %all-gather.21.cloned.1.call-update) | async-done | bytes 4718608 | tf_op jit(solution)/shard_map/all_gather | solution.py:326
  347.0 6.9 fusion.26
  354.6 39.5 %all-gather.1 = f32[32,24,8]{1,2,0:T(8,128)S(1)} all-gather(f32[1,24,8]{1,2,0:T(8,128)S(1)} %bitcast.320), channel_id=1, replica_groups=mesh['dp'=16,'tensor'=2] {'dp','tensor'}, dimensions={0}, use_global_device_ids=true | all-gather | bytes 25344 | tf_op jit(solution)/shard_map/all_gather | solution.py:319
  410.3 3.7 all-reduce
  418.4 2.4 fusion.89
  420.8 3.4 all-reduce.1
  424.7 3.2 scatter_custom_fusion
  427.8 3.9 convert_multiply_fusion
  440.0 3.8 all-reduce.2
  451.2 3.4 all-reduce.3
  454.7 3.2 scatter_custom_fusion.1
  463.0 6.0 all-gather.23.cloned.1.call-done
  469.0 10.2 convert_reduce_fusion
  480.9 6.0 fusion.27
  488.9 10.4 reduce-scatter.20.cloned.1.call-done
  499.4 2.7 multiply_reduce_fusion.1
  508.8 7.4 all-gather.25.cloned.1.call-done
  521.2 3.4 fusion.103
  526.8 5.2 fusion.74
  532.1 5.3 fusion.77
  543.9 2.7 copy.180
  551.1 5.5 convolution_bitcast_fusion
  562.6 2.7 multiply_bitcast_fusion.1
  565.4 4.3 pad_maximum_fusion.1
  569.7 15.1 %copy.191 = f32[2,1536,768]{1,0,2:T(2,128)} copy(f32[2,1536,768]{2,1,0:T(8,128)} %pad_maximum_fusion.1) | data formatting | bytes 18874368 | tf_op jit(solution)/shard_map/stack | solution.py:379
  584.7 2.5 fusion.58
  588.8 5.3 copy.190
  594.1 4.3 multiply_bitcast_fusion.5
  598.5 3.3 pad_maximum_fusion.2
  601.8 13.6 copy.189
  617.9 2.7 multiply_bitcast_fusion.3
  620.6 4.6 pad_maximum_fusion
  628.5 118.6 %all-reduce.15.cloned.1.call-done = (f32[2,6,768]{2,0,1:T(2,128)}, f32[2,2,768]{2,1,0:T(2,128)}, f32[8,768]{1,0:T(8,128)}) async-done(((f32[2,6,768]{2,0,1:T(2,128)}, f32[2,2,768]{2,1,0:T(2,128)}, f32[8,768]{1,0:T(8,128)}), (f32[2,6,768]{2,0,1:T(2,128)}, f32[2,2,768]{2,1,0:T(2,128)}, f32[8,768]{1,0:T(8,128)})) %all-reduce.15.cloned.1.call-update) | async-done | bytes 73744
  751.2 12.1 reduce-scatter.22.cloned.1.call-done
  763.3 2.8 add_add_fusion.3
  766.0 503.5 %all-reduce.17.cloned.1.call-done = (f32[2,768,3,384]{3,0,2,1:T(2,128)}, f32[2,384,768]{1,0,2:T(2,128)}, f32[2,1536,768]{1,0,2:T(2,128)}) async-done(((f32[2,768,3,384]{3,0,2,1:T(2,128)}, f32[2,384,768]{1,0,2:T(2,128)}, f32[2,1536,768]{1,0,2:T(2,128)}), (f32[2,768,3,384]{3,0,2,1:T(2,128)}, f32[2,384,768]{1,0,2:T(2,128)}, f32[2,1536,768]{1,0,2:T(2,128)})) %all-reduce.17.cloned.1.call-update) | async-done | bytes 18874384
  1275.2 171.2 %reduce-scatter.24.cloned.1.call-done = f32[2,48,1536]{2,1,0:T(8,128)} async-done(((f32[2,768,1536]{2,1,0:T(8,128)}), f32[2,48,1536]{2,1,0:T(8,128)}) %reduce-scatter.24.cloned.1.call-update) | async-done | bytes 589840 | tf_op jit(solution)/shard_map/reduce_scatter | solution.py:372
  (355 shorter events, 115.0 us)
Async XLA Ops:
  7.2 72.4 %all-gather.11.cloned.1.call-start = ((), (), s32[]{:S(2)}) async-start(), calls=%async_computation.6 | async-start | bytes 2359296 | tf_op jit(solution)/shard_map/all_gather | solution.py:27
  7.9 89.7 %all-gather.13.cloned.1.call-start = ((), (), s32[]{:S(2)}) async-start(), calls=%async_computation.7 | async-start | bytes 3760128 | tf_op jit(solution)/shard_map/all_gather | solution.py:323
  8.7 146.2 %all-gather.15.cloned.1.call-start = ((), (), s32[]{:S(2)}) async-start(), calls=%async_computation.8 | async-start | bytes 1253376 | tf_op jit(solution)/shard_map/all_gather | solution.py:324
  9.4 201.9 %reduce-scatter.16.cloned.1.call-start = ((), (), s32[]{:S(2)}) async-start(), calls=%async_computation.9 | async-start | bytes 4718592 | tf_op jit(solution)/shard_map/reduce_scatter | solution.py:31
  114.7 44.0 %copy-start.13 = (bf16[8,128,6,64]{1,0,3,2:T(8,128)(2,1)}, bf16[8,128,6,64]{1,0,3,2:T(8,128)(2,1)S(1)}, u32[]{:S(2)}) copy-start(bf16[8,128,6,64]{1,0,3,2:T(8,128)(2,1)S(1)} %copy.150) | copy-start | bytes 2359300
  154.8 4.5 copy-start.53
  158.6 52.7 %copy-start.10 = (bf16[1,512,768]{2,1,0:T(8,128)(2,1)S(1)}, bf16[1,512,768]{2,1,0:T(8,128)(2,1)}, u32[]{:S(2)}) copy-start(bf16[1,512,768]{2,1,0:T(8,128)(2,1)} %param.11) | copy-start | bytes 2359300
  158.7 94.9 %all-gather.19.cloned.1.call-start = ((), (), s32[]{:S(2)}) async-start(), calls=%async_computation.11 | async-start | bytes 5013504 | tf_op jit(solution)/shard_map/all_gather | solution.py:325
  159.3 104.1 %all-gather.17.cloned.1.call-start = ((), (), s32[]{:S(2)}) async-start(), calls=%async_computation.10 | async-start | bytes 2359296 | tf_op jit(solution)/shard_map/all_gather | solution.py:27
  213.1 2.4 copy-start.54
  214.6 132.3 %all-gather.21.cloned.1.call-start = ((), (), s32[]{:S(2)}) async-start(), calls=%async_computation.12 | async-start | bytes 5013504 | tf_op jit(solution)/shard_map/all_gather | solution.py:326
  215.4 182.4 %reduce-scatter.18.cloned.1.call-start = ((), (), s32[]{:S(2)}) async-start(), calls=%async_computation.13 | async-start | bytes 4718592 | tf_op jit(solution)/shard_map/reduce_scatter | solution.py:31
  253.6 29.8 %copy-start.50 = (f32[1536]{0:T(1024)}, f32[1536]{0:T(1024)S(1)}, u32[]{:S(2)}) copy-start(f32[1536]{0:T(1024)S(1)} %dynamic-slice_reduce_fusion.5) | copy-start | bytes 18436
  353.9 41.0 %copy-start.16 = (f32[1,1,768]{1,0,2:T(1,128)S(1)}, f32[1,1,768]{1,0,2:T(1,128)}, u32[]{:S(2)}) copy-start(f32[1,1,768]{1,0,2:T(1,128)} %get-tuple-element.108) | copy-start | bytes 9220
  353.9 42.6 %copy-start.59 = (u32[32]{0:T(128)S(1)}, u32[32]{0:T(128)}, u32[]{:S(2)}) copy-start(u32[32]{0:T(128)} %constant.223) | copy-start | bytes 388
  353.9 115.1 %all-gather.23.cloned.1.call-start = ((), (), s32[]{:S(2)}) async-start(), calls=%async_computation.14 | async-start | bytes 2359296 | tf_op jit(solution)/shard_map/all_gather | solution.py:27
  397.8 2.3 copy-start.42
  400.1 4.3 copy-start.31
  401.6 6.9 copy-start.60
  401.6 12.4 copy-start.49
  401.6 12.8 copy-start.43
  408.9 5.5 copy-start.36
  410.3 14.0 copy-start.48
  410.3 14.4 copy-start.35
  410.3 14.4 copy-start.47
  416.3 11.6 copy-start.33
  418.4 17.1 %copy-start.20 = (f32[8,1536]{1,0:T(8,128)}, f32[8,1536]{1,0:T(8,128)S(1)}, u32[]{:S(2)}) copy-start(f32[8,1536]{1,0:T(8,128)S(1)} %convolution_add_fusion) | copy-start | bytes 147460
  435.5 12.5 copy-start.38
  437.6 20.2 %copy-start.27 = (bf16[8,1536]{1,0:T(8,128)(2,1)}, bf16[8,1536]{1,0:T(8,128)(2,1)S(1)}, u32[]{:S(2)}) copy-start(bf16[8,1536]{1,0:T(8,128)(2,1)S(1)} %get-tuple-element.134) | copy-start | bytes 73732
  449.2 10.8 copy-start.26
  460.0 8.9 copy-start.51
  462.9 36.4 %reduce-scatter.20.cloned.1.call-start = ((), (), s32[]{:S(2)}) async-start(), calls=%async_computation.15 | async-start | bytes 4718592 | tf_op jit(solution)/shard_map/reduce_scatter | solution.py:31
  486.9 12.5 copy-start.41
  486.9 29.3 %all-gather.25.cloned.1.call-start = ((), (), s32[]{:S(2)}) async-start(), calls=%async_computation.16 | async-start | bytes 2359296 | tf_op jit(solution)/shard_map/all_gather | solution.py:27
  488.9 13.2 copy-start.46
  503.9 12.3 copy-start.14
  505.0 122.1 %reduce-scatter.26.cloned.1.call-start = ((), (), s32[]{:S(2)}) async-start(), calls=%async_computation.19 | async-start | bytes 1622016
  507.7 239.4 %all-reduce.15.cloned.1.call-start = ((), (), s32[]{:S(2)}) async-start(), calls=%async_computation.20 | async-start | bytes 147456
  519.8 4.9 copy-start.6
  543.9 7.3 copy-start.8
  551.1 212.2 %reduce-scatter.22.cloned.1.call-start = ((), (), s32[]{:S(2)}) async-start(), calls=%async_computation.17 | async-start | bytes 4718592 | tf_op jit(solution)/shard_map/reduce_scatter | solution.py:31
  556.7 712.9 %all-reduce.17.cloned.1.call-start = ((), (), s32[]{:S(2)}) async-start(), calls=%async_computation.21 | async-start | bytes 37748736
  557.4 2.8 copy-start.21
  557.4 2.8 copy-start.39
  560.3 2.4 copy-start.61
  584.7 2.5 copy-start.7
  615.4 831.1 %reduce-scatter.24.cloned.1.call-start = ((), (), s32[]{:S(2)}) async-start(), calls=%async_computation.18 | async-start | bytes 10027008 | tf_op jit(solution)/shard_map/reduce_scatter | solution.py:372
  625.2 138.1 %copy-start.3 = (f32[1,512,768]{2,1,0:T(8,128)S(1)}, f32[1,512,768]{2,1,0:T(8,128)}, u32[]{:S(2)}) copy-start(f32[1,512,768]{2,1,0:T(8,128)} %copy-done.2) | copy-start | bytes 4718596
  (30 other events, 42.0 us)
Sparse Core Ops, SparseCore 0:
  9.5 12.5 all-gather.10
  24.8 72.7 all-gather.12
  100.3 54.4 all-gather.14
  158.8 9.8 reduce-scatter.15
  171.2 81.5 all-gather.18
  254.8 8.4 all-gather.16
  266.1 80.8 all-gather.20
  354.0 9.8 reduce-scatter.17
  463.0 5.8 all-gather.22
  487.0 12.3 reduce-scatter.19
  505.1 11.0 all-gather.24
  521.3 99.0 reduce-scatter.25
  627.0 120.1 all-reduce.14
  749.2 13.9 reduce-scatter.21
  769.5 499.9 all-reduce.16
  1275.7 170.6 reduce-scatter.23
where the time goes:
time: 1460 us; the launch traced here: 1450 us
  waiting for transfers between devices  964 us (66%)
  blocking collectives  187 us (13%)
  local copies, waits for them, and re-layouts  122 us (8%)
  matrix products  110 us (8%)
  other arithmetic  50.2 us (3%)
  between operations  17.3 us (1%)
    unnamed x19, waiting for transfers between devices  626 us
    reduce_scatter x1, waiting for transfers between devices, local(): lax.psum_scatter(jnp.stack([scaled_one[2], mats_grad_two[2] * scale_two])...  171 us
    all_gather x1, waiting for transfers between devices, local(): lax.all_gather(w_down, 'dp', axis=2, tiled=True)  63.6 us
    all_gather x1, blocking collectives, local(): lax.all_gather(vec_bias, ('dp', 'tensor'), axis=2, tiled=True)  45.7 us
    all_gather x1, blocking collectives, local(): lax.all_gather(norm_gain, ('dp', 'tensor'), axis=2, tiled=True)  42.2 us
    all_gather x1, waiting for transfers between devices, local(): lax.all_gather(w_out, 'dp', axis=2, tiled=True)  40.2 us
    all_gather x1, blocking collectives, local(): lax.all_gather(seg_pos, ('dp', 'tensor'), axis=1, tiled=True)  39.5 us
    all_gather x1, blocking collectives, local(): lax.all_gather(bias_up, ('dp', 'tensor'), axis=1, tiled=True)  38 us
  transfers between devices with their start and end apart: 16, of which 11 were waited for; matrix products, arithmetic and copies ran while one was open for 14% of the time, Pallas kernels for 0%

commit v1 on v0

v1 whole, which is shorter than its diff:
```python
import functools
import math

import jax
import jax.numpy as jnp
from jax import lax
from jax.experimental import pallas as pl
from jax.experimental.pallas import tpu as pltpu
from jax.sharding import PartitionSpec as P

HD = 64
SEG = 128
NEG_FILL = -1000000000.0
EPS_NORM = 1e-06
BF = jnp.bfloat16
F32 = jnp.float32
INV_SQRT2 = 1.0 / math.sqrt(2.0)
INV_SQRT2PI = 1.0 / math.sqrt(2.0 * math.pi)
SM_SCALE = HD ** (-0.5)


def dot_nn(a, b):
    return lax.dot_general(a, b, (((1,), (0,)), ((), ())), preferred_element_type=F32)


def dot_nt(a, b):
    return lax.dot_general(a, b, (((1,), (1,)), ((), ())), preferred_element_type=F32)


def dot_tn(a, b):
    return lax.dot_general(a, b, (((0,), (0,)), ((), ())), preferred_element_type=F32)


def dot_exact(a, b):
    return lax.dot_general(
        a, b, (((1,), (0,)), ((), ())), precision=lax.Precision.HIGHEST, preferred_element_type=F32
    )


def swap_dp(values, bit, count):
    return lax.ppermute(values, "dp", [(i, i ^ (1 << bit)) for i in range(count)])


def swap_tensor(values):
    return lax.ppermute(values, "tensor", [(0, 1), (1, 0)])


def bit_orders(bits):
    if bits == 4:
        return ((3, 0, 1, 2), (3, 1, 2, 0), (3, 2, 0, 1))
    base = tuple(range(bits))
    return (base, base[1:] + base[:1], base[2:] + base[:2])


def gather_step(values, bit, bits, count):
    return jnp.concatenate([values, swap_dp(values, bit, count)], axis=bits - 1 - bit)


def gather_units(units, orders, bits, count):
    state = [unit.reshape((1,) * bits + unit.shape) for unit in units]
    for step in range(bits):
        state = [gather_step(v, orders[i][step], bits, count) for i, v in enumerate(state)]
    return [v.reshape((-1, v.shape[-1])) for v in state]


def scatter_unit(grad, order, bits, count):
    width = grad.shape[-1]
    v = grad.reshape((2,) * bits + (-1, width))
    for step, bit in enumerate(reversed(order)):
        axis = bits - 1 - bit
        send = lax.index_in_dim(v, 1, axis, keepdims=True)
        keep = lax.index_in_dim(v, 0, axis, keepdims=True).astype(F32)
        v = keep + swap_dp(send, bit, count).astype(F32)
        if step < bits - 1:
            v = v.astype(BF)
    return v.reshape((-1, width))


def sum_everywhere(values, bits, count):
    values = values + swap_tensor(values)
    for bit in range(bits):
        values = values + swap_dp(values, bit, count)
    return values


def pair_masks(rows):
    lane = lax.broadcasted_iota(jnp.int32, (rows, 2 * HD), 1)
    return lane < HD


def stack_heads(two, low_half):
    zero = jnp.zeros_like(two)
    return jnp.concatenate([jnp.where(low_half, two, zero), jnp.where(low_half, zero, two)], axis=0)


def merge_heads(stacked, low_half, rows):
    return jnp.where(low_half, stacked[:rows], stacked[rows:])


def pair_probs(q_stack, key_two, allowed):
    scores = dot_nt(q_stack, key_two) * SM_SCALE
    scores = jnp.where(allowed, scores, NEG_FILL)
    expo = jnp.exp(scores - jnp.max(scores, axis=-1, keepdims=True))
    return expo * (1.0 / jnp.sum(expo, axis=-1, keepdims=True))


def attn_fwd_kernel(count_ref, qkv_ref, out_ref):
    rows = qkv_ref.shape[0]
    width = out_ref.shape[1]
    low_half = pair_masks(rows)
    allowed = lax.broadcasted_iota(jnp.int32, (2 * rows, rows), 1) < count_ref[pl.program_id(0)]
    for pair in range(width // (2 * HD)):
        at = pair * 2 * HD
        q_stack = stack_heads(qkv_ref[:, at : at + 2 * HD], low_half)
        probs = pair_probs(q_stack, qkv_ref[:, width + at : width + at + 2 * HD], allowed)
        mixed = dot_nn(probs.astype(BF), qkv_ref[:, 2 * width + at : 2 * width + at + 2 * HD])
        out_ref[:, at : at + 2 * HD] = merge_heads(mixed, low_half, rows).astype(BF)


def attn_bwd_kernel(count_ref, qkv_ref, grad_ref, out_ref, sums_ref):
    rows = qkv_ref.shape[0]
    width = grad_ref.shape[1]
    low_half = pair_masks(rows)
    allowed = lax.broadcasted_iota(jnp.int32, (2 * rows, rows), 1) < count_ref[pl.program_id(0)]

    @pl.when(pl.program_id(0) == 0)
    def _():
        sums_ref[...] = jnp.zeros_like(sums_ref)

    def put(at, values):
        low = values.astype(BF)
        out_ref[:, at : at + 2 * HD] = low
        sums_ref[:, at : at + 2 * HD] += jnp.sum(low.astype(F32), axis=0, keepdims=True)

    for pair in range(width // (2 * HD)):
        at = pair * 2 * HD
        q_stack = stack_heads(qkv_ref[:, at : at + 2 * HD], low_half)
        key_two = qkv_ref[:, width + at : width + at + 2 * HD]
        value_two = qkv_ref[:, 2 * width + at : 2 * width + at + 2 * HD]
        g_stack = stack_heads(grad_ref[:, at : at + 2 * HD], low_half)
        probs = pair_probs(q_stack, key_two, allowed)
        grad_probs = dot_nt(g_stack, value_two)
        inner = jnp.sum(grad_probs * probs, axis=-1, keepdims=True)
        grad_scores = jnp.where(allowed, probs * (grad_probs - inner), 0.0).astype(BF)
        put(at, merge_heads(dot_nn(grad_scores, key_two), low_half, rows) * SM_SCALE)
        put(width + at, dot_tn(grad_scores, q_stack) * SM_SCALE)
        put(2 * width + at, dot_tn(probs.astype(BF), g_stack))


def attn_fwd(counts, qkv):
    rows, three = qkv.shape
    width = three // 3
    return pl.pallas_call(
        attn_fwd_kernel,
        grid_spec=pltpu.PrefetchScalarGridSpec(
            num_scalar_prefetch=1,
            grid=(rows // SEG,),
            in_specs=[pl.BlockSpec((SEG, three), lambda i, c: (i, 0))],
            out_specs=pl.BlockSpec((SEG, width), lambda i, c: (i, 0)),
        ),
        out_shape=jax.ShapeDtypeStruct((rows, width), BF),
        cost_estimate=pl.CostEstimate(
            flops=8 * rows * SEG * width, bytes_accessed=8 * rows * width, transcendentals=rows * SEG * width // HD
        ),
        name="attn_fwd",
    )(counts, qkv)


def attn_bwd(counts, qkv, grad):
    rows, three = qkv.shape
    width = three // 3
    return pl.pallas_call(
        attn_bwd_kernel,
        grid_spec=pltpu.PrefetchScalarGridSpec(
            num_scalar_prefetch=1,
            grid=(rows // SEG,),
            in_specs=[
                pl.BlockSpec((SEG, three), lambda i, c: (i, 0)),
                pl.BlockSpec((SEG, width), lambda i, c: (i, 0)),
            ],
            out_specs=[
                pl.BlockSpec((SEG, three), lambda i, c: (i, 0)),
                pl.BlockSpec((1, three), lambda i, c: (0, 0)),
            ],
        ),
        out_shape=[jax.ShapeDtypeStruct((rows, three), BF), jax.ShapeDtypeStruct((1, three), F32)],
        cost_estimate=pl.CostEstimate(
            flops=20 * rows * SEG * width, bytes_accessed=14 * rows * width, transcendentals=rows * SEG * width // HD
        ),
        name="attn_bwd",
    )(counts, qkv, grad)


def gelu_pair(pre):
    cdf = 0.5 * (1.0 + lax.erf(pre * INV_SQRT2))
    return pre * cdf, cdf + pre * (jnp.exp(-0.5 * pre * pre) * INV_SQRT2PI)


def up_kernel(rows_ref, w_ref, bias_ref, act_ref, slope_ref):
    pre = dot_nn(rows_ref[...], w_ref[...]) + bias_ref[...]
    act, slope = gelu_pair(pre)
    act_ref[...] = act.astype(BF)
    slope_ref[...] = slope.astype(BF)


def up_gelu(rows, w_up, bias):
    total, dim = rows.shape
    hidden = w_up.shape[1]
    tile_r = min(256, total)
    tile_h = min(512, hidden)
    spec_out = pl.BlockSpec((tile_r, tile_h), lambda j, i: (i, j))
    return pl.pallas_call(
        up_kernel,
        grid=(hidden // tile_h, total // tile_r),
        in_specs=[
            pl.BlockSpec((tile_r, dim), lambda j, i: (i, 0)),
            pl.BlockSpec((dim, tile_h), lambda j, i: (0, j)),
            pl.BlockSpec((1, tile_h), lambda j, i: (0, j)),
        ],
        out_specs=[spec_out, spec_out],
        out_shape=[jax.ShapeDtypeStruct((total, hidden), BF)] * 2,
        cost_estimate=pl.CostEstimate(
            flops=2 * total * dim * hidden, bytes_accessed=4 * total * hidden, transcendentals=2 * total * hidden
        ),
        name="up_gelu",
    )(rows, w_up, bias[None, :])


def norm_stats(values):
    centred = values - jnp.mean(values, axis=-1, keepdims=True)
    inv = lax.rsqrt(jnp.mean(centred * centred, axis=-1, keepdims=True) + EPS_NORM)
    return centred * inv, inv


def norm_bwd(grad, unit, inv, gain):
    scaled = grad * gain
    along = jnp.mean(scaled * unit, axis=-1, keepdims=True)
    return inv * (scaled - jnp.mean(scaled, axis=-1, keepdims=True) - unit * along)


def column_sum(values):
    return jnp.sum(values, axis=0)


def local(
    layer_input,
    cotangent,
    lengths,
    w_qkv,
    w_out,
    w_up,
    w_down,
    vec_bias,
    norm_gain,
    bias_up,
    seg_pos,
):
    count = lax.axis_size("dp")
    bits = count.bit_length() - 1
    me = lax.axis_index("dp")
    part = lax.axis_index("tensor")
    seqs_here, half, dim = layer_input.shape
    full_len = 2 * half
    segments = full_len // SEG
    seg_half = half // SEG
    chunk = dim // count
    width = w_qkv.shape[3]
    hidden = w_up.shape[2]
    orders = bit_orders(bits)
    swap_half = swap_tensor

    row_id = lax.broadcasted_iota(jnp.int32, (dim, dim), 0)
    col_id = lax.broadcasted_iota(jnp.int32, (dim, dim), 1)
    perm_hot = row_id == ((col_id // chunk) ^ me) * chunk + col_id % chunk
    perm = perm_hot.astype(BF)
    perm_f = perm_hot.astype(F32)

    def shards(block):
        return [
            jnp.concatenate([w_qkv[block].reshape(chunk, 3 * width), w_out[block].T], axis=1),
            w_up[block],
            w_down[block].T,
        ]

    units_one = gather_units(shards(0), orders, bits, count)
    second = shards(1)
    units_two = gather_units(
        [lax.optimization_barrier((s, units_one[0]))[0] for s in second], orders, bits, count
    )

    slot = me * 2 + part
    piece = vec_bias.shape[2]
    place = (
        lax.broadcasted_iota(jnp.int32, (piece, dim), 1)
        == lax.broadcasted_iota(jnp.int32, (piece, dim), 0) + slot * piece
    ).astype(F32)
    piece_up = bias_up.shape[1]
    hidden_all = piece_up * count * 2
    place_up = (
        lax.broadcasted_iota(jnp.int32, (piece_up, hidden_all), 1)
        == lax.broadcasted_iota(jnp.int32, (piece_up, hidden_all), 0) + slot * piece_up
    ).astype(F32)
    small_rows = jnp.concatenate(
        [vec_bias.reshape(-1, piece), norm_gain.reshape(-1, piece), seg_pos], axis=0
    )
    small = dot_exact(small_rows, place)
    small_up = dot_exact(bias_up, place_up)
    fold = hidden_all // dim
    small_all = sum_everywhere(
        jnp.concatenate([small, small_up.reshape(2 * fold, dim)], axis=0), bits, count
    )
    plain = small_all[: small_rows.shape[0]]
    up_all = small_all[small_rows.shape[0] :].reshape(2, 2, hidden)
    rel = dot_exact(plain, perm_f)

    def own_width(row):
        return jnp.where(part == 0, row[:width], row[width:])

    def block_vectors(block):
        base = 6 * block
        bias_qkv = jnp.concatenate(
            [own_width(plain[base]), jnp.zeros((width,), F32), own_width(plain[base + 1])]
        )
        hidden_bias = jnp.where(part == 0, up_all[block, 0], up_all[block, 1])
        gain_at = 12 + 2 * block
        return dict(
            qkv=bias_qkv,
            attn=rel[base + 2],
            mlp=rel[base + 3],
            shift_one=rel[base + 4],
            shift_two=rel[base + 5],
            gain_one=rel[gain_at],
            gain_two=rel[gain_at + 1],
            hidden=hidden_bias,
        )

    vec_one, vec_two = block_vectors(0), block_vectors(1)
    seg_rows = rel[16 : 16 + segments]

    length = lengths[0]
    seg_ids = jnp.concatenate(
        [part * seg_half + jnp.arange(seg_half), (1 - part) * seg_half + jnp.arange(seg_half)]
    ).astype(jnp.int32)
    seg_counts = jnp.clip(length - seg_ids * SEG, 0, SEG).astype(jnp.int32)

    def three_mats(units):
        return units[0][:, : 3 * width], units[0][:, 3 * width :], units[1], units[2]

    w_qkv_r, w_out_r, w_up_r, w_down_r = three_mats(units_one)
    x_own = dot_nn(layer_input[0], perm).astype(BF)
    x_full = jnp.concatenate([x_own, swap_half(x_own)], axis=0)
    qkv = (dot_nn(x_full, w_qkv_r) + vec_one["qkv"]).astype(BF)
    attended = attn_fwd(seg_counts, qkv)
    partial_attn = dot_nt(attended, w_out_r).astype(BF)
    first_sum = (
        partial_attn[:half].astype(F32)
        + swap_half(partial_attn[half:]).astype(F32)
        + vec_one["attn"]
        + x_own.astype(F32)
    )
    unit_one, inv_one = norm_stats(first_sum)
    first = unit_one * vec_one["gain_one"] + vec_one["shift_one"]
    first_low = first.astype(BF)
    first_full = jnp.concatenate([first_low, swap_half(first_low)], axis=0)
    act, slope = up_gelu(first_full, w_up_r, vec_one["hidden"])
    partial_mlp = dot_nt(act, w_down_r).astype(BF)
    second_sum = (
        partial_mlp[:half].astype(F32) + swap_half(partial_mlp[half:]).astype(F32) + vec_one["mlp"] + first
    )
    unit_two, inv_two = norm_stats(second_sum)
    first_out = unit_two * vec_one["gain_two"] + vec_one["shift_two"]

    v2 = vec_two
    y_qkv, y_out, y_up, y_down = three_mats(units_two)

    def both_halves(own_rows):
        other = swap_half(own_rows)
        return jnp.where(
            part == 0,
            jnp.concatenate([own_rows, other], axis=0),
            jnp.concatenate([other, own_rows], axis=0),
        )

    def own_half(rows):
        return jnp.where(part == 0, rows[:seg_half], rows[seg_half:])

    cls_own = first_out.reshape(seg_half, SEG, dim)[:, 0]
    cls_in = both_halves(cls_own) + seg_rows
    cls_low = cls_in.astype(BF)
    key_ok = (jnp.arange(segments) * SEG < length)[None, None, :]
    qkv_c = (dot_nn(cls_low, y_qkv) + v2["qkv"]).astype(BF)
    heads = width // HD
    q_c, k_c, v_c = (qkv_c[:, i * width : (i + 1) * width].reshape(segments, heads, HD) for i in range(3))
    scores_c = jnp.einsum("rhe,she->hrs", q_c, k_c, preferred_element_type=F32) * SM_SCALE
    scores_c = jnp.where(key_ok, scores_c, NEG_FILL)
    expo_c = jnp.exp(scores_c - jnp.max(scores_c, axis=-1, keepdims=True))
    probs_c = expo_c / jnp.sum(expo_c, axis=-1, keepdims=True)
    probs_c_low = probs_c.astype(BF)
    att_c = (
        jnp.einsum("hrs,she->rhe", probs_c_low, v_c, preferred_element_type=F32)
        .astype(BF)
        .reshape(segments, width)
    )
    part_c = dot_nt(att_c, y_out)
    sum_c1 = part_c + swap_half(part_c) + v2["attn"] + cls_in
    unit_c1, inv_c1 = norm_stats(sum_c1)
    first_c = unit_c1 * v2["gain_one"] + v2["shift_one"]
    first_c_low = first_c.astype(BF)
    act_f, slope_c = gelu_pair(dot_nn(first_c_low, y_up) + v2["hidden"])
    act_c = act_f.astype(BF)
    part_c2 = dot_nt(act_c, y_down)
    sum_c2 = part_c2 + swap_half(part_c2) + v2["mlp"] + first_c
    unit_c2, inv_c2 = norm_stats(sum_c2)
    cls_out = unit_c2 * v2["gain_two"] + v2["shift_two"]

    row_in = lax.broadcasted_iota(jnp.int32, (half, 1), 0)
    valid = part * half + row_in < length
    is_cls = (lax.broadcasted_iota(jnp.int32, (1, SEG, 1), 1) == 0)

    def with_cls(rows, cls):
        return jnp.where(is_cls, cls[:, None, :], rows.reshape(seg_half, SEG, dim)).reshape(half, dim)

    combined = jnp.where(valid, with_cls(first_out, own_half(cls_out)), 0.0).astype(BF)
    output = dot_nn(combined, perm).astype(BF)[None]

    cot = jnp.where(valid, cotangent[0], jnp.zeros_like(cotangent[0]))
    grad_y_low = dot_nn(cot, perm).astype(BF)
    cot_cls = grad_y_low.reshape(seg_half, SEG, dim)[:, 0]
    g_c = both_halves(cot_cls).astype(F32)
    g_second_c = norm_bwd(g_c, unit_c2, inv_c2, v2["gain_two"])
    g_mlp_c = g_second_c.astype(BF)
    gpre_c = (dot_nn(g_mlp_c, y_down) * slope_c).astype(BF)
    gw_down_c = dot_tn(g_mlp_c, act_c).astype(BF)
    gw_up_c = dot_tn(first_c_low, gpre_c).astype(BF)
    part_g1 = dot_nt(gpre_c, y_up)
    g_first_c = part_g1 + swap_half(part_g1) + g_second_c
    g_sum_c = norm_bwd(g_first_c, unit_c1, inv_c1, v2["gain_one"])
    g_attn_c = g_sum_c.astype(BF)
    gw_out_c = dot_tn(g_attn_c, att_c).astype(BF)
    g_att_c = dot_nn(g_attn_c, y_out).astype(BF).reshape(segments, heads, HD)
    gv_c = jnp.einsum("hrs,rhe->she", probs_c_low, g_att_c, preferred_element_type=F32)
    gp_c = jnp.einsum("rhe,she->hrs", g_att_c, v_c, preferred_element_type=F32)
    in_c = jnp.sum(gp_c * probs_c, axis=-1, keepdims=True)
    gs_c = jnp.where(key_ok, probs_c * (gp_c - in_c), 0.0).astype(BF)
    gq_c = jnp.einsum("hrs,she->rhe", gs_c, k_c, preferred_element_type=F32) * SM_SCALE
    gk_c = jnp.einsum("hrs,rhe->she", gs_c, q_c, preferred_element_type=F32) * SM_SCALE
    gqkv_c = jnp.concatenate([g.reshape(segments, width) for g in (gq_c, gk_c, gv_c)], axis=1).astype(BF)
    gw_qkv_c = dot_tn(cls_low, gqkv_c).astype(BF)
    part_g2 = dot_nt(gqkv_c, y_qkv)
    g_cls_in = part_g2 + swap_half(part_g2) + g_sum_c

    grad_out = with_cls(grad_y_low.astype(F32), own_half(g_cls_in))
    g_second = norm_bwd(grad_out, unit_two, inv_two, vec_one["gain_two"])
    g_second_low = g_second.astype(BF)
    g_mlp = jnp.concatenate([g_second_low, swap_half(g_second_low)], axis=0)
    gpre = (dot_nn(g_mlp, w_down_r) * slope.astype(F32)).astype(BF)
    gw_down = dot_tn(g_mlp, act).astype(BF)
    part_h = dot_nt(gpre, w_up_r).astype(BF)
    gw_up = dot_tn(first_full, gpre).astype(BF)
    g_first = part_h[:half].astype(F32) + swap_half(part_h[half:]).astype(F32) + g_second
    g_first_sum = norm_bwd(g_first, unit_one, inv_one, vec_one["gain_one"])
    g_first_low = g_first_sum.astype(BF)
    g_attn = jnp.concatenate([g_first_low, swap_half(g_first_low)], axis=0)
    gw_out = dot_tn(g_attn, attended).astype(BF)
    g_attended = dot_nn(g_attn, w_out_r).astype(BF)
    gqkv, gqkv_sums = attn_bwd(seg_counts, qkv, g_attended)
    part_x = dot_nt(gqkv, w_qkv_r).astype(BF)
    gw_qkv = dot_tn(x_full, gqkv).astype(BF)
    g_in = part_x[:half].astype(F32) + swap_half(part_x[half:]).astype(F32) + g_first_sum
    g_in_high = lax.reduce_precision(g_in, 8, 7)
    grad_input = (dot_nn(g_in_high.astype(BF), perm) + dot_nn((g_in - g_in_high).astype(BF), perm))[None]

    scale_one = 1.0 / math.sqrt(seqs_here * count * full_len)
    scale_two = 1.0 / math.sqrt(seqs_here * count * segments)

    def reduced(first_grad, second_grad, order):
        return (
            scatter_unit(first_grad, order, bits, count) * scale_one,
            scatter_unit(second_grad, order, bits, count) * scale_two,
        )

    down_one, down_two = reduced(gw_down, gw_down_c, orders[2])
    up_one, up_two = reduced(gw_up, gw_up_c, orders[1])
    out_one, out_two = reduced(gw_out, gw_out_c, orders[0])
    qkv_one, qkv_two = reduced(gw_qkv, gw_qkv_c, orders[0])
    grad_w_qkv = jnp.stack([qkv_one, qkv_two]).reshape(2, chunk, 3, width)
    grad_w_out = jnp.stack([out_one.T, out_two.T])
    grad_w_up = jnp.stack([up_one, up_two])
    grad_w_down = jnp.stack([down_one.T, down_two.T])

    def spread(values, total):
        zero = jnp.zeros((total - values.shape[0],), F32)
        return jnp.where(part == 0, jnp.concatenate([values, zero]), jnp.concatenate([zero, values]))

    rel_rows = jnp.stack(
        [
            column_sum(g_first_sum) * scale_one,
            column_sum(g_second) * scale_one,
            column_sum(g_first) * scale_one,
            column_sum(grad_out) * scale_one,
            column_sum(own_half(g_sum_c)) * scale_two,
            column_sum(own_half(g_second_c)) * scale_two,
            column_sum(own_half(g_first_c)) * scale_two,
            column_sum(own_half(g_c)) * scale_two,
            column_sum(g_first * unit_one) * scale_one,
            column_sum(grad_out * unit_two) * scale_one,
            column_sum(own_half(g_first_c * unit_c1)) * scale_two,
            column_sum(own_half(g_c * unit_c2)) * scale_two,
        ]
    )
    zeros_half = jnp.zeros((seg_half, dim), F32)
    cls_part = own_half(g_cls_in) * scale_two
    seg_grad = jnp.where(
        part == 0,
        jnp.concatenate([cls_part, zeros_half], axis=0),
        jnp.concatenate([zeros_half, cls_part], axis=0),
    )
    canon = dot_exact(jnp.concatenate([rel_rows, seg_grad], axis=0), perm_f)
    sums_c = column_sum(gqkv_c.astype(F32)) * scale_two
    sums_o = gqkv_sums[0] * scale_one
    bias_rows = jnp.stack(
        [
            spread(sums_o[:width], dim),
            spread(sums_o[2 * width :], dim),
            canon[0],
            canon[1],
            canon[2],
            canon[3],
            spread(sums_c[:width], dim),
            spread(sums_c[2 * width :], dim),
            canon[4],
            canon[5],
            canon[6],
            canon[7],
        ]
    )
    up_rows = jnp.stack(
        [
            spread(column_sum(gpre.astype(F32)) * scale_one, hidden_all),
            spread(column_sum(gpre_c.astype(F32)) * scale_two, hidden_all),
        ]
    )
    all_small = sum_everywhere(
        jnp.concatenate([bias_rows, canon[8:], up_rows.reshape(2 * fold, dim)], axis=0), bits, count
    )
    mine = dot_exact(all_small[:24], place.T)
    grad_vec = mine[:12].reshape(2, 6, piece)
    grad_gain = mine[12:16].reshape(2, 2, piece)
    grad_seg = mine[16:24]
    grad_up_vec = dot_exact(all_small[24:].reshape(2, hidden_all), place_up.T)
    return (
        output,
        grad_input,
        grad_w_qkv,
        grad_w_out,
        grad_w_up,
        grad_w_down,
        grad_vec,
        grad_gain,
        grad_up_vec,
        grad_seg,
    )


def solution(mesh):
    return jax.shard_map(
        local,
        mesh=mesh,
        in_specs=(
            P("dp", "tensor", None),
            P("dp", "tensor", None),
            P("dp"),
            P(None, "dp", None, "tensor"),
            P(None, "tensor", "dp"),
            P(None, "dp", "tensor"),
            P(None, "tensor", "dp"),
            P(None, None, ("dp", "tensor")),
            P(None, None, ("dp", "tensor")),
            P(None, ("dp", "tensor")),
            P(None, ("dp", "tensor")),
        ),
        out_specs=(
            P("dp", "tensor", None),
            P("dp", "tensor", None),
            P(None, "dp", None, "tensor"),
            P(None, "tensor", "dp"),
            P(None, "dp", "tensor"),
            P(None, "tensor", "dp"),
            P(None, None, ("dp", "tensor")),
            P(None, None, ("dp", "tensor")),
            P(None, ("dp", "tensor")),
            P(None, ("dp", "tensor")),
        ),
        check_vma=False,
    )
```

time: 1460 us -> 517 us (0.35)
  waiting for transfers between devices: 964 us -> 203 us
  blocking collectives: 187 us -> 0 us
  starting transfers between devices: 1.43 us -> 85.8 us
  local copies, waits for them, and re-layouts: 122 us -> 41.1 us
  matrix products: 110 us -> 71 us
  Pallas kernels: 0 us -> 37.8 us
  other arithmetic: 50.2 us -> 66.9 us
    unnamed x19 -> x0, waiting for transfers between devices: 626 us -> none
    ppermute x0 -> x80, waiting for transfers between devices: none -> 203 us  [the longest x64 202 us: swap_dp(): return lax.ppermute(values, 'dp', [(i, i ^ 1 << bit) for i in range(count)])]
    reduce_scatter x5 -> x0, waiting for transfers between devices: 194 us -> none  [the longest x1 171 us: local(): lax.psum_scatter(jnp.stack([scaled_one[2], mats_grad_two[2] * scale_two])...]
    all_gather x8 -> x0, blocking collectives: 173 us -> none  [the longest x1 45.7 us: local(): lax.all_gather(vec_bias, ('dp', 'tensor'), axis=2, tiled=True)]
    all_gather x8 -> x0, waiting for transfers between devices: 145 us -> none  [the longest x1 63.6 us: local(): lax.all_gather(w_down, 'dp', axis=2, tiled=True)]
    ppermute x0 -> x80, starting transfers between devices: none -> 85.8 us  [the longest x64 82.8 us: swap_dp(): return lax.ppermute(values, 'dp', [(i, i ^ 1 << bit) for i in range(count)])]
    another operation x26 -> x5, local copies, waits for them, and re-layouts: 42 us -> 1.2 us  [the longest x4 1.19 us: local(): jnp.stack([spread(sums_o[:width], dim), spread(sums_o[2 * width:], dim),...]
    dot_general x36 -> x39, matrix products: 110 us -> 69.6 us  [the longest x12 26.3 us: dot_nn(): lax.dot_general(a, b, (((1,), (0,)), ((), ())), preferred_element_type=F32)]
  transfers between devices with their start and end apart: 16 -> 80, of which waited for: 11 -> 34; matrix products, arithmetic and copies ran while one was open for 14% -> 31% of each run, Pallas kernels for 0% -> 7%
where the time goes in v1:
time: 517 us; the launch traced here: 510 us
  waiting for transfers between devices  203 us (39%)
  starting transfers between devices  85.8 us (17%)
  matrix products  71 us (14%)
  other arithmetic  66.9 us (13%)
  local copies, waits for them, and re-layouts  41.1 us (8%)
  Pallas kernels  37.8 us (7%)
    ppermute x64, waiting for transfers between devices, swap_dp(): return lax.ppermute(values, 'dp', [(i, i ^ 1 << bit) for i in range(count)])  202 us
    ppermute x64, starting transfers between devices, swap_dp(): return lax.ppermute(values, 'dp', [(i, i ^ 1 << bit) for i in range(count)])  82.8 us
    concatenate x24, other arithmetic, gather_step(): jnp.concatenate([values, swap_dp(values, bit, count)], axis=bits - 1 - bit)  27.2 us
    dot_general x12, matrix products, dot_nn(): lax.dot_general(a, b, (((1,), (0,)), ((), ())), preferred_element_type=F32)  26.3 us
    dot_general x8, matrix products, dot_nt(): lax.dot_general(a, b, (((1,), (1,)), ((), ())), preferred_element_type=F32)  19.3 us
    convert_element_type x24, other arithmetic, scatter_unit(): v = v.astype(BF)  18 us
    pallas_call x1, Pallas kernels, attn_bwd(): pl.pallas_call(attn_bwd_kernel, grid_spec=pltpu.PrefetchScalarGridSpec(nu...  15.8 us
    dot_general x8, matrix products, dot_tn(): lax.dot_general(a, b, (((0,), (0,)), ((), ())), preferred_element_type=F32)  15.5 us
  transfers between devices with their start and end apart: 80, of which 34 were waited for; matrix products, arithmetic and copies ran while one was open for 31% of the time, Pallas kernels for 7%

profile of v1, /device:TPU:0, one launch (start us, length us, event | category | flops | bytes accessed | tf_op | source)
XLA Modules:
  0.0 509.9 jit_solution(14383875031738022088)
XLA Ops:
  6.6 3.7 collective-permute-start.1
  17.6 2.6 collective-permute-start.16
  23.3 4.3 collective-permute-done.12
  31.4 7.0 %collective-permute-done.7 = f32[32,768]{1,0:T(8,128)S(1)} collective-permute-done((f32[32,768]{1,0:T(8,128)S(1)}, f32[32,768]{1,0:T(8,128)S(1)}, u32[]{:S(2)}, u32[]{:S(2)}) %collective-permute-start.7) | collective-permute-done | bytes 98336 | tf_op jit(solution)/shard_map/ppermute | solution.py:41
  43.2 2.3 collective-permute-start.9
  50.8 2.9 collective-permute-done.3
  59.3 3.6 collective-permute-done.14
  69.3 17.0 %collective-permute-done.4 = bf16[2,1,2,2,48,1536]{5,4,3,2,1,0:T(8,128)(2,1)} collective-permute-done((bf16[2,1,2,2,48,1536]{5,4,3,2,1,0:T(8,128)(2,1)}, bf16[2,1,2,2,48,1536]{5,4,3,2,1,0:T(8,128)(2,1)}, u32[]{:S(2)}, u32[]{:S(2)}) %collective-permute-start.4) | collective-permute-done | bytes 1179680 | tf_op jit(solution)/shard_map/ppermute | solution.py:41
  86.3 3.1 pad_maximum_fusion
  89.4 5.6 %add_convert_fusion.qkv_ref = bf16[1024,1152]{1,0:T(8,128)(2,1)} fusion(f32[1152]{0:T(1024)S(1)} %get-tuple-element.109, bf16[768,1536]{1,0:T(8,128)(2,1)} %bitcast.7, bf16[512,768]{1,0:T(8,128)(2,1)} %collective-permute-done, bf16[512,768]{1,0:T(8,128)(2,1)} %fusion.16), kind=kOutput, calls=%fused_computation.4 | convolution fusion | flops 1817444352 | bytes 5706240 | tf_op jit(solution)/shard_map/dot_general | solution.py:23
  95.0 9.5 %attn_fwd.1 = bf16[1024,384]{1,0:T(8,128)(2,1)} custom-call(s32[8]{0:T(128)} %fusion.110.count_ref, bf16[1024,1152]{1,0:T(8,128)(2,1)} %add_convert_fusion.qkv_ref), custom_call_target="tpu_custom_call" | custom-call | flops 402653184 | bytes 3145728 | tf_op jit(solution)/shard_map/attn_fwd/pallas_call | solution.py:153
  107.6 2.3 collective-permute-start.31
  110.5 2.7 pad_maximum_fusion.1
  113.2 10.9 %collective-permute-done.22 = bf16[1,1,1,1,48,1536]{5,4,3,2,1,0:T(8,128)(2,1)S(1)} collective-permute-done((bf16[1,1,1,1,48,1536]{5,4,3,2,1,0:T(8,128)(2,1)S(1)}, bf16[1,1,1,1,48,1536]{5,4,3,2,1,0:T(8,128)(2,1)S(1)}, u32[]{:S(2)}, u32[]{:S(2)}) %collective-permute-start.22) | collective-permute-done | bytes 147488 | tf_op jit(solution)/shard_map/ppermute | solution.py:41
  127.4 2.6 collective-permute-done.27
  136.7 2.6 pad_maximum_fusion.2
  143.4 7.7 %collective-permute-done.24 = bf16[2,1,1,2,48,1536]{5,4,3,2,1,0:T(8,128)(2,1)S(1)} collective-permute-done((bf16[2,1,1,2,48,1536]{5,4,3,2,1,0:T(8,128)(2,1)S(1)}, bf16[2,1,1,2,48,1536]{5,4,3,2,1,0:T(8,128)(2,1)S(1)}, u32[]{:S(2)}, u32[]{:S(2)}) %collective-permute-start.24) | collective-permute-done | bytes 589856 | tf_op jit(solution)/shard_map/ppermute | solution.py:41
  153.7 12.6 %up_gelu.1 = (bf16[1024,1536]{1,0:T(8,128)(2,1)}, bf16[1024,1536]{1,0:T(8,128)(2,1)}) custom-call(bf16[1024,768]{1,0:T(8,128)(2,1)} %pad_maximum_fusion.7.rows_ref, bf16[768,1536]{1,0:T(8,128)(2,1)} %bitcast.203, f32[1,1536]{1,0:T(1,128)} %get-tuple-element.102.bias_ref), custom_call_target="tpu_custom_call" | custom-call | flops 2415919104 | bytes 6291456 | tf_op jit(solution)/shard_map/up_gelu/pallas_call | solution.py:212
  166.3 5.2 %convolution_convert_fusion.9 = bf16[1024,768]{1,0:T(8,128)(2,1)S(1)} fusion(bf16[1024,1536]{1,0:T(8,128)(2,1)} %get-tuple-element.17, bf16[768,1536]{1,0:T(8,128)(2,1)} %bitcast.205), kind=kOutput, calls=%fused_computation.35 | convolution fusion | flops 2416705536 | bytes 7077888 | tf_op jit(solution)/shard_map/dot_general | solution.py:27
  179.1 4.7 collective-permute-done.25
  186.7 14.7 %collective-permute-done.34 = bf16[2,2,1,2,48,1536]{5,4,3,2,1,0:T(8,128)(2,1)S(1)} collective-permute-done((bf16[2,2,1,2,48,1536]{5,4,3,2,1,0:T(8,128)(2,1)S(1)}, bf16[2,2,1,2,48,1536]{5,4,3,2,1,0:T(8,128)(2,1)S(1)}, u32[]{:S(2)}, u32[]{:S(2)}) %collective-permute-start.34) | collective-permute-done | bytes 1179680 | tf_op jit(solution)/shard_map/ppermute | solution.py:41
  201.4 2.6 pad_maximum_fusion.5
  244.3 21.7 %collective-permute-done.55 = bf16[2,1,2,2,48,384]{5,4,3,2,1,0:T(8,128)(2,1)S(1)} collective-permute-done((bf16[2,1,2,2,48,384]{5,4,3,2,1,0:T(8,128)(2,1)S(1)}, bf16[2,1,2,2,48,384]{5,4,3,2,1,0:T(8,128)(2,1)S(1)}, u32[]{:S(2)}, u32[]{:S(2)}) %collective-permute-start.55) | collective-permute-done | bytes 294944 | tf_op jit(solution)/shard_map/ppermute | solution.py:41
  266.7 5.1 %collective-permute-done.56 = bf16[2,1,1,2,48,384]{5,4,3,2,1,0:T(8,128)(2,1)S(1)} collective-permute-done((bf16[2,1,1,2,48,384]{5,4,3,2,1,0:T(8,128)(2,1)S(1)}, bf16[2,1,1,2,48,384]{5,4,3,2,1,0:T(8,128)(2,1)S(1)}, u32[]{:S(2)}, u32[]{:S(2)}) %collective-permute-start.56) | collective-permute-done | bytes 147488 | tf_op jit(solution)/shard_map/ppermute | solution.py:41
  272.5 3.8 collective-permute-done.57
  281.4 3.7 convert_reduce_fusion
  285.1 2.6 convolution_convert_fusion.8
  289.9 3.1 convolution_convert_fusion.1
  295.3 2.9 convolution_convert_fusion
  306.9 31.0 %collective-permute-done.48 = bf16[2,1,1,2,48,1152]{5,4,3,2,1,0:T(8,128)(2,1)S(1)} collective-permute-done((bf16[2,1,1,2,48,1152]{5,4,3,2,1,0:T(8,128)(2,1)S(1)}, bf16[2,1,1,2,48,1152]{5,4,3,2,1,0:T(8,128)(2,1)S(1)}, u32[]{:S(2)}, u32[]{:S(2)}) %collective-permute-start.48) | collective-permute-done | bytes 442400 | tf_op jit(solution)/shard_map/ppermute | solution.py:41
  371.9 12.8 %collective-permute-done.66 = bf16[1,1,1,1,48,1536]{5,4,3,2,1,0:T(8,128)(2,1)S(1)} collective-permute-done((bf16[1,1,1,1,48,1536]{5,4,3,2,1,0:T(8,128)(2,1)S(1)}, bf16[1,1,1,1,48,1536]{5,4,3,2,1,0:T(8,128)(2,1)S(1)}, u32[]{:S(2)}, u32[]{:S(2)}) %collective-permute-start.66) | collective-permute-done | bytes 147488 | tf_op jit(solution)/shard_map/ppermute | solution.py:41
  384.7 2.4 collective-permute-done.74
  387.9 3.4 convolution_convert_fusion.10.grad_ref
  391.3 15.8 %attn_bwd.1 = (bf16[1024,1152]{1,0:T(8,128)(2,1)}, f32[1,1152]{1,0:T(1,128)}) custom-call(s32[8]{0:T(128)} %fusion.110.count_ref, bf16[1024,1152]{1,0:T(8,128)(2,1)} %add_convert_fusion.qkv_ref, bf16[1024,384]{1,0:T(8,128)(2,1)} %convolution_convert_fusion.10.grad_ref), custom_call_target="tpu_custom_call" | custom-call | flops 1006632960 | bytes 5505024 | tf_op jit(solution)/shard_map/attn_bwd/pallas_call | solution.py:172
  407.1 4.4 convolution_convert_fusion.7
  414.4 4.4 convolution_convert_fusion.3
  419.8 2.9 collective-permute-start.43
  424.3 2.4 convolution_convert_fusion.15
  433.6 15.5 %collective-permute-done.51 = bf16[2,1,2,2,48,384]{5,4,3,2,1,0:T(8,128)(2,1)S(1)} collective-permute-done((bf16[2,1,2,2,48,384]{5,4,3,2,1,0:T(8,128)(2,1)S(1)}, bf16[2,1,2,2,48,384]{5,4,3,2,1,0:T(8,128)(2,1)S(1)}, u32[]{:S(2)}, u32[]{:S(2)}) %collective-permute-start.51) | collective-permute-done | bytes 294944 | tf_op jit(solution)/shard_map/ppermute | solution.py:41
  458.5 4.0 collective-permute-done.79
  468.4 3.3 collective-permute-start.62
  474.0 2.9 collective-permute-start.70
  476.8 3.6 collective-permute-done.54
  481.2 2.6 collective-permute-done.70
  488.0 8.1 %collective-permute-done.44 = bf16[2,1,1,2,48,1152]{5,4,3,2,1,0:T(8,128)(2,1)S(1)} collective-permute-done((bf16[2,1,1,2,48,1152]{5,4,3,2,1,0:T(8,128)(2,1)S(1)}, bf16[2,1,1,2,48,1152]{5,4,3,2,1,0:T(8,128)(2,1)S(1)}, u32[]{:S(2)}, u32[]{:S(2)}) %collective-permute-start.44) | collective-permute-done | bytes 442400 | tf_op jit(solution)/shard_map/ppermute | solution.py:41
  499.2 3.1 collective-permute-done.45
  502.5 3.4 add_bitcast_fusion
  505.9 2.5 collective-permute-done.46
  (682 shorter events, 204.1 us)
Async XLA Ops:
  4.2 16.0 %collective-permute-start.5 = (f32[32,768]{1,0:T(8,128)S(1)}, f32[32,768]{1,0:T(8,128)}, u32[]{:S(2)}, u32[]{:S(2)}) collective-permute-start(f32[32,768]{1,0:T(8,128)S(1)} %pad_maximum_fusion.39), channel_id=1, source_target_pairs={{0,1},{1,0},{2,3},{3,2},{4,5},{5,4},{6,7},{7,6},{8,9},{9,8},{10,11... | collective-permute-start | bytes 294920 | tf_op jit(solution)/shard_map/ppermute | solution.py:45
  6.6 16.1 %collective-permute-start.1 = (bf16[1,1,1,1,48,1536]{5,4,3,2,1,0:T(8,128)(2,1)S(1)}, bf16[1,1,1,1,48,1536]{5,4,3,2,1,0:T(8,128)(2,1)S(1)}, u32[]{:S(2)}, u32[]{:S(2)}) collective-permute-start(bf16[1,1,1,1,48,1536]{5,4,3,2,1,0:T(8,128)(2,1)S(1)} %maximum_bitcast_fusion), channel_id=1, source_target_pairs={{0,16},{2,18},{4,20},{6,22},{8,24},{10,26},{12,28},{14,30},{16,0},... | collective-permute-start | bytes 442376 | tf_op jit(solution)/shard_map/ppermute | solution.py:41
  12.1 77.3 %collective-permute-start = (bf16[512,768]{1,0:T(8,128)(2,1)}, bf16[512,768]{1,0:T(8,128)(2,1)}, u32[]{:S(2)}, u32[]{:S(2)}) collective-permute-start(bf16[512,768]{1,0:T(8,128)(2,1)} %fusion.16), channel_id=1, source_target_pairs={{0,1},{1,0},{2,3},{3,2},{4,5},{5,4},{6,7},{7,6},{8,9},{9,8},{10,11... | collective-permute-start | bytes 2359304 | tf_op jit(solution)/shard_map/ppermute | solution.py:45
  12.4 15.3 %collective-permute-start.12 = (bf16[1,1,1,1,48,1536]{5,4,3,2,1,0:T(8,128)(2,1)S(1)}, bf16[1,1,1,1,48,1536]{5,4,3,2,1,0:T(8,128)(2,1)S(1)}, u32[]{:S(2)}, u32[]{:S(2)}) collective-permute-start(bf16[1,1,1,1,48,1536]{5,4,3,2,1,0:T(8,128)(2,1)S(1)} %get-tuple-element.92), channel_id=1, source_target_pairs={{0,16},{2,18},{4,20},{6,22},{8,24},{10,26},{12,28},{14,30},{16,0},... | collective-permute-start | bytes 442376 | tf_op jit(solution)/shard_map/ppermute | solution.py:41
  17.6 13.0 %collective-permute-start.16 = (bf16[1,1,1,1,48,1536]{5,4,3,2,1,0:T(8,128)(2,1)S(1)}, bf16[1,1,1,1,48,1536]{5,4,3,2,1,0:T(8,128)(2,1)S(1)}, u32[]{:S(2)}, u32[]{:S(2)}) collective-permute-start(bf16[1,1,1,1,48,1536]{5,4,3,2,1,0:T(8,128)(2,1)S(1)} %get-tuple-element.94), channel_id=1, source_target_pairs={{0,16},{2,18},{4,20},{6,22},{8,24},{10,26},{12,28},{14,30},{16,0},... | collective-permute-start | bytes 442376 | tf_op jit(solution)/shard_map/ppermute | solution.py:41
  22.7 16.7 %collective-permute-start.2 = (bf16[2,1,1,1,48,1536]{5,4,3,2,1,0:T(8,128)(2,1)S(1)}, bf16[2,1,1,1,48,1536]{5,4,3,2,1,0:T(8,128)(2,1)S(1)}, u32[]{:S(2)}, u32[]{:S(2)}) collective-permute-start(bf16[2,1,1,1,48,1536]{5,4,3,2,1,0:T(8,128)(2,1)S(1)} %pad_maximum_fusion.31), channel_id=1, source_target_pairs={{0,2},{2,0},{4,6},{6,4},{8,10},{10,8},{12,14},{14,12},{16,18},{18,... | collective-permute-start | bytes 884744 | tf_op jit(solution)/shard_map/ppermute | solution.py:41
  27.6 17.8 %collective-permute-start.13 = (bf16[2,1,1,1,48,1536]{5,4,3,2,1,0:T(8,128)(2,1)S(1)}, bf16[2,1,1,1,48,1536]{5,4,3,2,1,0:T(8,128)(2,1)S(1)}, u32[]{:S(2)}, u32[]{:S(2)}) collective-permute-start(bf16[2,1,1,1,48,1536]{5,4,3,2,1,0:T(8,128)(2,1)S(1)} %pad_maximum_fusion.32), channel_id=1, source_target_pairs={{0,4},{2,6},{4,0},{6,2},{8,12},{10,14},{12,8},{14,10},{16,20},{18,... | collective-permute-start | bytes 884744 | tf_op jit(solution)/shard_map/ppermute | solution.py:41
  30.6 17.8 %collective-permute-start.17 = (bf16[2,1,1,1,48,1536]{5,4,3,2,1,0:T(8,128)(2,1)S(1)}, bf16[2,1,1,1,48,1536]{5,4,3,2,1,0:T(8,128)(2,1)S(1)}, u32[]{:S(2)}, u32[]{:S(2)}) collective-permute-start(bf16[2,1,1,1,48,1536]{5,4,3,2,1,0:T(8,128)(2,1)S(1)} %pad_maximum_fusion.33), channel_id=1, source_target_pairs={{0,8},{2,10},{4,12},{6,14},{8,0},{10,2},{12,4},{14,6},{16,24},{18,... | collective-permute-start | bytes 884744 | tf_op jit(solution)/shard_map/ppermute | solution.py:41
  39.5 14.2 %collective-permute-start.3 = (bf16[2,1,1,2,48,1536]{5,4,3,2,1,0:T(8,128)(2,1)S(1)}, bf16[2,1,1,2,48,1536]{5,4,3,2,1,0:T(8,128)(2,1)S(1)}, u32[]{:S(2)}, u32[]{:S(2)}) collective-permute-start(bf16[2,1,1,2,48,1536]{5,4,3,2,1,0:T(8,128)(2,1)S(1)} %pad_maximum_fusion.22), channel_id=1, source_target_pairs={{0,4},{2,6},{4,0},{6,2},{8,12},{10,14},{12,8},{14,10},{16,20},{18,... | collective-permute-start | bytes 1769480 | tf_op jit(solution)/shard_map/ppermute | solution.py:41
  46.3 16.5 %collective-permute-start.14 = (bf16[2,1,2,1,48,1536]{5,4,3,2,1,0:T(8,128)(2,1)}, bf16[2,1,2,1,48,1536]{5,4,3,2,1,0:T(8,128)(2,1)}, u32[]{:S(2)}, u32[]{:S(2)}) collective-permute-start(bf16[2,1,2,1,48,1536]{5,4,3,2,1,0:T(8,128)(2,1)} %pad_maximum_fusion.23), channel_id=1, source_target_pairs={{0,8},{2,10},{4,12},{6,14},{8,0},{10,2},{12,4},{14,6},{16,24},{18,... | collective-permute-start | bytes 1769480 | tf_op jit(solution)/shard_map/ppermute | solution.py:41
  49.3 17.3 %collective-permute-start.18 = (bf16[2,2,1,1,48,1536]{5,4,3,2,1,0:T(8,128)(2,1)}, bf16[2,2,1,1,48,1536]{5,4,3,2,1,0:T(8,128)(2,1)S(1)}, u32[]{:S(2)}, u32[]{:S(2)}) collective-permute-start(bf16[2,2,1,1,48,1536]{5,4,3,2,1,0:T(8,128)(2,1)} %pad_maximum_fusion.24), channel_id=1, source_target_pairs={{0,2},{2,0},{4,6},{6,4},{8,10},{10,8},{12,14},{14,12},{16,18},{18,... | collective-permute-start | bytes 1769480 | tf_op jit(solution)/shard_map/ppermute | solution.py:41
  55.6 30.6 %collective-permute-start.4 = (bf16[2,1,2,2,48,1536]{5,4,3,2,1,0:T(8,128)(2,1)}, bf16[2,1,2,2,48,1536]{5,4,3,2,1,0:T(8,128)(2,1)}, u32[]{:S(2)}, u32[]{:S(2)}) collective-permute-start(bf16[2,1,2,2,48,1536]{5,4,3,2,1,0:T(8,128)(2,1)} %pad_maximum_fusion.10), channel_id=1, source_target_pairs={{0,8},{2,10},{4,12},{6,14},{8,0},{10,2},{12,4},{14,6},{16,24},{18,... | collective-permute-start | bytes 3538952 | tf_op jit(solution)/shard_map/ppermute | solution.py:41
  65.1 44.9 %collective-permute-start.15 = (bf16[2,2,2,1,48,1536]{5,4,3,2,1,0:T(8,128)(2,1)}, bf16[2,2,2,1,48,1536]{5,4,3,2,1,0:T(8,128)(2,1)}, u32[]{:S(2)}, u32[]{:S(2)}) collective-permute-start(bf16[2,2,2,1,48,1536]{5,4,3,2,1,0:T(8,128)(2,1)} %pad_maximum_fusion.11), channel_id=1, source_target_pairs={{0,2},{2,0},{4,6},{6,4},{8,10},{10,8},{12,14},{14,12},{16,18},{18,... | collective-permute-start | bytes 3538952 | tf_op jit(solution)/shard_map/ppermute | solution.py:41
  67.8 68.3 %collective-permute-start.19 = (bf16[2,2,1,2,48,1536]{5,4,3,2,1,0:T(8,128)(2,1)}, bf16[2,2,1,2,48,1536]{5,4,3,2,1,0:T(8,128)(2,1)}, u32[]{:S(2)}, u32[]{:S(2)}) collective-permute-start(bf16[2,2,1,2,48,1536]{5,4,3,2,1,0:T(8,128)(2,1)} %pad_maximum_fusion.12), channel_id=1, source_target_pairs={{0,4},{2,6},{4,0},{6,2},{8,12},{10,14},{12,8},{14,10},{16,20},{18,... | collective-permute-start | bytes 3538952 | tf_op jit(solution)/shard_map/ppermute | solution.py:41
  106.8 26.9 %collective-permute-start.10 = (bf16[512,768]{1,0:T(8,128)(2,1)S(1)}, bf16[512,768]{1,0:T(8,128)(2,1)S(1)}, u32[]{:S(2)}, u32[]{:S(2)}) collective-permute-start(bf16[512,768]{1,0:T(8,128)(2,1)S(1)} %slice.631), channel_id=1, source_target_pairs={{0,1},{1,0},{2,3},{3,2},{4,5},{5,4},{6,7},{7,6},{8,9},{9,8},{10,11... | collective-permute-start | bytes 2359304 | tf_op jit(solution)/shard_map/ppermute | solution.py:45
  106.9 17.2 %collective-permute-start.22 = (bf16[1,1,1,1,48,1536]{5,4,3,2,1,0:T(8,128)(2,1)S(1)}, bf16[1,1,1,1,48,1536]{5,4,3,2,1,0:T(8,128)(2,1)S(1)}, u32[]{:S(2)}, u32[]{:S(2)}) collective-permute-start(bf16[1,1,1,1,48,1536]{5,4,3,2,1,0:T(8,128)(2,1)S(1)} %bitcast.191), channel_id=1, source_target_pairs={{0,16},{2,18},{4,20},{6,22},{8,24},{10,26},{12,28},{14,30},{16,0},... | collective-permute-start | bytes 442376 | tf_op jit(solution)/shard_map/ppermute | solution.py:41
  107.6 19.7 %collective-permute-start.31 = (bf16[1,1,1,1,48,1536]{5,4,3,2,1,0:T(8,128)(2,1)S(1)}, bf16[1,1,1,1,48,1536]{5,4,3,2,1,0:T(8,128)(2,1)S(1)}, u32[]{:S(2)}, u32[]{:S(2)}) collective-permute-start(bf16[1,1,1,1,48,1536]{5,4,3,2,1,0:T(8,128)(2,1)S(1)} %bitcast.186), channel_id=1, source_target_pairs={{0,16},{2,18},{4,20},{6,22},{8,24},{10,26},{12,28},{14,30},{16,0},... | collective-permute-start | bytes 442376 | tf_op jit(solution)/shard_map/ppermute | solution.py:41
  109.9 20.0 %collective-permute-start.27 = (bf16[1,1,1,1,48,1536]{5,4,3,2,1,0:T(8,128)(2,1)S(1)}, bf16[1,1,1,1,48,1536]{5,4,3,2,1,0:T(8,128)(2,1)S(1)}, u32[]{:S(2)}, u32[]{:S(2)}) collective-permute-start(bf16[1,1,1,1,48,1536]{5,4,3,2,1,0:T(8,128)(2,1)S(1)} %bitcast.181), channel_id=1, source_target_pairs={{0,16},{2,18},{4,20},{6,22},{8,24},{10,26},{12,28},{14,30},{16,0},... | collective-permute-start | bytes 442376 | tf_op jit(solution)/shard_map/ppermute | solution.py:41
  132.2 18.9 %collective-permute-start.24 = (bf16[2,1,1,2,48,1536]{5,4,3,2,1,0:T(8,128)(2,1)S(1)}, bf16[2,1,1,2,48,1536]{5,4,3,2,1,0:T(8,128)(2,1)S(1)}, u32[]{:S(2)}, u32[]{:S(2)}) collective-permute-start(bf16[2,1,1,2,48,1536]{5,4,3,2,1,0:T(8,128)(2,1)S(1)} %pad_maximum_fusion.25), channel_id=1, source_target_pairs={{0,4},{2,6},{4,0},{6,2},{8,12},{10,14},{12,8},{14,10},{16,20},{18,... | collective-permute-start | bytes 1769480 | tf_op jit(solution)/shard_map/ppermute | solution.py:41
  136.0 16.3 %collective-permute-start.11 = (bf16[512,768]{1,0:T(8,128)(2,1)S(1)}, bf16[512,768]{1,0:T(8,128)(2,1)S(1)}, u32[]{:S(2)}, u32[]{:S(2)}) collective-permute-start(bf16[512,768]{1,0:T(8,128)(2,1)S(1)} %fusion.15), channel_id=1, source_target_pairs={{0,1},{1,0},{2,3},{3,2},{4,5},{5,4},{6,7},{7,6},{8,9},{9,8},{10,11... | collective-permute-start | bytes 2359304 | tf_op jit(solution)/shard_map/ppermute | solution.py:45
  140.3 31.5 %collective-permute-start.33 = (bf16[2,2,1,1,48,1536]{5,4,3,2,1,0:T(8,128)(2,1)}, bf16[2,2,1,1,48,1536]{5,4,3,2,1,0:T(8,128)(2,1)}, u32[]{:S(2)}, u32[]{:S(2)}) collective-permute-start(bf16[2,2,1,1,48,1536]{5,4,3,2,1,0:T(8,128)(2,1)} %pad_maximum_fusion.27), channel_id=1, source_target_pairs={{0,2},{2,0},{4,6},{6,4},{8,10},{10,8},{12,14},{14,12},{16,18},{18,... | collective-permute-start | bytes 1769480 | tf_op jit(solution)/shard_map/ppermute | solution.py:41
  143.4 32.0 %collective-permute-start.29 = (bf16[2,1,2,1,48,1536]{5,4,3,2,1,0:T(8,128)(2,1)}, bf16[2,1,2,1,48,1536]{5,4,3,2,1,0:T(8,128)(2,1)}, u32[]{:S(2)}, u32[]{:S(2)}) collective-permute-start(bf16[2,1,2,1,48,1536]{5,4,3,2,1,0:T(8,128)(2,1)} %pad_maximum_fusion.26), channel_id=1, source_target_pairs={{0,8},{2,10},{4,12},{6,14},{8,0},{10,2},{12,4},{14,6},{16,24},{18,... | collective-permute-start | bytes 1769480 | tf_op jit(solution)/shard_map/ppermute | solution.py:41
  152.3 31.5 %collective-permute-start.25 = (bf16[2,1,2,2,48,1536]{5,4,3,2,1,0:T(8,128)(2,1)}, bf16[2,1,2,2,48,1536]{5,4,3,2,1,0:T(8,128)(2,1)}, u32[]{:S(2)}, u32[]{:S(2)}) collective-permute-start(bf16[2,1,2,2,48,1536]{5,4,3,2,1,0:T(8,128)(2,1)} %pad_maximum_fusion.13), channel_id=1, source_target_pairs={{0,8},{2,10},{4,12},{6,14},{8,0},{10,2},{12,4},{14,6},{16,24},{18,... | collective-permute-start | bytes 3538952 | tf_op jit(solution)/shard_map/ppermute | solution.py:41
  171.7 13.6 %collective-permute-start.20 = (bf16[512,768]{1,0:T(8,128)(2,1)S(1)}, bf16[512,768]{1,0:T(8,128)(2,1)S(1)}, u32[]{:S(2)}, u32[]{:S(2)}) collective-permute-start(bf16[512,768]{1,0:T(8,128)(2,1)S(1)} %slice.640), channel_id=1, source_target_pairs={{0,1},{1,0},{2,3},{3,2},{4,5},{5,4},{6,7},{7,6},{8,9},{9,8},{10,11... | collective-permute-start | bytes 2359304 | tf_op jit(solution)/shard_map/ppermute | solution.py:45
  173.8 27.6 %collective-permute-start.34 = (bf16[2,2,1,2,48,1536]{5,4,3,2,1,0:T(8,128)(2,1)S(1)}, bf16[2,2,1,2,48,1536]{5,4,3,2,1,0:T(8,128)(2,1)S(1)}, u32[]{:S(2)}, u32[]{:S(2)}) collective-permute-start(bf16[2,2,1,2,48,1536]{5,4,3,2,1,0:T(8,128)(2,1)S(1)} %pad_maximum_fusion.15), channel_id=1, source_target_pairs={{0,4},{2,6},{4,0},{6,2},{8,12},{10,14},{12,8},{14,10},{16,20},{18,... | collective-permute-start | bytes 3538952 | tf_op jit(solution)/shard_map/ppermute | solution.py:41
  177.6 34.3 %collective-permute-start.30 = (bf16[2,2,2,1,48,1536]{5,4,3,2,1,0:T(8,128)(2,1)}, bf16[2,2,2,1,48,1536]{5,4,3,2,1,0:T(8,128)(2,1)}, u32[]{:S(2)}, u32[]{:S(2)}) collective-permute-start(bf16[2,2,2,1,48,1536]{5,4,3,2,1,0:T(8,128)(2,1)} %pad_maximum_fusion.14), channel_id=1, source_target_pairs={{0,2},{2,0},{4,6},{6,4},{8,10},{10,8},{12,14},{14,12},{16,18},{18,... | collective-permute-start | bytes 3538952 | tf_op jit(solution)/shard_map/ppermute | solution.py:41
  186.6 17.4 %collective-permute-start.21 = (f32[4,768]{1,0:T(4,128)S(1)}, f32[4,768]{1,0:T(4,128)S(1)}, u32[]{:S(2)}, u32[]{:S(2)}) collective-permute-start(f32[4,768]{1,0:T(4,128)S(1)} %bitcast.220), channel_id=1, source_target_pairs={{0,1},{1,0},{2,3},{3,2},{4,5},{5,4},{6,7},{7,6},{8,9},{9,8},{10,11... | collective-permute-start | bytes 36872 | tf_op jit(solution)/shard_map/ppermute | solution.py:45
  225.1 77.8 %collective-permute-start.63 = (bf16[2,2,2,1,48,1536]{5,4,3,2,1,0:T(8,128)(2,1)}, bf16[2,2,2,1,48,1536]{5,4,3,2,1,0:T(8,128)(2,1)}, u32[]{:S(2)}, u32[]{:S(2)}) collective-permute-start(bf16[2,2,2,1,48,1536]{5,4,3,2,1,0:T(8,128)(2,1)} %slice.713), channel_id=1, source_target_pairs={{0,2},{2,0},{4,6},{6,4},{8,10},{10,8},{12,14},{14,12},{16,18},{18,... | collective-permute-start | bytes 3538952 | tf_op jit(solution)/shard_map/ppermute | solution.py:41
  227.8 111.7 %collective-permute-start.71 = (bf16[2,2,1,2,48,1536]{5,4,3,2,1,0:T(8,128)(2,1)}, bf16[2,2,1,2,48,1536]{5,4,3,2,1,0:T(8,128)(2,1)}, u32[]{:S(2)}, u32[]{:S(2)}) collective-permute-start(bf16[2,2,1,2,48,1536]{5,4,3,2,1,0:T(8,128)(2,1)} %slice.729), channel_id=1, source_target_pairs={{0,4},{2,6},{4,0},{6,2},{8,12},{10,14},{12,8},{14,10},{16,20},{18,... | collective-permute-start | bytes 3538952 | tf_op jit(solution)/shard_map/ppermute | solution.py:41
  237.2 63.6 %collective-permute-start.47 = (bf16[2,1,2,2,48,1152]{5,4,3,2,1,0:T(8,128)(2,1)}, bf16[2,1,2,2,48,1152]{5,4,3,2,1,0:T(8,128)(2,1)}, u32[]{:S(2)}, u32[]{:S(2)}) collective-permute-start(bf16[2,1,2,2,48,1152]{5,4,3,2,1,0:T(8,128)(2,1)} %slice.681), channel_id=1, source_target_pairs={{0,8},{2,10},{4,12},{6,14},{8,0},{10,2},{12,4},{14,6},{16,24},{18,... | collective-permute-start | bytes 2654216 | tf_op jit(solution)/shard_map/ppermute | solution.py:41
  239.2 26.8 %collective-permute-start.55 = (bf16[2,1,2,2,48,384]{5,4,3,2,1,0:T(8,128)(2,1)S(1)}, bf16[2,1,2,2,48,384]{5,4,3,2,1,0:T(8,128)(2,1)S(1)}, u32[]{:S(2)}, u32[]{:S(2)}) collective-permute-start(bf16[2,1,2,2,48,384]{5,4,3,2,1,0:T(8,128)(2,1)S(1)} %slice.697), channel_id=1, source_target_pairs={{0,8},{2,10},{4,12},{6,14},{8,0},{10,2},{12,4},{14,6},{16,24},{18,... | collective-permute-start | bytes 884744 | tf_op jit(solution)/shard_map/ppermute | solution.py:41
  244.1 37.3 %collective-permute-start.39 = (bf16[512,768]{1,0:T(8,128)(2,1)S(1)}, bf16[512,768]{1,0:T(8,128)(2,1)S(1)}, u32[]{:S(2)}, u32[]{:S(2)}) collective-permute-start(bf16[512,768]{1,0:T(8,128)(2,1)S(1)} %convert_element_type.453), channel_id=1, source_target_pairs={{0,1},{1,0},{2,3},{3,2},{4,5},{5,4},{6,7},{7,6},{8,9},{9,8},{10,11... | collective-permute-start | bytes 2359304 | tf_op jit(solution)/shard_map/ppermute | solution.py:45
  289.1 58.6 %collective-permute-start.40 = (bf16[512,768]{1,0:T(8,128)(2,1)}, bf16[512,768]{1,0:T(8,128)(2,1)}, u32[]{:S(2)}, u32[]{:S(2)}) collective-permute-start(bf16[512,768]{1,0:T(8,128)(2,1)} %slice.669), channel_id=1, source_target_pairs={{0,1},{1,0},{2,3},{3,2},{4,5},{5,4},{6,7},{7,6},{8,9},{9,8},{10,11... | collective-permute-start | bytes 2359304 | tf_op jit(solution)/shard_map/ppermute | solution.py:45
  294.7 66.7 %collective-permute-start.59 = (bf16[2,2,2,1,48,1536]{5,4,3,2,1,0:T(8,128)(2,1)}, bf16[2,2,2,1,48,1536]{5,4,3,2,1,0:T(8,128)(2,1)}, u32[]{:S(2)}, u32[]{:S(2)}) collective-permute-start(bf16[2,2,2,1,48,1536]{5,4,3,2,1,0:T(8,128)(2,1)} %slice.705), channel_id=1, source_target_pairs={{0,2},{2,0},{4,6},{6,4},{8,10},{10,8},{12,14},{14,12},{16,18},{18,... | collective-permute-start | bytes 3538952 | tf_op jit(solution)/shard_map/ppermute | solution.py:41
  300.8 63.8 %collective-permute-start.67 = (bf16[2,2,1,2,48,1536]{5,4,3,2,1,0:T(8,128)(2,1)}, bf16[2,2,1,2,48,1536]{5,4,3,2,1,0:T(8,128)(2,1)}, u32[]{:S(2)}, u32[]{:S(2)}) collective-permute-start(bf16[2,2,1,2,48,1536]{5,4,3,2,1,0:T(8,128)(2,1)} %slice.721), channel_id=1, source_target_pairs={{0,4},{2,6},{4,0},{6,2},{8,12},{10,14},{12,8},{14,10},{16,20},{18,... | collective-permute-start | bytes 3538952 | tf_op jit(solution)/shard_map/ppermute | solution.py:41
  302.9 35.0 %collective-permute-start.48 = (bf16[2,1,1,2,48,1152]{5,4,3,2,1,0:T(8,128)(2,1)S(1)}, bf16[2,1,1,2,48,1152]{5,4,3,2,1,0:T(8,128)(2,1)S(1)}, u32[]{:S(2)}, u32[]{:S(2)}) collective-permute-start(bf16[2,1,1,2,48,1152]{5,4,3,2,1,0:T(8,128)(2,1)S(1)} %slice.683), channel_id=1, source_target_pairs={{0,4},{2,6},{4,0},{6,2},{8,12},{10,14},{12,8},{14,10},{16,20},{18,... | collective-permute-start | bytes 1327112 | tf_op jit(solution)/shard_map/ppermute | solution.py:41
  337.9 18.3 %collective-permute-start.64 = (bf16[2,1,2,1,48,1536]{5,4,3,2,1,0:T(8,128)(2,1)}, bf16[2,1,2,1,48,1536]{5,4,3,2,1,0:T(8,128)(2,1)}, u32[]{:S(2)}, u32[]{:S(2)}) collective-permute-start(bf16[2,1,2,1,48,1536]{5,4,3,2,1,0:T(8,128)(2,1)} %slice.715), channel_id=1, source_target_pairs={{0,8},{2,10},{4,12},{6,14},{8,0},{10,2},{12,4},{14,6},{16,24},{18,... | collective-permute-start | bytes 1769480 | tf_op jit(solution)/shard_map/ppermute | solution.py:41
  345.5 13.1 %collective-permute-start.72 = (bf16[2,2,1,1,48,1536]{5,4,3,2,1,0:T(8,128)(2,1)}, bf16[2,2,1,1,48,1536]{5,4,3,2,1,0:T(8,128)(2,1)}, u32[]{:S(2)}, u32[]{:S(2)}) collective-permute-start(bf16[2,2,1,1,48,1536]{5,4,3,2,1,0:T(8,128)(2,1)} %slice.731), channel_id=1, source_target_pairs={{0,2},{2,0},{4,6},{6,4},{8,10},{10,8},{12,14},{14,12},{16,18},{18,... | collective-permute-start | bytes 1769480 | tf_op jit(solution)/shard_map/ppermute | solution.py:41
  354.5 33.5 %collective-permute-start.41 = (bf16[512,768]{1,0:T(8,128)(2,1)}, bf16[512,768]{1,0:T(8,128)(2,1)}, u32[]{:S(2)}, u32[]{:S(2)}) collective-permute-start(bf16[512,768]{1,0:T(8,128)(2,1)} %convert_element_type.459), channel_id=1, source_target_pairs={{0,1},{1,0},{2,3},{3,2},{4,5},{5,4},{6,7},{7,6},{8,9},{9,8},{10,11... | collective-permute-start | bytes 2359304 | tf_op jit(solution)/shard_map/ppermute | solution.py:45
  364.0 63.5 %collective-permute-start.60 = (bf16[2,1,2,1,48,1536]{5,4,3,2,1,0:T(8,128)(2,1)}, bf16[2,1,2,1,48,1536]{5,4,3,2,1,0:T(8,128)(2,1)}, u32[]{:S(2)}, u32[]{:S(2)}) collective-permute-start(bf16[2,1,2,1,48,1536]{5,4,3,2,1,0:T(8,128)(2,1)} %slice.707), channel_id=1, source_target_pairs={{0,8},{2,10},{4,12},{6,14},{8,0},{10,2},{12,4},{14,6},{16,24},{18,... | collective-permute-start | bytes 1769480 | tf_op jit(solution)/shard_map/ppermute | solution.py:41
  367.1 83.8 %collective-permute-start.68 = (bf16[2,2,1,1,48,1536]{5,4,3,2,1,0:T(8,128)(2,1)}, bf16[2,2,1,1,48,1536]{5,4,3,2,1,0:T(8,128)(2,1)}, u32[]{:S(2)}, u32[]{:S(2)}) collective-permute-start(bf16[2,2,1,1,48,1536]{5,4,3,2,1,0:T(8,128)(2,1)} %slice.723), channel_id=1, source_target_pairs={{0,2},{2,0},{4,6},{6,4},{8,10},{10,8},{12,14},{14,12},{16,18},{18,... | collective-permute-start | bytes 1769480 | tf_op jit(solution)/shard_map/ppermute | solution.py:41
  368.7 16.0 %collective-permute-start.66 = (bf16[1,1,1,1,48,1536]{5,4,3,2,1,0:T(8,128)(2,1)S(1)}, bf16[1,1,1,1,48,1536]{5,4,3,2,1,0:T(8,128)(2,1)S(1)}, u32[]{:S(2)}, u32[]{:S(2)}) collective-permute-start(bf16[1,1,1,1,48,1536]{5,4,3,2,1,0:T(8,128)(2,1)S(1)} %slice.719), channel_id=1, source_target_pairs={{0,16},{2,18},{4,20},{6,22},{8,24},{10,26},{12,28},{14,30},{16,0},... | collective-permute-start | bytes 442376 | tf_op jit(solution)/shard_map/ppermute | solution.py:41
  370.6 16.5 %collective-permute-start.74 = (bf16[1,1,1,1,48,1536]{5,4,3,2,1,0:T(8,128)(2,1)S(1)}, bf16[1,1,1,1,48,1536]{5,4,3,2,1,0:T(8,128)(2,1)S(1)}, u32[]{:S(2)}, u32[]{:S(2)}) collective-permute-start(bf16[1,1,1,1,48,1536]{5,4,3,2,1,0:T(8,128)(2,1)S(1)} %slice.735), channel_id=1, source_target_pairs={{0,16},{2,18},{4,20},{6,22},{8,24},{10,26},{12,28},{14,30},{16,0},... | collective-permute-start | bytes 442376 | tf_op jit(solution)/shard_map/ppermute | solution.py:41
  413.6 83.3 %collective-permute-start.42 = (bf16[512,768]{1,0:T(8,128)(2,1)}, bf16[512,768]{1,0:T(8,128)(2,1)}, u32[]{:S(2)}, u32[]{:S(2)}) collective-permute-start(bf16[512,768]{1,0:T(8,128)(2,1)} %slice.671), channel_id=1, source_target_pairs={{0,1},{1,0},{2,3},{3,2},{4,5},{5,4},{6,7},{7,6},{8,9},{9,8},{10,11... | collective-permute-start | bytes 2359304 | tf_op jit(solution)/shard_map/ppermute | solution.py:45
  419.8 64.0 %collective-permute-start.43 = (bf16[2,1,2,2,48,1152]{5,4,3,2,1,0:T(8,128)(2,1)}, bf16[2,1,2,2,48,1152]{5,4,3,2,1,0:T(8,128)(2,1)}, u32[]{:S(2)}, u32[]{:S(2)}) collective-permute-start(bf16[2,1,2,2,48,1152]{5,4,3,2,1,0:T(8,128)(2,1)} %slice.673), channel_id=1, source_target_pairs={{0,8},{2,10},{4,12},{6,14},{8,0},{10,2},{12,4},{14,6},{16,24},{18,... | collective-permute-start | bytes 2654216 | tf_op jit(solution)/shard_map/ppermute | solution.py:41
  427.4 21.6 %collective-permute-start.51 = (bf16[2,1,2,2,48,384]{5,4,3,2,1,0:T(8,128)(2,1)S(1)}, bf16[2,1,2,2,48,384]{5,4,3,2,1,0:T(8,128)(2,1)S(1)}, u32[]{:S(2)}, u32[]{:S(2)}) collective-permute-start(bf16[2,1,2,2,48,384]{5,4,3,2,1,0:T(8,128)(2,1)S(1)} %slice.689), channel_id=1, source_target_pairs={{0,8},{2,10},{4,12},{6,14},{8,0},{10,2},{12,4},{14,6},{16,24},{18,... | collective-permute-start | bytes 884744 | tf_op jit(solution)/shard_map/ppermute | solution.py:41
  432.2 35.2 %collective-permute-start.61 = (bf16[2,1,1,1,48,1536]{5,4,3,2,1,0:T(8,128)(2,1)}, bf16[2,1,1,1,48,1536]{5,4,3,2,1,0:T(8,128)(2,1)}, u32[]{:S(2)}, u32[]{:S(2)}) collective-permute-start(bf16[2,1,1,1,48,1536]{5,4,3,2,1,0:T(8,128)(2,1)} %slice.709), channel_id=1, source_target_pairs={{0,4},{2,6},{4,0},{6,2},{8,12},{10,14},{12,8},{14,10},{16,20},{18,... | collective-permute-start | bytes 884744 | tf_op jit(solution)/shard_map/ppermute | solution.py:41
  454.4 18.5 %collective-permute-start.69 = (bf16[2,1,1,1,48,1536]{5,4,3,2,1,0:T(8,128)(2,1)}, bf16[2,1,1,1,48,1536]{5,4,3,2,1,0:T(8,128)(2,1)}, u32[]{:S(2)}, u32[]{:S(2)}) collective-permute-start(bf16[2,1,1,1,48,1536]{5,4,3,2,1,0:T(8,128)(2,1)} %slice.725), channel_id=1, source_target_pairs={{0,8},{2,10},{4,12},{6,14},{8,0},{10,2},{12,4},{14,6},{16,24},{18,... | collective-permute-start | bytes 884744 | tf_op jit(solution)/shard_map/ppermute | solution.py:41
  (162 other events, 1301.0 us)

commit v2 on v1

v2 whole, which is shorter than its diff:
```python
import functools
import math

import jax
import jax.numpy as jnp
import numpy as np
from jax import lax
from jax.experimental import pallas as pl
from jax.experimental.pallas import tpu as pltpu
from jax.sharding import PartitionSpec as P

HD = 64
SEG = 128
NEG_FILL = -1000000000.0
EPS_NORM = 1e-06
BF = jnp.bfloat16
F32 = jnp.float32
INV_SQRT2 = 1.0 / math.sqrt(2.0)
INV_SQRT2PI = 1.0 / math.sqrt(2.0 * math.pi)
SM_SCALE = HD ** (-0.5)
PAIR = 2 * HD
PIECES = 3
BRIEF = pl.CostEstimate(flops=1, bytes_accessed=1, transcendentals=0)


def dot_nn(a, b):
    return lax.dot_general(a, b, (((1,), (0,)), ((), ())), preferred_element_type=F32)


def dot_nt(a, b):
    return lax.dot_general(a, b, (((1,), (1,)), ((), ())), preferred_element_type=F32)


def dot_tn(a, b):
    return lax.dot_general(a, b, (((0,), (0,)), ((), ())), preferred_element_type=F32)


def dot_exact(a, b):
    return lax.dot_general(
        a, b, (((1,), (0,)), ((), ())), precision=lax.Precision.HIGHEST, preferred_element_type=F32
    )


def swap_dp(values, bit, count):
    return lax.ppermute(values, "dp", [(i, i ^ (1 << bit)) for i in range(count)])


def swap_tensor(values):
    return lax.ppermute(values, "tensor", [(0, 1), (1, 0)])


def bit_orders(bits):
    if bits == 4:
        return ((3, 2, 0, 1), (3, 1, 2, 0), (3, 0, 1, 2))
    base = tuple(range(bits))
    return (base, base[1:] + base[:1], base[2:] + base[:2])


def tie(*values):
    return lax.optimization_barrier(values)


def join(low, high, bit, bits):
    return jnp.concatenate([low, high], axis=bits - 1 - bit)


class Gather:
    def __init__(self, pieces, orders, bits, count):
        self.state = [u.reshape((1,) * bits + u.shape) for u in pieces]
        self.orders, self.bits, self.count, self.step = orders, bits, count, 0

    def send(self):
        self.flying = [
            swap_dp(v, self.orders[i][self.step], self.count) for i, v in enumerate(self.state)
        ]

    def land(self):
        self.state = [
            join(v, f, self.orders[i][self.step], self.bits)
            for i, (v, f) in enumerate(zip(self.state, self.flying))
        ]
        self.step += 1

    def left(self):
        return self.bits - self.step

    def results(self):
        return [v.reshape((-1, v.shape[-1])) for v in self.state]


def half_of(values, axis, index):
    return lax.index_in_dim(values, index, axis, keepdims=True)


class Scatter:
    def __init__(self, pieces, orders, bits, count):
        self.bits, self.count, self.step = bits, count, 0
        self.orders = [tuple(reversed(o)) for o in orders]
        self.parts = [[[m.reshape((2,) * bits + (-1, m.shape[-1])) for m in piece]] for piece in pieces]

    def half(self, which, index):
        axis = self.bits - 1 - self.orders[which][self.step]
        cut = [
            jnp.concatenate([half_of(m, axis, index) for m in part], axis=-1).astype(F32)
            for part in self.parts[which]
        ]
        return sum(cut[1:], cut[0]).astype(BF)

    def prepare(self):
        self.leaving = [self.half(i, 1) for i in range(len(self.parts))]

    def send(self):
        self.flying = [
            swap_dp(v, self.orders[i][self.step], self.count) for i, v in enumerate(self.leaving)
        ]
        self.kept = [self.half(i, 0) for i in range(len(self.parts))]

    def land(self):
        self.parts = [[[k], [f]] for k, f in zip(self.kept, self.flying)]
        self.step += 1

    def left(self):
        return self.bits - self.step

    def pairs(self):
        return [side[0].reshape((-1, side[0].shape[-1])) for part in self.parts for side in part]


def settle(anchor, *moving):
    flat = [f for m in moving for f in m.flying]
    anchor, *flat = tie(anchor, *flat)
    for m in moving:
        m.flying = flat[: len(m.flying)]
        flat = flat[len(m.flying) :]
        m.land()
    return anchor


def launch(anchor, *moving):
    for m in moving:
        if isinstance(m, Scatter):
            m.prepare()
            anchor, *m.leaving = tie(anchor, *m.leaving)
        elif isinstance(m, Gather):
            anchor, *m.state = tie(anchor, *m.state)
        else:
            anchor, m.state = tie(anchor, m.state)
        m.send()
    return anchor


def pair_masks(rows):
    lane = lax.broadcasted_iota(jnp.int32, (rows, PAIR), 1)
    return lane < HD


def stack_heads(two, low_half):
    zero = jnp.zeros_like(two)
    return jnp.concatenate([jnp.where(low_half, two, zero), jnp.where(low_half, zero, two)], axis=0)


def merge_heads(stacked, low_half, rows):
    return jnp.where(low_half, stacked[:rows], stacked[rows:])


def pair_probs(q_stack, key_two, allowed):
    scores = dot_nt(q_stack, key_two) * SM_SCALE
    scores = jnp.where(allowed, scores, NEG_FILL)
    expo = jnp.exp(scores - jnp.max(scores, axis=-1, keepdims=True))
    return expo * (1.0 / jnp.sum(expo, axis=-1, keepdims=True))


def row_window(rows):
    return [pl.BlockSpec((SEG, cols), lambda i, c: (i, 0)) for cols in rows]


def attn_fwd_kernel(count_ref, qkv_ref, out_ref):
    rows = qkv_ref.shape[0]
    low_half = pair_masks(rows)
    allowed = lax.broadcasted_iota(jnp.int32, (2 * rows, rows), 1) < count_ref[pl.program_id(0)]
    for pair in range(out_ref.shape[1] // PAIR):
        at = 3 * pair * PAIR
        q_stack = stack_heads(qkv_ref[:, at : at + PAIR], low_half)
        probs = pair_probs(q_stack, qkv_ref[:, at + PAIR : at + 2 * PAIR], allowed)
        mixed = dot_nn(probs.astype(BF), qkv_ref[:, at + 2 * PAIR : at + 3 * PAIR])
        out_ref[:, pair * PAIR : (pair + 1) * PAIR] = merge_heads(mixed, low_half, rows).astype(BF)


def pair_bwd(qkv, grad, allowed, low_half):
    rows = grad.shape[0]
    key_two = qkv[:, PAIR : 2 * PAIR]
    q_stack = stack_heads(qkv[:, :PAIR], low_half)
    g_stack = stack_heads(grad, low_half)
    probs = pair_probs(q_stack, key_two, allowed)
    grad_probs = dot_nt(g_stack, qkv[:, 2 * PAIR :])
    inner = jnp.sum(grad_probs * probs, axis=-1, keepdims=True)
    grad_scores = jnp.where(allowed, probs * (grad_probs - inner), 0.0).astype(BF)
    return (
        merge_heads(dot_nn(grad_scores, key_two), low_half, rows) * SM_SCALE,
        dot_tn(grad_scores, q_stack) * SM_SCALE,
        dot_tn(probs.astype(BF), g_stack),
    )


def attn_bwd_kernel(count_ref, qkv_ref, grad_ref, first_ref, out_ref, sums_ref):
    rows = qkv_ref.shape[0]
    low_half = pair_masks(rows)
    allowed = lax.broadcasted_iota(jnp.int32, (2 * rows, rows), 1) < count_ref[pl.program_id(0)]
    is_first = lax.broadcasted_iota(jnp.int32, (rows, PAIR), 0) == 0

    @pl.when(pl.program_id(0) == 0)
    def _():
        sums_ref[...] = jnp.zeros_like(sums_ref)

    for pair in range(grad_ref.shape[1] // PAIR):
        at = 3 * pair * PAIR
        span = slice(pair * PAIR, (pair + 1) * PAIR)
        grad = jnp.where(is_first, first_ref[0, :, span], grad_ref[:, span].astype(F32)).astype(BF)
        for k, values in enumerate(pair_bwd(qkv_ref[:, at : at + 3 * PAIR], grad, allowed, low_half)):
            low = values.astype(BF)
            to = slice(at + k * PAIR, at + (k + 1) * PAIR)
            out_ref[:, to] = low
            sums_ref[:, to] += jnp.sum(low.astype(F32), axis=0, keepdims=True)


def attn_fwd(counts, qkv):
    rows, three = qkv.shape
    width = three // 3
    return pl.pallas_call(
        attn_fwd_kernel,
        grid_spec=pltpu.PrefetchScalarGridSpec(
            num_scalar_prefetch=1,
            grid=(rows // SEG,),
            in_specs=row_window([three]),
            out_specs=row_window([width])[0],
        ),
        out_shape=jax.ShapeDtypeStruct((rows, width), BF),
        cost_estimate=BRIEF,
        name="attn_fwd",
    )(counts, qkv)


def attn_bwd(counts, qkv, grad, grad_first):
    rows, three = qkv.shape
    width = three // 3
    return pl.pallas_call(
        attn_bwd_kernel,
        grid_spec=pltpu.PrefetchScalarGridSpec(
            num_scalar_prefetch=1,
            grid=(rows // SEG,),
            in_specs=row_window([three, width]) + [pl.BlockSpec((1, 1, width), lambda i, c: (i, 0, 0))],
            out_specs=row_window([three]) + [pl.BlockSpec((1, three), lambda i, c: (0, 0))],
        ),
        out_shape=[jax.ShapeDtypeStruct((rows, three), BF), jax.ShapeDtypeStruct((1, three), F32)],
        cost_estimate=BRIEF,
        name="attn_bwd",
    )(counts, qkv, grad, grad_first.astype(F32)[:, None, :])


def gelu_pair(pre):
    cdf = 0.5 * (1.0 + lax.erf(pre * INV_SQRT2))
    return pre * cdf, cdf + pre * (jnp.exp(-0.5 * pre * pre) * INV_SQRT2PI)


def up_kernel(rows_ref, w_ref, bias_ref, act_ref, slope_ref):
    act, slope = gelu_pair(dot_nn(rows_ref[...], w_ref[...]) + bias_ref[...])
    act_ref[...] = act.astype(BF)
    slope_ref[...] = slope.astype(BF)


def up_gelu(rows, w_up, bias):
    total, dim = rows.shape
    hidden = w_up.shape[1]
    tile_r = min(256, total)
    tile_h = min(512, hidden)
    spec_out = pl.BlockSpec((tile_r, tile_h), lambda j, i: (i, j))
    return pl.pallas_call(
        up_kernel,
        grid=(hidden // tile_h, total // tile_r),
        in_specs=[
            pl.BlockSpec((tile_r, dim), lambda j, i: (i, 0)),
            pl.BlockSpec((dim, tile_h), lambda j, i: (0, j)),
            pl.BlockSpec((1, tile_h), lambda j, i: (0, j)),
        ],
        out_specs=[spec_out, spec_out],
        out_shape=[jax.ShapeDtypeStruct((total, hidden), BF)] * 2,
        cost_estimate=BRIEF,
        name="up_gelu",
    )(rows, w_up, bias[None, :])


def cls_attn_kernel(count_ref, rows_ref, w0, w1, w2, bias_ref, qkv_ref, att_ref, sum_ref):
    rows = rows_ref.shape[0]
    low_half = pair_masks(rows)
    allowed = lax.broadcasted_iota(jnp.int32, (2 * rows, rows), 1) < count_ref[0]
    total = jnp.zeros(sum_ref.shape, F32)
    for p, w in enumerate((w0, w1, w2)):
        span = slice(3 * p * PAIR, 3 * (p + 1) * PAIR)
        qkv = (dot_nn(rows_ref[...], w[:, : 3 * PAIR]) + bias_ref[:, span]).astype(BF)
        qkv_ref[:, span] = qkv
        probs = pair_probs(stack_heads(qkv[:, :PAIR], low_half), qkv[:, PAIR : 2 * PAIR], allowed)
        att = merge_heads(dot_nn(probs.astype(BF), qkv[:, 2 * PAIR :]), low_half, rows).astype(BF)
        att_ref[:, p * PAIR : (p + 1) * PAIR] = att[: att_ref.shape[0]]
        total += dot_nt(att, w[:, 3 * PAIR :])
    sum_ref[...] = total


def cls_attn_back_kernel(count_ref, grad_ref, w0, w1, w2, qkv_ref, out_ref, sum_ref):
    rows = grad_ref.shape[0]
    low_half = pair_masks(rows)
    allowed = lax.broadcasted_iota(jnp.int32, (2 * rows, rows), 1) < count_ref[0]
    total = jnp.zeros(sum_ref.shape, F32)
    for p, w in enumerate((w0, w1, w2)):
        span = slice(3 * p * PAIR, 3 * (p + 1) * PAIR)
        grad = dot_nn(grad_ref[...], w[:, 3 * PAIR :]).astype(BF)
        low = jnp.concatenate(pair_bwd(qkv_ref[:, span], grad, allowed, low_half), axis=1).astype(BF)
        out_ref[:, span] = low[: out_ref.shape[0]]
        total += dot_nt(low, w[:, : 3 * PAIR])
    sum_ref[...] = total


def cls_up_kernel(rows_ref, u0, u1, u2, d0, d1, d2, bias_ref, act_ref, slope_ref, sum_ref):
    tile = u0.shape[1]
    total = jnp.zeros(sum_ref.shape, F32)
    for p, (u, d) in enumerate(((u0, d0), (u1, d1), (u2, d2))):
        span = slice(p * tile, (p + 1) * tile)
        act, slope = gelu_pair(dot_nn(rows_ref[...], u[...]) + bias_ref[:, span])
        low = act.astype(BF)
        act_ref[:, span] = low[: act_ref.shape[0]]
        slope_ref[:, span] = slope
        total += dot_nt(low, d[...])
    sum_ref[...] = total


def cls_up_back_kernel(rows_ref, u0, u1, u2, d0, d1, d2, slope_ref, out_ref, sum_ref):
    tile = u0.shape[1]
    total = jnp.zeros(sum_ref.shape, F32)
    for p, (u, d) in enumerate(((u0, d0), (u1, d1), (u2, d2))):
        span = slice(p * tile, (p + 1) * tile)
        low = (dot_nn(rows_ref[...], d[...]) * slope_ref[:, span]).astype(BF)
        out_ref[:, span] = low[: out_ref.shape[0]]
        total += dot_nt(low, u[...])
    sum_ref[...] = total


def block_at(at, *_):
    return 0, at


def whole(array):
    return pl.BlockSpec(array.shape, lambda *_: (0,) * array.ndim)


def cls_call(kernel, name, count, before, weights, tile, after, outs):
    shapes = [jax.ShapeDtypeStruct(*o) for o in outs]
    dim = weights[0][0].shape[0]
    scalars = [] if count is None else [count]
    return pl.pallas_call(
        kernel,
        grid_spec=pltpu.PrefetchScalarGridSpec(
            num_scalar_prefetch=len(scalars),
            grid=(1,),
            in_specs=[whole(before)]
            + [pl.BlockSpec((dim, tile), functools.partial(block_at, at)) for _, at in weights]
            + [whole(after)],
            out_specs=[whole(o) for o in shapes],
        ),
        out_shape=shapes,
        cost_estimate=BRIEF,
        name=name,
    )(*scalars, before, *[w for w, _ in weights], after)


def owner_kernel(
    shape, two_ref, one_ref, pick_ref, uk, uf, dk, df, l0k, l0f, l1k, l1f, l2k, l2f,
    qkv_ref, out_ref, up_ref, down_ref, small_ref,
):
    width, hidden, dim, chunk, segments, scale_one, scale_two = shape
    rows = two_ref.shape[0]
    three = 3 * PAIR

    def put_kinds(block, values, add):
        for p in range(PIECES):
            for k in range(3):
                to = slice(k * width + p * PAIR, k * width + (p + 1) * PAIR)
                got = values[p][:, k * PAIR : (k + 1) * PAIR]
                qkv_ref[block, :, to] = qkv_ref[block, :, to] + got if add else got

    @pl.when(pl.program_id(0) == 0)
    def _():
        both = lambda a, b: (a[...].astype(F32) + b[...].astype(F32)) * scale_one
        up_ref[0] = both(uk, uf)
        down_ref[0] = both(dk, df)
        up_ref[1] = jnp.zeros_like(up_ref[1])
        down_ref[1] = jnp.zeros_like(down_ref[1])
        out_ref[1] = jnp.zeros_like(out_ref[1])
        qkv_ref[1] = jnp.zeros_like(qkv_ref[1])
        late = [both(a, b) for a, b in ((l0k, l0f), (l1k, l1f), (l2k, l2f))]
        put_kinds(0, late, False)
        for p in range(PIECES):
            out_ref[0, :, p * PAIR : (p + 1) * PAIR] = late[p][:, three : three + PAIR]
        small_ref[...] = l0k[:, three + PAIR :].astype(F32) + l0f[:, three + PAIR :].astype(F32)

    block = (lax.broadcasted_iota(jnp.int32, (rows, dim), 0) + rows * pl.program_id(0)) // segments
    col = lax.broadcasted_iota(jnp.int32, (rows, dim), 1)
    mine = (col >= block * chunk) & (col < block * chunk + chunk)

    def near(ref, at):
        picked = jnp.where(mine, ref[:, at : at + dim].astype(F32), 0.0).astype(BF)
        return dot_nn(picked, pick_ref[...]).astype(BF)

    at_pre, at_att, at_qkv = hidden, 2 * hidden, 2 * hidden + width
    at_two, at_one = at_qkv + 3 * width, at_qkv
    in_f, first_f, g_attn_f, g_mlp_f = (near(two_ref, at_two + k * dim) for k in range(4))
    first_1, g_mlp_1, g_attn_1 = (near(one_ref, at_one + k * dim) for k in range(3))
    up_ref[0] += dot_tn(first_1, one_ref[:, at_pre:at_att]) * scale_one
    down_ref[0] += dot_tn(g_mlp_1, one_ref[:, :at_pre]) * scale_one
    out_ref[0] += dot_tn(g_attn_1, one_ref[:, at_att:at_qkv]) * scale_one
    up_ref[1] += dot_tn(first_f, two_ref[:, at_pre:at_att]) * scale_two
    down_ref[1] += dot_tn(g_mlp_f, two_ref[:, :at_pre]) * scale_two
    out_ref[1] += dot_tn(g_attn_f, two_ref[:, at_att:at_qkv]) * scale_two
    grad = dot_tn(in_f, two_ref[:, at_qkv:at_two]) * scale_two
    put_kinds(1, [grad[:, p * three : (p + 1) * three] for p in range(PIECES)], True)


def owner_sums(shape, two, one, sums):
    width, hidden, dim, chunk, segments, _, _ = shape
    rows = min(128, two.shape[0])
    pick = jnp.asarray(np.tile(np.eye(chunk), (dim // chunk, 1)), BF)
    outs = [
        jax.ShapeDtypeStruct(o, F32)
        for o in ((2, chunk, 3 * width), (2, chunk, width), (2, chunk, hidden), (2, chunk, hidden), (chunk, PAIR))
    ]
    return pl.pallas_call(
        functools.partial(owner_kernel, shape),
        grid=(two.shape[0] // rows,),
        in_specs=[pl.BlockSpec((rows, m.shape[1]), lambda i: (i, 0)) for m in (two, one)]
        + [whole(m) for m in (pick, *sums)],
        out_specs=[whole(o) for o in outs],
        out_shape=outs,
        cost_estimate=BRIEF,
        name="owner_sums",
    )(two, one, pick, *sums)


def norm_stats(values):
    centred = values - jnp.mean(values, axis=-1, keepdims=True)
    inv = lax.rsqrt(jnp.mean(centred * centred, axis=-1, keepdims=True) + EPS_NORM)
    return centred * inv, inv


def norm_bwd(grad, unit, inv, gain):
    scaled = grad * gain
    along = jnp.mean(scaled * unit, axis=-1, keepdims=True)
    return inv * (scaled - jnp.mean(scaled, axis=-1, keepdims=True) - unit * along)


def column_sum(values):
    return jnp.sum(values, axis=0)


def advance(anchor, *moving):
    anchor = settle(anchor, *moving)
    going = [m for m in moving if m.left()]
    return launch(anchor, *going)


def local(
    layer_input,
    cotangent,
    lengths,
    w_qkv,
    w_out,
    w_up,
    w_down,
    vec_bias,
    norm_gain,
    bias_up,
    seg_pos,
):
    count = lax.axis_size("dp")
    bits = count.bit_length() - 1
    me = lax.axis_index("dp")
    part = lax.axis_index("tensor")
    seqs_here, half, dim = layer_input.shape
    full_len = 2 * half
    segments = full_len // SEG
    seg_half = half // SEG
    chunk = dim // count
    width = w_qkv.shape[3]
    hidden = w_up.shape[2]
    tile = hidden // PIECES
    three = 3 * PAIR
    orders = bit_orders(bits)
    swap_half = swap_tensor

    row_id = lax.broadcasted_iota(jnp.int32, (dim, dim), 0)
    col_id = lax.broadcasted_iota(jnp.int32, (dim, dim), 1)
    perm_hot = row_id == ((col_id // chunk) ^ me) * chunk + col_id % chunk
    perm = perm_hot.astype(BF)
    perm_f = perm_hot.astype(F32)

    def cut(matrix, size, p):
        return matrix[:, p * size : (p + 1) * size]

    def attn_piece(w_three, w_last, p):
        return jnp.concatenate([cut(w_three[:, k], PAIR, p) for k in range(3)] + [cut(w_last.T, PAIR, p)], axis=1)

    span = range(PIECES)
    one_q = Gather([attn_piece(w_qkv[0], w_out[0], p) for p in span], orders, bits, count)

    slot = me * 2 + part
    piece = vec_bias.shape[2]
    place = (
        lax.broadcasted_iota(jnp.int32, (piece, dim), 1)
        == lax.broadcasted_iota(jnp.int32, (piece, dim), 0) + slot * piece
    ).astype(F32)
    piece_up = bias_up.shape[1]
    hidden_all = piece_up * count * 2
    place_up = (
        lax.broadcasted_iota(jnp.int32, (piece_up, hidden_all), 1)
        == lax.broadcasted_iota(jnp.int32, (piece_up, hidden_all), 0) + slot * piece_up
    ).astype(F32)
    small_rows = jnp.concatenate(
        [vec_bias.reshape(-1, piece), norm_gain.reshape(-1, piece), seg_pos], axis=0
    )
    fold = hidden_all // dim
    small = jnp.concatenate(
        [dot_exact(small_rows, place), dot_exact(bias_up, place_up).reshape(2 * fold, dim)], axis=0
    )
    one_q.send()
    small = small + swap_tensor(small)
    for bit in range(bits - 2):
        small = small + swap_dp(small, bit, count)
    small = settle(small, one_q)
    small, w_qkv, w_out, w_up, w_down = tie(small, w_qkv, w_out, w_up, w_down)
    two_attn = jnp.concatenate([attn_piece(w_qkv[1], w_out[1], p) for p in span], axis=1)
    one_m = Gather([w_up[0], w_down[0].T, two_attn], orders[1:] + orders[:1], bits, count)
    two = Gather([w_up[1], w_down[1].T], orders[1:], bits, count)
    got = swap_dp(small, bits - 2, count)
    one_q.send()
    small = small + settle(got, one_q)
    small = launch(small, one_q)
    last = swap_dp(small, bits - 1, count)
    small = advance(small, one_q)
    while one_q.left() > 1:
        small = advance(small, one_q)
    small, *one_m.state = tie(small, *one_m.state)
    small = launch(small, one_m)
    small = small + last

    plain = small[: small_rows.shape[0]]
    up_all = small[small_rows.shape[0] :].reshape(2, 2, hidden)
    rel = dot_exact(plain, perm_f)

    def own_width(row):
        return jnp.where(part == 0, row[:width], row[width:])

    def block_vectors(block, order):
        base = 6 * block
        zero = jnp.zeros((PAIR,), F32)
        bias_q, bias_v = own_width(plain[base]), own_width(plain[base + 1])
        bias_qkv = jnp.concatenate(
            [v for p in span for v in (bias_q[p * PAIR : (p + 1) * PAIR], zero, bias_v[p * PAIR : (p + 1) * PAIR])]
        )
        gain_at = 12 + 2 * block
        return dict(
            qkv=bias_qkv,
            attn=order[base + 2],
            mlp=order[base + 3],
            shift_one=order[base + 4],
            shift_two=order[base + 5],
            gain_one=order[gain_at],
            gain_two=order[gain_at + 1],
            hidden=jnp.where(part == 0, up_all[block, 0], up_all[block, 1]),
        )

    v1, v2 = block_vectors(0, rel), block_vectors(1, rel)
    seg_rows = rel[16 : 16 + segments]

    length = lengths[0]
    seg_ids = jnp.concatenate(
        [part * seg_half + jnp.arange(seg_half), (1 - part) * seg_half + jnp.arange(seg_half)]
    ).astype(jnp.int32)
    seg_counts = jnp.clip(length - seg_ids * SEG, 0, SEG).astype(jnp.int32)
    cls_count = ((lengths + (SEG - 1)) // SEG).astype(jnp.int32)

    pad_rows = -segments % 16

    def padded(rows):
        return jnp.concatenate([rows, jnp.zeros((pad_rows, rows.shape[1]), rows.dtype)], axis=0)

    def turned(rows):
        return jnp.where(part == 0, rows, jnp.concatenate([rows[seg_half:], rows[:seg_half]], axis=0))

    def both_halves(own_rows):
        return turned(jnp.concatenate([own_rows, swap_half(own_rows)], axis=0))

    def own_half(rows):
        return jnp.where(part == 0, rows[:seg_half], rows[seg_half:segments])

    def firsts(rows):
        return rows.reshape(-1, SEG, rows.shape[-1])[:, 0]

    x_own = dot_nn(layer_input[0], perm).astype(BF)
    x_full = jnp.concatenate([x_own, swap_half(x_own)], axis=0)
    x_full = settle(x_full, one_q)
    attn_r = one_q.results()
    w_qkv_r = jnp.concatenate([w[:, :three] for w in attn_r], axis=1)
    w_out_r = jnp.concatenate([w[:, three:] for w in attn_r], axis=1)
    qkv = (dot_nn(x_full, w_qkv_r) + v1["qkv"]).astype(BF)
    qkv = advance(qkv, one_m)
    attended = attn_fwd(seg_counts, qkv)
    while one_m.left() > 2:
        attended = advance(attended, one_m)
    attended, *two.state = tie(attended, *two.state)
    attended = launch(attended, two)
    partial_attn = dot_nt(attended, w_out_r).astype(BF)
    first_sum = (
        partial_attn[:half].astype(F32)
        + swap_half(partial_attn[half:]).astype(F32)
        + v1["attn"]
        + x_own.astype(F32)
    )
    unit_one, inv_one = norm_stats(first_sum)
    first = unit_one * v1["gain_one"] + v1["shift_one"]
    first_low = first.astype(BF)
    first_full = jnp.concatenate([first_low, swap_half(first_low)], axis=0)
    first_full = settle(first_full, one_m, two)
    first_full = launch(first_full, one_m)
    first_full = launch(first_full, two)
    first_full = settle(first_full, one_m)
    w_up_r, w_down_r, two_attn_r = one_m.results()
    act, slope = up_gelu(first_full, w_up_r, v1["hidden"])
    while two.left() > 3:
        act = advance(act, two)
    act = advance(act, two)
    partial_mlp = dot_nt(act, w_down_r).astype(BF)
    second_sum = (
        partial_mlp[:half].astype(F32) + swap_half(partial_mlp[half:]).astype(F32) + v1["mlp"] + first
    )
    while two.left() > 1:
        second_sum = advance(second_sum, two)
    unit_two, inv_two = norm_stats(second_sum)
    first_out = unit_two * v1["gain_two"] + v1["shift_two"]

    row_in = lax.broadcasted_iota(jnp.int32, (half, 1), 0)
    valid = part * half + row_in < length
    is_cls = lax.broadcasted_iota(jnp.int32, (1, SEG, 1), 1) == 0

    def with_cls(rows, cls):
        return jnp.where(is_cls, cls[:, None, :], rows.reshape(seg_half, SEG, dim)).reshape(half, dim)

    cot = jnp.where(valid, cotangent[0], jnp.zeros_like(cotangent[0]))
    grad_y_low = dot_nn(cot, perm).astype(BF)
    grad_out = with_cls(grad_y_low.astype(F32), jnp.zeros((seg_half, dim), F32))
    g_second = norm_bwd(grad_out, unit_two, inv_two, v1["gain_two"])
    g_second_low = g_second.astype(BF)
    g_mlp = jnp.concatenate([g_second_low, swap_half(g_second_low)], axis=0)
    gpre = (dot_nn(g_mlp, w_down_r) * slope.astype(F32)).astype(BF)
    part_h = dot_nt(gpre, w_up_r).astype(BF)
    gw_up = dot_tn(first_full, gpre).astype(BF)
    gw_down = dot_tn(g_mlp, act).astype(BF)
    g_first = part_h[:half].astype(F32) + swap_half(part_h[half:]).astype(F32) + g_second
    g_first_sum = norm_bwd(g_first, unit_one, inv_one, v1["gain_one"])
    g_first_low = g_first_sum.astype(BF)
    g_attn = jnp.concatenate([g_first_low, swap_half(g_first_low)], axis=0)
    g_attended = dot_nn(g_attn, w_out_r).astype(BF)
    gw_out = dot_tn(g_attn, attended).astype(BF)
    early = Scatter([[gw_up], [gw_down]], orders[1:], bits, count)
    g_attended = launch(g_attended, early)

    sums_own = jnp.concatenate([firsts(second_sum), firsts(first_sum)], axis=0)
    sums_other = swap_half(sums_own)
    second_sum_1 = padded(turned(jnp.concatenate([sums_own[:seg_half], sums_other[:seg_half]], axis=0)))
    first_sum_1 = padded(turned(jnp.concatenate([sums_own[seg_half:], sums_other[seg_half:]], axis=0)))
    unit_two_1, inv_two_1 = norm_stats(second_sum_1)
    unit_one_1, inv_one_1 = norm_stats(first_sum_1)
    first_low_1 = (unit_one_1 * v1["gain_one"] + v1["shift_one"]).astype(BF)
    act_1, slope_1, att_1 = (turned(firsts(v)) for v in (act, slope, attended))
    cls_rel = unit_two_1 * v1["gain_two"] + v1["shift_two"]
    cls_in = padded(cls_rel[:segments] + seg_rows)
    g_c = padded(both_halves(firsts(grad_y_low))).astype(F32)

    cls_in, g_attended, gw_out = tie(cls_in, g_attended, gw_out)
    cls_in = settle(cls_in, two)
    attn_w = [(two_attn_r, p) for p in span]
    up_w, down_w = ([(w, p) for p in span] for w in two.results())
    cls_low = cls_in.astype(BF)
    rows_c = cls_in.shape[0]
    qkv_c, att_c, part_c = cls_call(
        cls_attn_kernel, "cls_attn", cls_count, cls_low, attn_w, tile, v2["qkv"][None, :],
        [((rows_c, 3 * width), BF), ((segments, width), BF), ((rows_c, dim), F32)],
    )
    sum_c1 = part_c + swap_half(part_c) + v2["attn"] + cls_in
    unit_c1, inv_c1 = norm_stats(sum_c1)
    first_c = unit_c1 * v2["gain_one"] + v2["shift_one"]
    first_c_low = first_c.astype(BF)
    act_c, slope_c, part_c2 = cls_call(
        cls_up_kernel, "cls_up", None, first_c_low, up_w + down_w, tile, v2["hidden"][None, :],
        [((segments, hidden), BF), ((rows_c, hidden), F32), ((rows_c, dim), F32)],
    )
    sum_c2 = part_c2 + swap_half(part_c2) + v2["mlp"] + first_c
    unit_c2, inv_c2 = norm_stats(sum_c2)
    cls_out = unit_c2 * v2["gain_two"] + v2["shift_two"]
    combined = jnp.where(valid, with_cls(first_out, own_half(cls_out)), 0.0).astype(BF)
    output = dot_nn(combined, perm).astype(BF)[None]

    g_second_c = norm_bwd(g_c, unit_c2, inv_c2, v2["gain_two"])
    g_mlp_c = g_second_c.astype(BF)
    back_outs = [((segments, hidden), BF), ((rows_c, dim), F32)]
    gpre_c, part_g1 = cls_call(
        cls_up_back_kernel, "cls_up_back", None, g_mlp_c, up_w + down_w, tile, slope_c, back_outs
    )
    g_first_c = part_g1 + swap_half(part_g1) + g_second_c
    g_sum_c = norm_bwd(g_first_c, unit_c1, inv_c1, v2["gain_one"])
    g_attn_c = g_sum_c.astype(BF)
    gqkv_c, part_g2 = cls_call(
        cls_attn_back_kernel, "cls_attn_back", cls_count, g_attn_c, attn_w, tile, qkv_c,
        [((segments, 3 * width), BF), ((rows_c, dim), F32)],
    )
    g_cls_in = part_g2 + swap_half(part_g2) + g_sum_c
    near_two = tuple(f[:segments] for f in (cls_low, first_c_low, g_attn_c, g_mlp_c))
    far_two = (act_c, gpre_c, att_c, gqkv_c) + near_two
    wide_two = Gather([jnp.concatenate(far_two, axis=1)], orders[:1], bits, count)
    while early.left() > 3:
        g_cls_in = advance(g_cls_in, early)
    g_cls_in = launch(g_cls_in, wide_two)

    g_second_1 = norm_bwd(g_cls_in, unit_two_1, inv_two_1, v1["gain_two"])
    g_mlp_1 = g_second_1.astype(BF)
    gpre_1, part_1 = cls_call(
        cls_up_back_kernel, "cls_up_back", None, g_mlp_1, [(w, p) for w in (w_up_r, w_down_r) for p in span], tile,
        padded(slope_1.astype(F32)), back_outs
    )
    g_first_1 = part_1 + swap_half(part_1) + g_second_1
    g_sum_1 = norm_bwd(g_first_1, unit_one_1, inv_one_1, v1["gain_one"])
    g_attn_1 = g_sum_1.astype(BF)
    g_att_1 = turned(dot_nn(g_attn_1, w_out_r).astype(BF)[:segments])

    near_one = tuple(f[:segments] for f in (first_low_1, g_mlp_1, g_attn_1))
    far_one = (act_1, gpre_1, att_1) + near_one
    wide_one = Gather([jnp.concatenate(far_one, axis=1)], orders[1:2], bits, count)
    g_att_1 = advance(g_att_1, early, wide_two)
    g_att_1 = launch(g_att_1, wide_one)

    scale_one = 1.0 / math.sqrt(seqs_here * count * full_len)
    scale_two = 1.0 / math.sqrt(seqs_here * count * segments)

    def spread(values, total):
        zero = jnp.zeros((total - values.shape[0],), F32)
        return jnp.where(part == 0, jnp.concatenate([values, zero]), jnp.concatenate([zero, values]))

    def both_sums(rows, cls):
        return (column_sum(rows) + column_sum(own_half(cls))) * scale_one

    def cls_sums(cls):
        return column_sum(own_half(cls)) * scale_two

    sums_c = column_sum(gqkv_c.astype(F32)).reshape(PIECES, 3, PAIR) * scale_two
    rel_rows = jnp.stack(
        [
            both_sums(g_first_sum, g_sum_1),
            both_sums(g_second, g_second_1),
            both_sums(g_first, g_first_1),
            both_sums(grad_out, g_cls_in),
            cls_sums(g_sum_c),
            cls_sums(g_second_c),
            cls_sums(g_first_c),
            cls_sums(g_c),
            both_sums(g_first * unit_one, g_first_1 * unit_one_1),
            both_sums(grad_out * unit_two, g_cls_in * unit_two_1),
            cls_sums(g_first_c * unit_c1),
            cls_sums(g_c * unit_c2),
        ]
    )
    zeros_half = jnp.zeros((seg_half, dim), F32)
    cls_part = own_half(g_cls_in) * scale_two
    seg_grad = jnp.where(
        part == 0,
        jnp.concatenate([cls_part, zeros_half], axis=0),
        jnp.concatenate([zeros_half, cls_part], axis=0),
    )
    up_rows = jnp.stack(
        [
            spread((dot_nn(jnp.ones((16, 2 * half), BF), gpre)[0] + column_sum(gpre_1.astype(F32))) * scale_one, hidden_all),
            spread(column_sum(gpre_c.astype(F32)) * scale_two, hidden_all),
        ]
    )
    per_row = 2 * hidden_all // dim
    by_owner = up_rows.reshape(2, count, -1).transpose(1, 0, 2).reshape(dim, per_row)
    plain_rows = jnp.stack([spread(sums_c[:, k].reshape(-1), dim) for k in (0, 2)])
    canon = dot_exact(jnp.concatenate([plain_rows, by_owner.T], axis=0), perm_f)
    small_rows = jnp.concatenate([rel_rows, seg_grad, canon], axis=0)
    small_rows = small_rows + swap_tensor(small_rows)
    filler = jnp.zeros((PAIR - small_rows.shape[0] - 2, dim), F32)
    small_cols = jnp.concatenate([small_rows, filler], axis=0).T.astype(BF)
    g_att_1, small_cols = tie(g_att_1, small_cols)

    gqkv, gqkv_sums = attn_bwd(seg_counts, qkv, g_attended, g_att_1)
    gqkv = advance(gqkv, early, wide_two, wide_one)
    gw_qkv = dot_tn(x_full, gqkv).astype(BF)
    sums_o = gqkv_sums.reshape(PIECES, 3, PAIR) * scale_one
    bias_own = jnp.stack([spread(sums_o[:, k].reshape(-1), dim) for k in (0, 2)])
    bias_cols = dot_exact(bias_own + swap_tensor(bias_own), perm_f).T.astype(BF)
    small_cols = jnp.concatenate([small_cols, bias_cols], axis=1)
    late = Scatter(
        [[cut(gw_qkv, three, p), cut(gw_out, PAIR, p)] + [small_cols] * (p == 0) for p in span], orders, bits, count
    )
    gqkv = launch(gqkv, late)
    wides = (wide_two, wide_one)
    gqkv = advance(gqkv, *wides)
    part_x = dot_nt(gqkv, w_qkv_r).astype(BF)

    part_x = advance(part_x, late)
    g_first_all = with_cls(g_first_sum, own_half(g_sum_1))
    g_in = part_x[:half].astype(F32) + swap_half(part_x[half:]).astype(F32) + g_first_all
    g_in_high = lax.reduce_precision(g_in, 8, 7)
    grad_input = (dot_nn(g_in_high.astype(BF), perm) + dot_nn((g_in - g_in_high).astype(BF), perm))[None]
    anchor = jnp.zeros((), F32)
    while any(m.left() > 1 for m in (early, *wides)):
        anchor = advance(anchor, *[m for m in (early, *wides) if m.left() > 1])
    while late.left() > 1:
        anchor = advance(anchor, late)
    anchor = settle(anchor, late, early, *wides)

    shape = (width, hidden, dim, chunk, segments, scale_one, scale_two)
    grad_three, grad_last, grad_w_up, grad_down, small_own = owner_sums(
        shape, wide_two.results()[0], wide_one.results()[0], early.pairs() + late.pairs()
    )
    grad_w_qkv = grad_three.reshape(2, chunk, 3, width)
    grad_w_out = grad_last.transpose(0, 2, 1)
    grad_w_down = grad_down.transpose(0, 2, 1)

    mine = small_own.T
    rows_own = jnp.where(part == 0, mine[:, :piece], mine[:, piece:])
    vecs = rows_own[:12]
    grad_vec = jnp.concatenate([rows_own[PAIR - 2 :], vecs[:4], rows_own[20:22], vecs[4:8]], axis=0).reshape(2, 6, piece)
    grad_gain = vecs[8:].reshape(2, 2, piece)
    grad_seg = rows_own[12:20]
    up_own = mine[22 : 22 + per_row].T.reshape(2, 2, piece_up)
    grad_up_vec = jnp.where(part == 0, up_own[:, 0], up_own[:, 1])
    return (
        output,
        grad_input,
        grad_w_qkv,
        grad_w_out,
        grad_w_up,
        grad_w_down,
        grad_vec,
        grad_gain,
        grad_up_vec,
        grad_seg,
    )


def solution(mesh):
    return jax.shard_map(
        local,
        mesh=mesh,
        in_specs=(
            P("dp", "tensor", None),
            P("dp", "tensor", None),
            P("dp"),
            P(None, "dp", None, "tensor"),
            P(None, "tensor", "dp"),
            P(None, "dp", "tensor"),
            P(None, "tensor", "dp"),
            P(None, None, ("dp", "tensor")),
            P(None, None, ("dp", "tensor")),
            P(None, ("dp", "tensor")),
            P(None, ("dp", "tensor")),
        ),
        out_specs=(
            P("dp", "tensor", None),
            P("dp", "tensor", None),
            P(None, "dp", None, "tensor"),
            P(None, "tensor", "dp"),
            P(None, "dp", "tensor"),
            P(None, "tensor", "dp"),
            P(None, None, ("dp", "tensor")),
            P(None, None, ("dp", "tensor")),
            P(None, ("dp", "tensor")),
            P(None, ("dp", "tensor")),
        ),
        check_vma=False,
    )
```

time: 517 us -> 436 us (0.84)
  waiting for transfers between devices: 203 us -> 101 us
  matrix products: 71 us -> 43 us
  Pallas kernels: 37.8 us -> 64 us
  other arithmetic: 66.9 us -> 82.5 us
  local copies, waits for them, and re-layouts: 41.1 us -> 55.3 us
  starting transfers between devices: 85.8 us -> 77.3 us
    ppermute x64, waiting for transfers between devices: 202 us -> 99.8 us  [swap_dp(): return lax.ppermute(values, 'dp', [(i, i ^ 1 << bit) for i in range(count)])]
    pallas_call x0 -> x6, Pallas kernels: none -> 25.4 us  [the longest x5 21 us: cls_call(): pl.pallas_call(kernel, grid_spec=pltpu.PrefetchScalarGridSpec(num_scalar_...]
    dot_general x8 -> x4, matrix products: 19.3 us -> 8.49 us  [dot_nt(): lax.dot_general(a, b, (((1,), (1,)), ((), ())), preferred_element_type=F32)]
    ppermute x64, starting transfers between devices: 82.8 us -> 73.4 us  [swap_dp(): return lax.ppermute(values, 'dp', [(i, i ^ 1 << bit) for i in range(count)])]
    dot_general x12 -> x10, matrix products: 26.3 us -> 17.3 us  [dot_nn(): lax.dot_general(a, b, (((1,), (0,)), ((), ())), preferred_element_type=F32)]
    unnamed x267 -> x324, local copies, waits for them, and re-layouts: 12.2 us -> 21.1 us
    concatenate x28 -> x50, other arithmetic: 27.3 us -> 35.4 us  [the longest x40 34.3 us: join(): return jnp.concatenate([low, high], axis=bits - 1 - bit)]
    convert_element_type x25 -> x17, other arithmetic: 18 us -> 11.8 us  [the longest x10 8.4 us: half(): return sum(cut[1:], cut[0]).astype(BF)]
  transfers between devices with their start and end apart: 80 -> 82, of which waited for: 34 -> 34; matrix products, arithmetic and copies ran while one was open for 31% -> 28% of each run, Pallas kernels for 7% -> 8%
where the time goes in v2:
time: 436 us; the launch traced here: 428 us
  waiting for transfers between devices  101 us (23%)
  other arithmetic  82.5 us (19%)
  starting transfers between devices  77.3 us (18%)
  Pallas kernels  64 us (15%)
  local copies, waits for them, and re-layouts  55.3 us (13%)
  matrix products  43 us (10%)
  between operations  4.4 us (1%)
    ppermute x64, waiting for transfers between devices, swap_dp(): return lax.ppermute(values, 'dp', [(i, i ^ 1 << bit) for i in range(count)])  99.8 us
    ppermute x64, starting transfers between devices, swap_dp(): return lax.ppermute(values, 'dp', [(i, i ^ 1 << bit) for i in range(count)])  73.4 us
    concatenate x40, other arithmetic, join(): return jnp.concatenate([low, high], axis=bits - 1 - bit)  34.3 us
    unnamed x324, local copies, waits for them, and re-layouts  21.1 us
    pallas_call x5, Pallas kernels, cls_call(): pl.pallas_call(kernel, grid_spec=pltpu.PrefetchScalarGridSpec(num_scalar_...  21 us
    dot_general x10, matrix products, dot_nn(): lax.dot_general(a, b, (((1,), (0,)), ((), ())), preferred_element_type=F32)  17.3 us
    pallas_call x1, Pallas kernels, attn_bwd(): pl.pallas_call(attn_bwd_kernel, grid_spec=pltpu.PrefetchScalarGridSpec(nu...  15.9 us
    pallas_call x1, Pallas kernels, up_gelu(): pl.pallas_call(up_kernel, grid=(hidden // tile_h, total // tile_r), in_sp...  12.7 us
  transfers between devices with their start and end apart: 82, of which 34 were waited for; matrix products, arithmetic and copies ran while one was open for 28% of the time, Pallas kernels for 8%

profile of v2, /device:TPU:0, one launch (start us, length us, event | category | flops | bytes accessed | tf_op | source)
XLA Modules:
  0.0 427.8 jit_solution(12450967499814019900)
XLA Ops:
  6.0 3.7 collective-permute-start.4
  9.7 3.0 collective-permute-start.6
  17.2 3.0 collective-permute-done.2
  22.4 2.6 collective-permute-done.3
  37.0 3.5 collective-permute-done.11
  53.3 6.1 %collective-permute-done.16 = bf16[2,1,2,2,48,512]{5,4,3,2,1,0:T(8,128)(2,1)S(1)} collective-permute-done((bf16[2,1,2,2,48,512]{5,4,3,2,1,0:T(8,128)(2,1)S(1)}, bf16[2,1,2,2,48,512]{5,4,3,2,1,0:T(8,128)(2,1)S(1)}, u32[]{:S(2)}, u32[]{:S(2)}) %collective-permute-start.16) | collective-permute-done | bytes 393248 | tf_op jit(solution)/shard_map/ppermute | solution.py:45
  60.4 3.6 add_convert_fusion.qkv_ref
  68.4 10.0 %attn_fwd.1 = bf16[1024,384]{1,0:T(8,128)(2,1)} custom-call(s32[8]{0:T(128)} %fusion.73.count_ref, bf16[1024,1152]{1,0:T(8,128)(2,1)} %add_convert_fusion.qkv_ref), custom_call_target="tpu_custom_call" | custom-call | flops 1 | bytes 1 | tf_op jit(solution)/shard_map/attn_fwd/pallas_call | solution.py:229
  89.1 2.1 collective-permute-start.26
  97.5 10.6 %collective-permute-done.29 = bf16[1,1,1,1,48,1536]{5,4,3,2,1,0:T(8,128)(2,1)S(1)} collective-permute-done((bf16[1,1,1,1,48,1536]{5,4,3,2,1,0:T(8,128)(2,1)S(1)}, bf16[1,1,1,1,48,1536]{5,4,3,2,1,0:T(8,128)(2,1)S(1)}, u32[]{:S(2)}, u32[]{:S(2)}) %collective-permute-start.29) | collective-permute-done | bytes 147488 | tf_op jit(solution)/shard_map/ppermute | solution.py:45
  108.1 2.7 collective-permute-done.30
  125.3 17.9 %collective-permute-done.31 = bf16[2,2,2,1,48,1536]{5,4,3,2,1,0:T(8,128)(2,1)} collective-permute-done((bf16[2,2,2,1,48,1536]{5,4,3,2,1,0:T(8,128)(2,1)}, bf16[2,2,2,1,48,1536]{5,4,3,2,1,0:T(8,128)(2,1)}, u32[]{:S(2)}, u32[]{:S(2)}) %collective-permute-start.31) | collective-permute-done | bytes 1179680 | tf_op jit(solution)/shard_map/ppermute | solution.py:45
  143.2 2.9 collective-permute-done.33
  146.0 3.2 pad_maximum_fusion
  149.3 12.7 %up_gelu.1 = (bf16[1024,1536]{1,0:T(8,128)(2,1)}, bf16[1024,1536]{1,0:T(8,128)(2,1)}) custom-call(bf16[1024,768]{1,0:T(8,128)(2,1)} %pad_maximum_fusion.8.rows_ref, bf16[768,1536]{1,0:T(8,128)(2,1)} %bitcast.268, f32[1,1536]{1,0:T(1,128)} %get-tuple-element.563.bias_ref), custom_call_target="tpu_custom_call" | custom-call | flops 1 | bytes 1 | tf_op jit(solution)/shard_map/up_gelu/pallas_call | solution.py:277
  167.9 2.0 pad_maximum_fusion.1
  171.7 2.6 convolution_convert_fusion.6
  175.1 2.9 pad_maximum_fusion.2
  179.2 2.4 collective-permute-done.37
  193.7 3.6 multiply_convert_fusion
  197.3 2.6 convolution_convert_fusion.5
  201.3 2.9 convolution_convert_fusion.1
  210.3 3.3 convolution_convert_fusion
  218.9 3.4 pad_maximum_fusion.3
  222.9 4.2 cls_attn.1
  229.1 3.0 pad_maximum_fusion.4
  236.1 4.2 cls_up.1
  244.6 4.1 cls_up_back.2
  255.1 4.3 %cls_attn_back.1 = (bf16[8,1152]{1,0:T(8,128)(2,1)}, f32[16,768]{1,0:T(8,128)}) custom-call(s32[1]{0:T(128)S(6)} %select_n.252.count_ref, bf16[16,768]{1,0:T(8,128)(2,1)} %get-tuple-element.462.grad_ref, bf16[768,1536]{1,0:T(8,128)(2,1)} %bitcast.253, bf16[768,1536]{1,0:T(8,128)(2,1)} %bitcast.254, bf16[768,1536]{1,0:T(8,128)(2,1)} %bitcast.255, ...), custom_call_target="tpu_custom_call" | custom-call | flops 1 | bytes 1 | tf_op jit(solution)/shard_map/cls_attn_back/pallas_call | solution.py:358
  268.9 2.8 add_convert_fusion.1
  274.4 4.1 cls_up_back.3
  300.7 2.1 collective-permute-done.53
  304.7 2.0 add_convert_fusion.5
  309.0 15.9 %attn_bwd.1 = (bf16[1024,1152]{1,0:T(8,128)(2,1)}, f32[1,1152]{1,0:T(1,128)}) custom-call(s32[8]{0:T(128)} %fusion.73.count_ref, bf16[1024,1152]{1,0:T(8,128)(2,1)} %add_convert_fusion.qkv_ref, bf16[1024,384]{1,0:T(8,128)(2,1)} %convolution_convert_fusion.7.grad_ref, f32[8,1,384]{2,1,0:T(1,128)} %reshape.620.first_ref), custom_call_target="tpu_custom_call" | custom-call | flops 1 | bytes 1 | tf_op jit(solution)/shard_map/attn_bwd/pallas_call | solution.py:246
  331.5 2.0 collective-permute-start.59
  339.0 3.0 collective-permute-done.59
  347.8 3.9 convolution_convert_fusion.2
  357.1 9.0 %collective-permute-done.62 = bf16[2,2,1,1,8,7680]{5,4,3,2,1,0:T(8,128)(2,1)S(1)} collective-permute-done((bf16[2,2,1,1,8,7680]{5,4,3,2,1,0:T(8,128)(2,1)S(1)}, bf16[2,2,1,1,8,7680]{5,4,3,2,1,0:T(8,128)(2,1)S(1)}, u32[]{:S(2)}, u32[]{:S(2)}) %collective-permute-start.62) | collective-permute-done | bytes 491552 | tf_op jit(solution)/shard_map/ppermute | solution.py:45
  366.4 2.2 convolution_convert_fusion.4
  368.7 3.7 collective-permute-done.65
  381.1 3.1 collective-permute-start.72
  384.2 5.3 %collective-permute-done.80 = bf16[2,1,2,1,8,5760]{5,4,3,2,1,0:T(8,128)(2,1)S(1)} collective-permute-done((bf16[2,1,2,1,8,5760]{5,4,3,2,1,0:T(8,128)(2,1)S(1)}, bf16[2,1,2,1,8,5760]{5,4,3,2,1,0:T(8,128)(2,1)S(1)}, u32[]{:S(2)}, u32[]{:S(2)}) %collective-permute-start.80) | collective-permute-done | bytes 368672 | tf_op jit(solution)/shard_map/ppermute | solution.py:45
  390.1 2.1 collective-permute-start.78
  399.9 2.9 collective-permute-start.76
  402.9 2.0 add_bitcast_fusion
  405.6 2.7 collective-permute-done.74
  408.4 5.7 %collective-permute-done.79 = bf16[2,2,1,2,8,7680]{5,4,3,2,1,0:T(8,128)(2,1)S(1)} collective-permute-done((bf16[2,2,1,2,8,7680]{5,4,3,2,1,0:T(8,128)(2,1)S(1)}, bf16[2,2,1,2,8,7680]{5,4,3,2,1,0:T(8,128)(2,1)S(1)}, u32[]{:S(2)}, u32[]{:S(2)}) %collective-permute-start.79) | collective-permute-done | bytes 983072 | tf_op jit(solution)/shard_map/ppermute | solution.py:45
  416.8 4.5 %owner_sums.1 = (f32[2,48,1152]{2,1,0:T(8,128)}, f32[2,48,384]{2,1,0:T(8,128)}, f32[2,48,1536]{2,1,0:T(8,128)}, f32[2,48,1536]{2,1,0:T(8,128)}, f32[48,128]{1,0:T(8,128)}) custom-call(bf16[128,7680]{1,0:T(8,128)(2,1)} %bitcast.280, bf16[128,5760]{1,0:T(8,128)(2,1)} %bitcast.281, bf16[768,48]{1,0:T(8,128)(2,1)} %constant.124.clone.pick_ref, ...), custom_call_target="tpu_custom_call" | custom-call | flops 1 | bytes 1 | tf_op jit(solution)/shard_map/owner_sums/pallas_call | solution.py:434
  (766 shorter events, 211.2 us)
Async XLA Ops:
  3.7 11.4 %collective-permute-start.1 = (f32[32,768]{1,0:T(8,128)S(1)}, f32[32,768]{1,0:T(8,128)S(1)}, u32[]{:S(2)}, u32[]{:S(2)}) collective-permute-start(f32[32,768]{1,0:T(8,128)S(1)} %pad_maximum_fusion.56), channel_id=1, source_target_pairs={{0,1},{1,0},{2,3},{3,2},{4,5},{5,4},{6,7},{7,6},{8,9},{9,8},{10,11... | collective-permute-start | bytes 294920 | tf_op jit(solution)/shard_map/ppermute | solution.py:49
  6.0 19.0 %collective-permute-start.4 = (bf16[1,1,1,1,48,512]{5,4,3,2,1,0:T(8,128)(2,1)S(1)}, bf16[1,1,1,1,48,512]{5,4,3,2,1,0:T(8,128)(2,1)S(1)}, u32[]{:S(2)}, u32[]{:S(2)}) collective-permute-start(bf16[1,1,1,1,48,512]{5,4,3,2,1,0:T(8,128)(2,1)S(1)} %maximum_bitcast_fusion), channel_id=1, source_target_pairs={{0,16},{2,18},{4,20},{6,22},{8,24},{10,26},{12,28},{14,30},{16,0},... | collective-permute-start | bytes 147464 | tf_op jit(solution)/shard_map/ppermute | solution.py:45
  9.6 15.4 %collective-permute-start.5 = (bf16[1,1,1,1,48,512]{5,4,3,2,1,0:T(8,128)(2,1)S(1)}, bf16[1,1,1,1,48,512]{5,4,3,2,1,0:T(8,128)(2,1)S(1)}, u32[]{:S(2)}, u32[]{:S(2)}) collective-permute-start(bf16[1,1,1,1,48,512]{5,4,3,2,1,0:T(8,128)(2,1)S(1)} %maximum_bitcast_fusion.1), channel_id=1, source_target_pairs={{0,16},{2,18},{4,20},{6,22},{8,24},{10,26},{12,28},{14,30},{16,0},... | collective-permute-start | bytes 147464 | tf_op jit(solution)/shard_map/ppermute | solution.py:45
  9.7 15.3 %collective-permute-start.6 = (bf16[1,1,1,1,48,512]{5,4,3,2,1,0:T(8,128)(2,1)S(1)}, bf16[1,1,1,1,48,512]{5,4,3,2,1,0:T(8,128)(2,1)S(1)}, u32[]{:S(2)}, u32[]{:S(2)}) collective-permute-start(bf16[1,1,1,1,48,512]{5,4,3,2,1,0:T(8,128)(2,1)S(1)} %maximum_bitcast_fusion.2), channel_id=1, source_target_pairs={{0,16},{2,18},{4,20},{6,22},{8,24},{10,26},{12,28},{14,30},{16,0},... | collective-permute-start | bytes 147464 | tf_op jit(solution)/shard_map/ppermute | solution.py:45
  13.7 35.0 %collective-permute-start = (bf16[512,768]{1,0:T(8,128)(2,1)S(1)}, bf16[512,768]{1,0:T(8,128)(2,1)S(1)}, u32[]{:S(2)}, u32[]{:S(2)}) collective-permute-start(bf16[512,768]{1,0:T(8,128)(2,1)S(1)} %fusion.8), channel_id=1, source_target_pairs={{0,1},{1,0},{2,3},{3,2},{4,5},{5,4},{6,7},{7,6},{8,9},{9,8},{10,11... | collective-permute-start | bytes 2359304 | tf_op jit(solution)/shard_map/ppermute | solution.py:49
  47.2 12.2 %collective-permute-start.16 = (bf16[2,1,2,2,48,512]{5,4,3,2,1,0:T(8,128)(2,1)S(1)}, bf16[2,1,2,2,48,512]{5,4,3,2,1,0:T(8,128)(2,1)S(1)}, u32[]{:S(2)}, u32[]{:S(2)}) collective-permute-start(bf16[2,1,2,2,48,512]{5,4,3,2,1,0:T(8,128)(2,1)S(1)} %pad_maximum_fusion.39), channel_id=1, source_target_pairs={{0,8},{2,10},{4,12},{6,14},{8,0},{10,2},{12,4},{14,6},{16,24},{18,... | collective-permute-start | bytes 1179656 | tf_op jit(solution)/shard_map/ppermute | solution.py:45
  47.5 16.6 %collective-permute-start.18 = (bf16[1,1,1,1,48,1536]{5,4,3,2,1,0:T(8,128)(2,1)S(1)}, bf16[1,1,1,1,48,1536]{5,4,3,2,1,0:T(8,128)(2,1)S(1)}, u32[]{:S(2)}, u32[]{:S(2)}) collective-permute-start(bf16[1,1,1,1,48,1536]{5,4,3,2,1,0:T(8,128)(2,1)S(1)} %get-tuple-element.223), channel_id=1, source_target_pairs={{0,16},{2,18},{4,20},{6,22},{8,24},{10,26},{12,28},{14,30},{16,0},... | collective-permute-start | bytes 442376 | tf_op jit(solution)/shard_map/ppermute | solution.py:45
  48.8 15.3 %collective-permute-start.19 = (bf16[1,1,1,1,48,1536]{5,4,3,2,1,0:T(8,128)(2,1)S(1)}, bf16[1,1,1,1,48,1536]{5,4,3,2,1,0:T(8,128)(2,1)S(1)}, u32[]{:S(2)}, u32[]{:S(2)}) collective-permute-start(bf16[1,1,1,1,48,1536]{5,4,3,2,1,0:T(8,128)(2,1)S(1)} %get-tuple-element.224), channel_id=1, source_target_pairs={{0,16},{2,18},{4,20},{6,22},{8,24},{10,26},{12,28},{14,30},{16,0},... | collective-permute-start | bytes 442376 | tf_op jit(solution)/shard_map/ppermute | solution.py:45
  51.7 12.4 %collective-permute-start.20 = (bf16[1,1,1,1,48,1536]{5,4,3,2,1,0:T(8,128)(2,1)S(1)}, bf16[1,1,1,1,48,1536]{5,4,3,2,1,0:T(8,128)(2,1)S(1)}, u32[]{:S(2)}, u32[]{:S(2)}) collective-permute-start(bf16[1,1,1,1,48,1536]{5,4,3,2,1,0:T(8,128)(2,1)S(1)} %bitcast.305), channel_id=1, source_target_pairs={{0,16},{2,18},{4,20},{6,22},{8,24},{10,26},{12,28},{14,30},{16,0},... | collective-permute-start | bytes 442376 | tf_op jit(solution)/shard_map/ppermute | solution.py:45
  65.6 12.9 %collective-permute-start.21 = (bf16[2,1,1,1,48,1536]{5,4,3,2,1,0:T(8,128)(2,1)S(1)}, bf16[2,1,1,1,48,1536]{5,4,3,2,1,0:T(8,128)(2,1)}, u32[]{:S(2)}, u32[]{:S(2)}) collective-permute-start(bf16[2,1,1,1,48,1536]{5,4,3,2,1,0:T(8,128)(2,1)S(1)} %pad_maximum_fusion.43), channel_id=1, source_target_pairs={{0,4},{2,6},{4,0},{6,2},{8,12},{10,14},{12,8},{14,10},{16,20},{18,... | collective-permute-start | bytes 884744 | tf_op jit(solution)/shard_map/ppermute | solution.py:45
  66.8 11.7 %collective-permute-start.22 = (bf16[2,1,1,1,48,1536]{5,4,3,2,1,0:T(8,128)(2,1)}, bf16[2,1,1,1,48,1536]{5,4,3,2,1,0:T(8,128)(2,1)}, u32[]{:S(2)}, u32[]{:S(2)}) collective-permute-start(bf16[2,1,1,1,48,1536]{5,4,3,2,1,0:T(8,128)(2,1)} %pad_maximum_fusion.44), channel_id=1, source_target_pairs={{0,2},{2,0},{4,6},{6,4},{8,10},{10,8},{12,14},{14,12},{16,18},{18,... | collective-permute-start | bytes 884744 | tf_op jit(solution)/shard_map/ppermute | solution.py:45
  67.7 10.8 %collective-permute-start.23 = (bf16[2,1,1,1,48,1536]{5,4,3,2,1,0:T(8,128)(2,1)}, bf16[2,1,1,1,48,1536]{5,4,3,2,1,0:T(8,128)(2,1)}, u32[]{:S(2)}, u32[]{:S(2)}) collective-permute-start(bf16[2,1,1,1,48,1536]{5,4,3,2,1,0:T(8,128)(2,1)} %pad_maximum_fusion.45), channel_id=1, source_target_pairs={{0,8},{2,10},{4,12},{6,14},{8,0},{10,2},{12,4},{14,6},{16,24},{18,... | collective-permute-start | bytes 884744 | tf_op jit(solution)/shard_map/ppermute | solution.py:45
  89.1 22.4 %collective-permute-start.26 = (bf16[2,1,2,1,48,1536]{5,4,3,2,1,0:T(8,128)(2,1)S(1)}, bf16[2,1,2,1,48,1536]{5,4,3,2,1,0:T(8,128)(2,1)S(1)}, u32[]{:S(2)}, u32[]{:S(2)}) collective-permute-start(bf16[2,1,2,1,48,1536]{5,4,3,2,1,0:T(8,128)(2,1)S(1)} %pad_maximum_fusion.28), channel_id=1, source_target_pairs={{0,8},{2,10},{4,12},{6,14},{8,0},{10,2},{12,4},{14,6},{16,24},{18,... | collective-permute-start | bytes 1769480 | tf_op jit(solution)/shard_map/ppermute | solution.py:45
  91.2 20.3 %collective-permute-start.27 = (bf16[2,1,1,2,48,1536]{5,4,3,2,1,0:T(8,128)(2,1)S(1)}, bf16[2,1,1,2,48,1536]{5,4,3,2,1,0:T(8,128)(2,1)S(1)}, u32[]{:S(2)}, u32[]{:S(2)}) collective-permute-start(bf16[2,1,1,2,48,1536]{5,4,3,2,1,0:T(8,128)(2,1)S(1)} %pad_maximum_fusion.29), channel_id=1, source_target_pairs={{0,4},{2,6},{4,0},{6,2},{8,12},{10,14},{12,8},{14,10},{16,20},{18,... | collective-permute-start | bytes 1769480 | tf_op jit(solution)/shard_map/ppermute | solution.py:45
  91.9 19.6 %collective-permute-start.28 = (bf16[2,2,1,1,48,1536]{5,4,3,2,1,0:T(8,128)(2,1)S(1)}, bf16[2,2,1,1,48,1536]{5,4,3,2,1,0:T(8,128)(2,1)S(1)}, u32[]{:S(2)}, u32[]{:S(2)}) collective-permute-start(bf16[2,2,1,1,48,1536]{5,4,3,2,1,0:T(8,128)(2,1)S(1)} %pad_maximum_fusion.30), channel_id=1, source_target_pairs={{0,2},{2,0},{4,6},{6,4},{8,10},{10,8},{12,14},{14,12},{16,18},{18,... | collective-permute-start | bytes 1769480 | tf_op jit(solution)/shard_map/ppermute | solution.py:45
  93.2 14.9 %collective-permute-start.29 = (bf16[1,1,1,1,48,1536]{5,4,3,2,1,0:T(8,128)(2,1)S(1)}, bf16[1,1,1,1,48,1536]{5,4,3,2,1,0:T(8,128)(2,1)S(1)}, u32[]{:S(2)}, u32[]{:S(2)}) collective-permute-start(bf16[1,1,1,1,48,1536]{5,4,3,2,1,0:T(8,128)(2,1)S(1)} %copy-done.30), channel_id=1, source_target_pairs={{0,16},{2,18},{4,20},{6,22},{8,24},{10,26},{12,28},{14,30},{16,0},... | collective-permute-start | bytes 442376 | tf_op jit(solution)/shard_map/ppermute | solution.py:45
  94.3 16.5 %collective-permute-start.30 = (bf16[1,1,1,1,48,1536]{5,4,3,2,1,0:T(8,128)(2,1)S(1)}, bf16[1,1,1,1,48,1536]{5,4,3,2,1,0:T(8,128)(2,1)S(1)}, u32[]{:S(2)}, u32[]{:S(2)}) collective-permute-start(bf16[1,1,1,1,48,1536]{5,4,3,2,1,0:T(8,128)(2,1)S(1)} %copy-done.31), channel_id=1, source_target_pairs={{0,16},{2,18},{4,20},{6,22},{8,24},{10,26},{12,28},{14,30},{16,0},... | collective-permute-start | bytes 442376 | tf_op jit(solution)/shard_map/ppermute | solution.py:45
  114.0 29.2 %collective-permute-start.31 = (bf16[2,2,2,1,48,1536]{5,4,3,2,1,0:T(8,128)(2,1)}, bf16[2,2,2,1,48,1536]{5,4,3,2,1,0:T(8,128)(2,1)}, u32[]{:S(2)}, u32[]{:S(2)}) collective-permute-start(bf16[2,2,2,1,48,1536]{5,4,3,2,1,0:T(8,128)(2,1)} %pad_maximum_fusion.12), channel_id=1, source_target_pairs={{0,2},{2,0},{4,6},{6,4},{8,10},{10,8},{12,14},{14,12},{16,18},{18,... | collective-permute-start | bytes 3538952 | tf_op jit(solution)/shard_map/ppermute | solution.py:45
  115.2 28.0 %collective-permute-start.32 = (bf16[2,1,2,2,48,1536]{5,4,3,2,1,0:T(8,128)(2,1)}, bf16[2,1,2,2,48,1536]{5,4,3,2,1,0:T(8,128)(2,1)}, u32[]{:S(2)}, u32[]{:S(2)}) collective-permute-start(bf16[2,1,2,2,48,1536]{5,4,3,2,1,0:T(8,128)(2,1)} %pad_maximum_fusion.13), channel_id=1, source_target_pairs={{0,8},{2,10},{4,12},{6,14},{8,0},{10,2},{12,4},{14,6},{16,24},{18,... | collective-permute-start | bytes 3538952 | tf_op jit(solution)/shard_map/ppermute | solution.py:45
  117.1 28.9 %collective-permute-start.33 = (bf16[2,2,1,2,48,1536]{5,4,3,2,1,0:T(8,128)(2,1)S(1)}, bf16[2,2,1,2,48,1536]{5,4,3,2,1,0:T(8,128)(2,1)}, u32[]{:S(2)}, u32[]{:S(2)}) collective-permute-start(bf16[2,2,1,2,48,1536]{5,4,3,2,1,0:T(8,128)(2,1)S(1)} %pad_maximum_fusion.14), channel_id=1, source_target_pairs={{0,4},{2,6},{4,0},{6,2},{8,12},{10,14},{12,8},{14,10},{16,20},{18,... | collective-permute-start | bytes 3538952 | tf_op jit(solution)/shard_map/ppermute | solution.py:45
  124.2 39.7 %collective-permute-start.34 = (bf16[2,1,1,1,48,1536]{5,4,3,2,1,0:T(8,128)(2,1)S(1)}, bf16[2,1,1,1,48,1536]{5,4,3,2,1,0:T(8,128)(2,1)}, u32[]{:S(2)}, u32[]{:S(2)}) collective-permute-start(bf16[2,1,1,1,48,1536]{5,4,3,2,1,0:T(8,128)(2,1)S(1)} %pad_maximum_fusion.46), channel_id=1, source_target_pairs={{0,4},{2,6},{4,0},{6,2},{8,12},{10,14},{12,8},{14,10},{16,20},{18,... | collective-permute-start | bytes 884744 | tf_op jit(solution)/shard_map/ppermute | solution.py:45
  124.8 39.1 %collective-permute-start.35 = (bf16[2,1,1,1,48,1536]{5,4,3,2,1,0:T(8,128)(2,1)S(1)}, bf16[2,1,1,1,48,1536]{5,4,3,2,1,0:T(8,128)(2,1)}, u32[]{:S(2)}, u32[]{:S(2)}) collective-permute-start(bf16[2,1,1,1,48,1536]{5,4,3,2,1,0:T(8,128)(2,1)S(1)} %pad_maximum_fusion.47), channel_id=1, source_target_pairs={{0,2},{2,0},{4,6},{6,4},{8,10},{10,8},{12,14},{14,12},{16,18},{18,... | collective-permute-start | bytes 884744 | tf_op jit(solution)/shard_map/ppermute | solution.py:45
  170.0 11.6 %collective-permute-start.37 = (bf16[2,1,2,1,48,1536]{5,4,3,2,1,0:T(8,128)(2,1)S(1)}, bf16[2,1,2,1,48,1536]{5,4,3,2,1,0:T(8,128)(2,1)S(1)}, u32[]{:S(2)}, u32[]{:S(2)}) collective-permute-start(bf16[2,1,2,1,48,1536]{5,4,3,2,1,0:T(8,128)(2,1)S(1)} %pad_maximum_fusion.32), channel_id=1, source_target_pairs={{0,8},{2,10},{4,12},{6,14},{8,0},{10,2},{12,4},{14,6},{16,24},{18,... | collective-permute-start | bytes 1769480 | tf_op jit(solution)/shard_map/ppermute | solution.py:45
  170.1 12.0 %collective-permute-start.38 = (bf16[2,1,1,2,48,1536]{5,4,3,2,1,0:T(8,128)(2,1)S(1)}, bf16[2,1,1,2,48,1536]{5,4,3,2,1,0:T(8,128)(2,1)S(1)}, u32[]{:S(2)}, u32[]{:S(2)}) collective-permute-start(bf16[2,1,1,2,48,1536]{5,4,3,2,1,0:T(8,128)(2,1)S(1)} %pad_maximum_fusion.33), channel_id=1, source_target_pairs={{0,4},{2,6},{4,0},{6,2},{8,12},{10,14},{12,8},{14,10},{16,20},{18,... | collective-permute-start | bytes 1769480 | tf_op jit(solution)/shard_map/ppermute | solution.py:45
  187.7 31.2 %collective-permute-start.43 = (bf16[2,2,2,1,48,1536]{5,4,3,2,1,0:T(8,128)(2,1)}, bf16[2,2,2,1,48,1536]{5,4,3,2,1,0:T(8,128)(2,1)S(1)}, u32[]{:S(2)}, u32[]{:S(2)}) collective-permute-start(bf16[2,2,2,1,48,1536]{5,4,3,2,1,0:T(8,128)(2,1)} %pad_maximum_fusion.15), channel_id=1, source_target_pairs={{0,2},{2,0},{4,6},{6,4},{8,10},{10,8},{12,14},{14,12},{16,18},{18,... | collective-permute-start | bytes 3538952 | tf_op jit(solution)/shard_map/ppermute | solution.py:45
  188.5 30.4 %collective-permute-start.44 = (bf16[2,1,2,2,48,1536]{5,4,3,2,1,0:T(8,128)(2,1)}, bf16[2,1,2,2,48,1536]{5,4,3,2,1,0:T(8,128)(2,1)S(1)}, u32[]{:S(2)}, u32[]{:S(2)}) collective-permute-start(bf16[2,1,2,2,48,1536]{5,4,3,2,1,0:T(8,128)(2,1)} %pad_maximum_fusion.16), channel_id=1, source_target_pairs={{0,8},{2,10},{4,12},{6,14},{8,0},{10,2},{12,4},{14,6},{16,24},{18,... | collective-permute-start | bytes 3538952 | tf_op jit(solution)/shard_map/ppermute | solution.py:45
  232.8 35.1 %collective-permute-start.50 = (bf16[2,2,2,1,48,1536]{5,4,3,2,1,0:T(8,128)(2,1)}, bf16[2,2,2,1,48,1536]{5,4,3,2,1,0:T(8,128)(2,1)S(1)}, u32[]{:S(2)}, u32[]{:S(2)}) collective-permute-start(bf16[2,2,2,1,48,1536]{5,4,3,2,1,0:T(8,128)(2,1)} %slice.1167), channel_id=1, source_target_pairs={{0,2},{2,0},{4,6},{6,4},{8,10},{10,8},{12,14},{14,12},{16,18},{18,... | collective-permute-start | bytes 3538952 | tf_op jit(solution)/shard_map/ppermute | solution.py:45
  234.3 34.7 %collective-permute-start.51 = (bf16[2,1,2,2,48,1536]{5,4,3,2,1,0:T(8,128)(2,1)}, bf16[2,1,2,2,48,1536]{5,4,3,2,1,0:T(8,128)(2,1)}, u32[]{:S(2)}, u32[]{:S(2)}) collective-permute-start(bf16[2,1,2,2,48,1536]{5,4,3,2,1,0:T(8,128)(2,1)} %slice.1168), channel_id=1, source_target_pairs={{0,8},{2,10},{4,12},{6,14},{8,0},{10,2},{12,4},{14,6},{16,24},{18,... | collective-permute-start | bytes 3538952 | tf_op jit(solution)/shard_map/ppermute | solution.py:45
  280.8 12.1 %collective-permute-start.52 = (f32[16,768]{1,0:T(8,128)}, f32[16,768]{1,0:T(8,128)}, u32[]{:S(2)}, u32[]{:S(2)}) collective-permute-start(f32[16,768]{1,0:T(8,128)} %get-tuple-element.299), channel_id=1, source_target_pairs={{0,1},{1,0},{2,3},{3,2},{4,5},{5,4},{6,7},{7,6},{8,9},{9,8},{10,11... | collective-permute-start | bytes 147464 | tf_op jit(solution)/shard_map/ppermute | solution.py:49
  281.3 19.5 %collective-permute-start.55 = (bf16[1,1,1,1,8,7680]{5,4,3,2,1,0:T(8,128)(2,1)}, bf16[1,1,1,1,8,7680]{5,4,3,2,1,0:T(8,128)(2,1)}, u32[]{:S(2)}, u32[]{:S(2)}) collective-permute-start(bf16[1,1,1,1,8,7680]{5,4,3,2,1,0:T(8,128)(2,1)} %bitcast.65), channel_id=1, source_target_pairs={{0,16},{2,18},{4,20},{6,22},{8,24},{10,26},{12,28},{14,30},{16,0},... | collective-permute-start | bytes 368648 | tf_op jit(solution)/shard_map/ppermute | solution.py:45
  285.6 17.2 %collective-permute-start.53 = (bf16[2,1,2,1,48,1536]{5,4,3,2,1,0:T(8,128)(2,1)}, bf16[2,1,2,1,48,1536]{5,4,3,2,1,0:T(8,128)(2,1)}, u32[]{:S(2)}, u32[]{:S(2)}) collective-permute-start(bf16[2,1,2,1,48,1536]{5,4,3,2,1,0:T(8,128)(2,1)} %get-tuple-element.300), channel_id=1, source_target_pairs={{0,8},{2,10},{4,12},{6,14},{8,0},{10,2},{12,4},{14,6},{16,24},{18,... | collective-permute-start | bytes 1769480 | tf_op jit(solution)/shard_map/ppermute | solution.py:45
  286.4 16.4 %collective-permute-start.54 = (bf16[2,1,1,2,48,1536]{5,4,3,2,1,0:T(8,128)(2,1)}, bf16[2,1,1,2,48,1536]{5,4,3,2,1,0:T(8,128)(2,1)}, u32[]{:S(2)}, u32[]{:S(2)}) collective-permute-start(bf16[2,1,1,2,48,1536]{5,4,3,2,1,0:T(8,128)(2,1)} %get-tuple-element.301), channel_id=1, source_target_pairs={{0,4},{2,6},{4,0},{6,2},{8,12},{10,14},{12,8},{14,10},{16,20},{18,... | collective-permute-start | bytes 1769480 | tf_op jit(solution)/shard_map/ppermute | solution.py:45
  331.5 10.5 %collective-permute-start.59 = (bf16[2,1,1,1,8,7680]{5,4,3,2,1,0:T(8,128)(2,1)}, bf16[2,1,1,1,8,7680]{5,4,3,2,1,0:T(8,128)(2,1)S(1)}, u32[]{:S(2)}, u32[]{:S(2)}) collective-permute-start(bf16[2,1,1,1,8,7680]{5,4,3,2,1,0:T(8,128)(2,1)} %pad_maximum_fusion.48), channel_id=1, source_target_pairs={{0,8},{2,10},{4,12},{6,14},{8,0},{10,2},{12,4},{14,6},{16,24},{18,... | collective-permute-start | bytes 737288 | tf_op jit(solution)/shard_map/ppermute | solution.py:45
  333.5 9.1 %collective-permute-start.57 = (bf16[2,1,1,1,48,1536]{5,4,3,2,1,0:T(8,128)(2,1)}, bf16[2,1,1,1,48,1536]{5,4,3,2,1,0:T(8,128)(2,1)S(1)}, u32[]{:S(2)}, u32[]{:S(2)}) collective-permute-start(bf16[2,1,1,1,48,1536]{5,4,3,2,1,0:T(8,128)(2,1)} %get-tuple-element.313), channel_id=1, source_target_pairs={{0,4},{2,6},{4,0},{6,2},{8,12},{10,14},{12,8},{14,10},{16,20},{18,... | collective-permute-start | bytes 884744 | tf_op jit(solution)/shard_map/ppermute | solution.py:45
  335.1 8.8 %collective-permute-start.58 = (bf16[2,1,1,1,48,1536]{5,4,3,2,1,0:T(8,128)(2,1)}, bf16[2,1,1,1,48,1536]{5,4,3,2,1,0:T(8,128)(2,1)S(1)}, u32[]{:S(2)}, u32[]{:S(2)}) collective-permute-start(bf16[2,1,1,1,48,1536]{5,4,3,2,1,0:T(8,128)(2,1)} %get-tuple-element.314), channel_id=1, source_target_pairs={{0,2},{2,0},{4,6},{6,4},{8,10},{10,8},{12,14},{14,12},{16,18},{18,... | collective-permute-start | bytes 884744 | tf_op jit(solution)/shard_map/ppermute | solution.py:45
  347.3 9.8 %collective-permute-start.63 = (bf16[2,1,1,1,8,5760]{5,4,3,2,1,0:T(8,128)(2,1)S(1)}, bf16[2,1,1,1,8,5760]{5,4,3,2,1,0:T(8,128)(2,1)S(1)}, u32[]{:S(2)}, u32[]{:S(2)}) collective-permute-start(bf16[2,1,1,1,8,5760]{5,4,3,2,1,0:T(8,128)(2,1)S(1)} %pad_maximum_fusion.55), channel_id=1, source_target_pairs={{0,4},{2,6},{4,0},{6,2},{8,12},{10,14},{12,8},{14,10},{16,20},{18,... | collective-permute-start | bytes 552968 | tf_op jit(solution)/shard_map/ppermute | solution.py:45
  352.0 14.2 %collective-permute-start.62 = (bf16[2,2,1,1,8,7680]{5,4,3,2,1,0:T(8,128)(2,1)S(1)}, bf16[2,2,1,1,8,7680]{5,4,3,2,1,0:T(8,128)(2,1)S(1)}, u32[]{:S(2)}, u32[]{:S(2)}) collective-permute-start(bf16[2,2,1,1,8,7680]{5,4,3,2,1,0:T(8,128)(2,1)S(1)} %pad_maximum_fusion.34), channel_id=1, source_target_pairs={{0,2},{2,0},{4,6},{6,4},{8,10},{10,8},{12,14},{14,12},{16,18},{18,... | collective-permute-start | bytes 1474568 | tf_op jit(solution)/shard_map/ppermute | solution.py:45
  353.7 18.7 %collective-permute-start.65 = (bf16[2,2,2,1,48,512]{5,4,3,2,1,0:T(8,128)(2,1)S(1)}, bf16[2,2,2,1,48,512]{5,4,3,2,1,0:T(8,128)(2,1)S(1)}, u32[]{:S(2)}, u32[]{:S(2)}) collective-permute-start(bf16[2,2,2,1,48,512]{5,4,3,2,1,0:T(8,128)(2,1)S(1)} %pad_maximum_fusion.40), channel_id=1, source_target_pairs={{0,2},{2,0},{4,6},{6,4},{8,10},{10,8},{12,14},{14,12},{16,18},{18,... | collective-permute-start | bytes 1179656 | tf_op jit(solution)/shard_map/ppermute | solution.py:45
  355.2 17.2 %collective-permute-start.66 = (bf16[2,1,2,2,48,512]{5,4,3,2,1,0:T(8,128)(2,1)S(1)}, bf16[2,1,2,2,48,512]{5,4,3,2,1,0:T(8,128)(2,1)S(1)}, u32[]{:S(2)}, u32[]{:S(2)}) collective-permute-start(bf16[2,1,2,2,48,512]{5,4,3,2,1,0:T(8,128)(2,1)S(1)} %pad_maximum_fusion.41), channel_id=1, source_target_pairs={{0,8},{2,10},{4,12},{6,14},{8,0},{10,2},{12,4},{14,6},{16,24},{18,... | collective-permute-start | bytes 1179656 | tf_op jit(solution)/shard_map/ppermute | solution.py:45
  355.5 16.9 %collective-permute-start.64 = (bf16[2,2,1,2,48,640]{5,4,3,2,1,0:T(8,128)(2,1)S(1)}, bf16[2,2,1,2,48,640]{5,4,3,2,1,0:T(8,128)(2,1)S(1)}, u32[]{:S(2)}, u32[]{:S(2)}) collective-permute-start(bf16[2,2,1,2,48,640]{5,4,3,2,1,0:T(8,128)(2,1)S(1)} %pad_maximum_fusion.35), channel_id=1, source_target_pairs={{0,4},{2,6},{4,0},{6,2},{8,12},{10,14},{12,8},{14,10},{16,20},{18,... | collective-permute-start | bytes 1474568 | tf_op jit(solution)/shard_map/ppermute | solution.py:45
  377.0 22.8 %collective-permute-start.77 = (bf16[1,1,1,1,48,1536]{5,4,3,2,1,0:T(8,128)(2,1)S(1)}, bf16[1,1,1,1,48,1536]{5,4,3,2,1,0:T(8,128)(2,1)S(1)}, u32[]{:S(2)}, u32[]{:S(2)}) collective-permute-start(bf16[1,1,1,1,48,1536]{5,4,3,2,1,0:T(8,128)(2,1)S(1)} %get-tuple-element.360), channel_id=1, source_target_pairs={{0,16},{2,18},{4,20},{6,22},{8,24},{10,26},{12,28},{14,30},{16,0},... | collective-permute-start | bytes 442376 | tf_op jit(solution)/shard_map/ppermute | solution.py:45
  378.7 10.8 %collective-permute-start.80 = (bf16[2,1,2,1,8,5760]{5,4,3,2,1,0:T(8,128)(2,1)S(1)}, bf16[2,1,2,1,8,5760]{5,4,3,2,1,0:T(8,128)(2,1)S(1)}, u32[]{:S(2)}, u32[]{:S(2)}) collective-permute-start(bf16[2,1,2,1,8,5760]{5,4,3,2,1,0:T(8,128)(2,1)S(1)} %pad_maximum_fusion.42), channel_id=1, source_target_pairs={{0,8},{2,10},{4,12},{6,14},{8,0},{10,2},{12,4},{14,6},{16,24},{18,... | collective-permute-start | bytes 1105928 | tf_op jit(solution)/shard_map/ppermute | solution.py:45
  380.6 17.9 %collective-permute-start.67 = (bf16[512,768]{1,0:T(8,128)(2,1)S(1)}, bf16[512,768]{1,0:T(8,128)(2,1)S(1)}, u32[]{:S(2)}, u32[]{:S(2)}) collective-permute-start(bf16[512,768]{1,0:T(8,128)(2,1)S(1)} %slice.1052), channel_id=1, source_target_pairs={{0,1},{1,0},{2,3},{3,2},{4,5},{5,4},{6,7},{7,6},{8,9},{9,8},{10,11... | collective-permute-start | bytes 2359304 | tf_op jit(solution)/shard_map/ppermute | solution.py:49
  381.1 8.9 %collective-permute-start.72 = (bf16[2,1,1,1,48,512]{5,4,3,2,1,0:T(8,128)(2,1)S(1)}, bf16[2,1,1,1,48,512]{5,4,3,2,1,0:T(8,128)(2,1)S(1)}, u32[]{:S(2)}, u32[]{:S(2)}) collective-permute-start(bf16[2,1,1,1,48,512]{5,4,3,2,1,0:T(8,128)(2,1)S(1)} %get-tuple-element.352), channel_id=1, source_target_pairs={{0,4},{2,6},{4,0},{6,2},{8,12},{10,14},{12,8},{14,10},{16,20},{18,... | collective-permute-start | bytes 294920 | tf_op jit(solution)/shard_map/ppermute | solution.py:45
  384.2 8.0 %collective-permute-start.73 = (bf16[2,1,1,1,48,512]{5,4,3,2,1,0:T(8,128)(2,1)S(1)}, bf16[2,1,1,1,48,512]{5,4,3,2,1,0:T(8,128)(2,1)S(1)}, u32[]{:S(2)}, u32[]{:S(2)}) collective-permute-start(bf16[2,1,1,1,48,512]{5,4,3,2,1,0:T(8,128)(2,1)S(1)} %get-tuple-element.353), channel_id=1, source_target_pairs={{0,2},{2,0},{4,6},{6,4},{8,10},{10,8},{12,14},{14,12},{16,18},{18,... | collective-permute-start | bytes 294920 | tf_op jit(solution)/shard_map/ppermute | solution.py:45
  390.1 12.7 %collective-permute-start.78 = (bf16[1,1,1,1,48,1536]{5,4,3,2,1,0:T(8,128)(2,1)S(1)}, bf16[1,1,1,1,48,1536]{5,4,3,2,1,0:T(8,128)(2,1)S(1)}, u32[]{:S(2)}, u32[]{:S(2)}) collective-permute-start(bf16[1,1,1,1,48,1536]{5,4,3,2,1,0:T(8,128)(2,1)S(1)} %get-tuple-element.361), channel_id=1, source_target_pairs={{0,16},{2,18},{4,20},{6,22},{8,24},{10,26},{12,28},{14,30},{16,0},... | collective-permute-start | bytes 442376 | tf_op jit(solution)/shard_map/ppermute | solution.py:45
  392.2 21.9 %collective-permute-start.79 = (bf16[2,2,1,2,8,7680]{5,4,3,2,1,0:T(8,128)(2,1)S(1)}, bf16[2,2,1,2,8,7680]{5,4,3,2,1,0:T(8,128)(2,1)S(1)}, u32[]{:S(2)}, u32[]{:S(2)}) collective-permute-start(bf16[2,2,1,2,8,7680]{5,4,3,2,1,0:T(8,128)(2,1)S(1)} %pad_maximum_fusion.21), channel_id=1, source_target_pairs={{0,4},{2,6},{4,0},{6,2},{8,12},{10,14},{12,8},{14,10},{16,20},{18,... | collective-permute-start | bytes 2949128 | tf_op jit(solution)/shard_map/ppermute | solution.py:45
  395.0 19.0 %collective-permute-start.81 = (bf16[2,2,2,1,8,5760]{5,4,3,2,1,0:T(8,128)(2,1)S(1)}, bf16[2,2,2,1,8,5760]{5,4,3,2,1,0:T(8,128)(2,1)S(1)}, u32[]{:S(2)}, u32[]{:S(2)}) collective-permute-start(bf16[2,2,2,1,8,5760]{5,4,3,2,1,0:T(8,128)(2,1)S(1)} %pad_maximum_fusion.25), channel_id=1, source_target_pairs={{0,2},{2,0},{4,6},{6,4},{8,10},{10,8},{12,14},{14,12},{16,18},{18,... | collective-permute-start | bytes 2211848 | tf_op jit(solution)/shard_map/ppermute | solution.py:45
  (173 other events, 1655.9 us)

commit v3 on v2

--- a/solution.py
+++ b/solution.py
@@ -286,7 +286,7 @@
         out_shape=[jax.ShapeDtypeStruct((total, hidden), BF)] * 2,
         cost_estimate=BRIEF,
         name="up_gelu",
-    )(rows, w_up, bias[None, :])
+    )(rows, w_up, bias)
 
 
 def cls_attn_kernel(count_ref, rows_ref, w0, w1, w2, bias_ref, qkv_ref, att_ref, sum_ref):
@@ -369,6 +369,43 @@
         cost_estimate=BRIEF,
         name=name,
     )(*scalars, before, *[w for w, _ in weights], after)
+
+
+def own_bias_kernel(part_ref, rows_ref, qkv_ref, hidden_ref):
+    width = rows_ref.shape[1] // 2
+    first = part_ref[0] == 0
+    fold = (rows_ref.shape[0] - 24) // 2
+
+    def own(row, at, size):
+        return jnp.where(first, rows_ref[row : row + 1, at : at + size], rows_ref[row : row + 1, width + at : width + at + size])
+
+    for block in range(2):
+        for p in range(PIECES):
+            parts = (own(6 * block, p * PAIR, PAIR), jnp.zeros((1, PAIR), F32), own(6 * block + 1, p * PAIR, PAIR))
+            for k, value in enumerate(parts):
+                at = (3 * p + k) * PAIR
+                qkv_ref[block : block + 1, at : at + PAIR] = value
+        base = 24 + fold * block
+        for k in range(fold // 2):
+            low, high = base + k, base + fold // 2 + k
+            value = jnp.where(first, rows_ref[low : low + 1, :], rows_ref[high : high + 1, :])
+            hidden_ref[block : block + 1, 2 * width * k : 2 * width * (k + 1)] = value
+
+
+def own_biases(part, rows, width, hidden):
+    outs = [jax.ShapeDtypeStruct((2, 3 * width), F32), jax.ShapeDtypeStruct((2, hidden), F32)]
+    return pl.pallas_call(
+        own_bias_kernel,
+        grid_spec=pltpu.PrefetchScalarGridSpec(
+            num_scalar_prefetch=1,
+            grid=(1,),
+            in_specs=[whole(rows)],
+            out_specs=[whole(o) for o in outs],
+        ),
+        out_shape=outs,
+        cost_estimate=BRIEF,
+        name="own_biases",
+    )(part.reshape(1).astype(jnp.int32), rows)
 
 
 def owner_kernel(
@@ -530,49 +567,54 @@
     )
     one_q.send()
     small = small + swap_tensor(small)
-    for bit in range(bits - 2):
+    for bit in range(bits - 3):
         small = small + swap_dp(small, bit, count)
     small = settle(small, one_q)
     small, w_qkv, w_out, w_up, w_down = tie(small, w_qkv, w_out, w_up, w_down)
     two_attn = jnp.concatenate([attn_piece(w_qkv[1], w_out[1], p) for p in span], axis=1)
     one_m = Gather([w_up[0], w_down[0].T, two_attn], orders[1:] + orders[:1], bits, count)
     two = Gather([w_up[1], w_down[1].T], orders[1:], bits, count)
+    got = swap_dp(small, bits - 3, count)
+    one_q.send()
+    one_q.state[0], *one_m.state = tie(one_q.state[0], *one_m.state)
+    one_m.send()
+    got = settle(got, one_q)
+    small = small + got
     got = swap_dp(small, bits - 2, count)
     one_q.send()
-    small = small + settle(got, one_q)
+    got = settle(got, one_q, one_m)
+    small = small + got
+    last = swap_dp(small, bits - 1, count)
     small = launch(small, one_q)
-    last = swap_dp(small, bits - 1, count)
-    small = advance(small, one_q)
+    small = launch(small, one_m)
     while one_q.left() > 1:
         small = advance(small, one_q)
-    small, *one_m.state = tie(small, *one_m.state)
-    small = launch(small, one_m)
+    x_own = dot_nn(layer_input[0], perm).astype(BF)
+    x_full = jnp.concatenate([x_own, swap_half(x_own)], axis=0)
+    x_full = settle(x_full, one_q, one_m)
+    x_full, *two.state = tie(x_full, *two.state)
+    x_full = launch(x_full, one_m)
+    x_full = launch(x_full, two)
+    x_full, last = tie(x_full, last)
     small = small + last
 
     plain = small[: small_rows.shape[0]]
-    up_all = small[small_rows.shape[0] :].reshape(2, 2, hidden)
     rel = dot_exact(plain, perm_f)
 
-    def own_width(row):
-        return jnp.where(part == 0, row[:width], row[width:])
+    bias_qkv, bias_hidden = own_biases(part, small, width, hidden)
 
     def block_vectors(block, order):
         base = 6 * block
-        zero = jnp.zeros((PAIR,), F32)
-        bias_q, bias_v = own_width(plain[base]), own_width(plain[base + 1])
-        bias_qkv = jnp.concatenate(
-            [v for p in span for v in (bias_q[p * PAIR : (p + 1) * PAIR], zero, bias_v[p * PAIR : (p + 1) * PAIR])]
-        )
         gain_at = 12 + 2 * block
         return dict(
-            qkv=bias_qkv,
+            qkv=bias_qkv[block : block + 1],
             attn=order[base + 2],
             mlp=order[base + 3],
             shift_one=order[base + 4],
             shift_two=order[base + 5],
             gain_one=order[gain_at],
             gain_two=order[gain_at + 1],
-            hidden=jnp.where(part == 0, up_all[block, 0], up_all[block, 1]),
+            hidden=bias_hidden[block : block + 1],
         )
 
     v1, v2 = block_vectors(0, rel), block_vectors(1, rel)
@@ -602,19 +644,14 @@
     def firsts(rows):
         return rows.reshape(-1, SEG, rows.shape[-1])[:, 0]
 
-    x_own = dot_nn(layer_input[0], perm).astype(BF)
-    x_full = jnp.concatenate([x_own, swap_half(x_own)], axis=0)
-    x_full = settle(x_full, one_q)
     attn_r = one_q.results()
     w_qkv_r = jnp.concatenate([w[:, :three] for w in attn_r], axis=1)
     w_out_r = jnp.concatenate([w[:, three:] for w in attn_r], axis=1)
     qkv = (dot_nn(x_full, w_qkv_r) + v1["qkv"]).astype(BF)
-    qkv = advance(qkv, one_m)
     attended = attn_fwd(seg_counts, qkv)
-    while one_m.left() > 2:
+    while one_m.left() > 1:
         attended = advance(attended, one_m)
-    attended, *two.state = tie(attended, *two.state)
-    attended = launch(attended, two)
+    attended = advance(attended, two)
     partial_attn = dot_nt(attended, w_out_r).astype(BF)
     first_sum = (
         partial_attn[:half].astype(F32)
@@ -626,9 +663,6 @@
     first = unit_one * v1["gain_one"] + v1["shift_one"]
     first_low = first.astype(BF)
     first_full = jnp.concatenate([first_low, swap_half(first_low)], axis=0)
-    first_full = settle(first_full, one_m, two)
-    first_full = launch(first_full, one_m)
-    first_full = launch(first_full, two)
     first_full = settle(first_full, one_m)
     w_up_r, w_down_r, two_attn_r = one_m.results()
     act, slope = up_gelu(first_full, w_up_r, v1["hidden"])
@@ -689,7 +723,7 @@
     cls_low = cls_in.astype(BF)
     rows_c = cls_in.shape[0]
     qkv_c, att_c, part_c = cls_call(
-        cls_attn_kernel, "cls_attn", cls_count, cls_low, attn_w, tile, v2["qkv"][None, :],
+        cls_attn_kernel, "cls_attn", cls_count, cls_low, attn_w, tile, v2["qkv"],
         [((rows_c, 3 * width), BF), ((segments, width), BF), ((rows_c, dim), F32)],
     )
     sum_c1 = part_c + swap_half(part_c) + v2["attn"] + cls_in
@@ -697,7 +731,7 @@
     first_c = unit_c1 * v2["gain_one"] + v2["shift_one"]
     first_c_low = first_c.astype(BF)
     act_c, slope_c, part_c2 = cls_call(
-        cls_up_kernel, "cls_up", None, first_c_low, up_w + down_w, tile, v2["hidden"][None, :],
+        cls_up_kernel, "cls_up", None, first_c_low, up_w + down_w, tile, v2["hidden"],
         [((segments, hidden), BF), ((rows_c, hidden), F32), ((rows_c, dim), F32)],
     )
     sum_c2 = part_c2 + swap_half(part_c2) + v2["mlp"] + first_c
@@ -733,6 +767,7 @@
         cls_up_back_kernel, "cls_up_back", None, g_mlp_1, [(w, p) for w in (w_up_r, w_down_r) for p in span], tile,
         padded(slope_1.astype(F32)), back_outs
     )
+    part_1 = advance(part_1, wide_two)
     g_first_1 = part_1 + swap_half(part_1) + g_second_1
     g_sum_1 = norm_bwd(g_first_1, unit_one_1, inv_one_1, v1["gain_one"])
     g_attn_1 = g_sum_1.astype(BF)
@@ -795,10 +830,9 @@
     small_rows = small_rows + swap_tensor(small_rows)
     filler = jnp.zeros((PAIR - small_rows.shape[0] - 2, dim), F32)
     small_cols = jnp.concatenate([small_rows, filler], axis=0).T.astype(BF)
-    g_att_1, small_cols = tie(g_att_1, small_cols)
+    g_att_1, small_cols, output = tie(g_att_1, small_cols, output)
 
     gqkv, gqkv_sums = attn_bwd(seg_counts, qkv, g_attended, g_att_1)
-    gqkv = advance(gqkv, early, wide_two, wide_one)
     gw_qkv = dot_tn(x_full, gqkv).astype(BF)
     sums_o = gqkv_sums.reshape(PIECES, 3, PAIR) * scale_one
     bias_own = jnp.stack([spread(sums_o[:, k].reshape(-1), dim) for k in (0, 2)])
@@ -809,19 +843,21 @@
     )
     gqkv = launch(gqkv, late)
     wides = (wide_two, wide_one)
-    gqkv = advance(gqkv, *wides)
+    gqkv = advance(gqkv, early, wide_one)
     part_x = dot_nt(gqkv, w_qkv_r).astype(BF)
 
-    part_x = advance(part_x, late)
+    part_x = advance(part_x, late, wide_two)
+    part_x = advance(part_x, wide_one)
     g_first_all = with_cls(g_first_sum, own_half(g_sum_1))
     g_in = part_x[:half].astype(F32) + swap_half(part_x[half:]).astype(F32) + g_first_all
     g_in_high = lax.reduce_precision(g_in, 8, 7)
     grad_input = (dot_nn(g_in_high.astype(BF), perm) + dot_nn((g_in - g_in_high).astype(BF), perm))[None]
     anchor = jnp.zeros((), F32)
-    while any(m.left() > 1 for m in (early, *wides)):
-        anchor = advance(anchor, *[m for m in (early, *wides) if m.left() > 1])
-    while late.left() > 1:
-        anchor = advance(anchor, late)
+    movers = (late, early, *wides)
+    while any(m.left() > 1 for m in movers):
+        for m in movers:
+            if m.left() > 1:
+                anchor = advance(anchor, m)
     anchor = settle(anchor, late, early, *wides)
 
     shape = (width, hidden, dim, chunk, segments, scale_one, scale_two)

time: 436 us -> 428 us (0.982)
  waiting for transfers between devices: 101 us -> 78.4 us
  other arithmetic: 82.5 us -> 88.5 us
    ppermute x64, waiting for transfers between devices: 99.8 us -> 78 us  [swap_dp(): return lax.ppermute(values, 'dp', [(i, i ^ 1 << bit) for i in range(count)])]
    concatenate x40 -> x39, other arithmetic: 34.3 us -> 37.7 us  [join(): return jnp.concatenate([low, high], axis=bits - 1 - bit)]
    unnamed x324 -> x345, local copies, waits for them, and re-layouts: 21.1 us -> 19.2 us
  transfers between devices with their start and end apart: 82 -> 82, of which waited for: 34 -> 27; matrix products, arithmetic and copies ran while one was open for 28% -> 34% of each run, Pallas kernels for 8% -> 8%
where the time goes in v3:
time: 428 us; the launch traced here: 420 us
  other arithmetic  88.5 us (21%)
  waiting for transfers between devices  78.4 us (18%)
  starting transfers between devices  77.6 us (18%)
  Pallas kernels  65.2 us (15%)
  local copies, waits for them, and re-layouts  59.5 us (14%)
  matrix products  45.9 us (11%)
  between operations  4.5 us (1%)
    ppermute x64, waiting for transfers between devices, swap_dp(): return lax.ppermute(values, 'dp', [(i, i ^ 1 << bit) for i in range(count)])  78 us
    ppermute x64, starting transfers between devices, swap_dp(): return lax.ppermute(values, 'dp', [(i, i ^ 1 << bit) for i in range(count)])  73.6 us
    concatenate x39, other arithmetic, join(): return jnp.concatenate([low, high], axis=bits - 1 - bit)  37.7 us
    pallas_call x5, Pallas kernels, cls_call(): pl.pallas_call(kernel, grid_spec=pltpu.PrefetchScalarGridSpec(num_scalar_...  21.1 us
    unnamed x345, local copies, waits for them, and re-layouts  19.2 us
    dot_general x10, matrix products, dot_nn(): lax.dot_general(a, b, (((1,), (0,)), ((), ())), preferred_element_type=F32)  17.4 us
    pallas_call x1, Pallas kernels, attn_bwd(): pl.pallas_call(attn_bwd_kernel, grid_spec=pltpu.PrefetchScalarGridSpec(nu...  15.7 us
    pallas_call x1, Pallas kernels, up_gelu(): pl.pallas_call(up_kernel, grid=(hidden // tile_h, total // tile_r), in_sp...  12.6 us
  transfers between devices with their start and end apart: 82, of which 27 were waited for; matrix products, arithmetic and copies ran while one was open for 34% of the time, Pallas kernels for 8%

profile of v3, /device:TPU:0, one launch (start us, length us, event | category | flops | bytes accessed | tf_op | source)
XLA Modules:
  0.0 419.7 jit_solution(7050944025999608347)
XLA Ops:
  6.0 3.7 collective-permute-start.3
  9.8 3.0 collective-permute-start.5
  14.4 3.1 collective-permute-done.2
  24.4 2.3 collective-permute-start.14
  27.4 2.3 collective-permute-start.16
  31.5 8.3 %collective-permute-done.14 = bf16[1,1,1,1,48,1536]{5,4,3,2,1,0:T(8,128)(2,1)S(1)} collective-permute-done((bf16[1,1,1,1,48,1536]{5,4,3,2,1,0:T(8,128)(2,1)S(1)}, bf16[1,1,1,1,48,1536]{5,4,3,2,1,0:T(8,128)(2,1)S(1)}, u32[]{:S(2)}, u32[]{:S(2)}) %collective-permute-start.14) | collective-permute-done | bytes 147488 | tf_op jit(solution)/shard_map/ppermute | solution.py:45
  40.0 3.0 collective-permute-done.15
  45.4 4.1 collective-permute-done.12
  54.0 5.8 %collective-permute-done.20 = bf16[2,1,1,1,48,1536]{5,4,3,2,1,0:T(8,128)(2,1)S(1)} collective-permute-done((bf16[2,1,1,1,48,1536]{5,4,3,2,1,0:T(8,128)(2,1)S(1)}, bf16[2,1,1,1,48,1536]{5,4,3,2,1,0:T(8,128)(2,1)S(1)}, u32[]{:S(2)}, u32[]{:S(2)}) %collective-permute-start.20) | collective-permute-done | bytes 294944 | tf_op jit(solution)/shard_map/ppermute | solution.py:45
  61.1 2.4 pad_maximum_fusion.7
  63.5 5.3 %collective-permute-done.21 = bf16[2,1,1,1,48,1536]{5,4,3,2,1,0:T(8,128)(2,1)S(1)} collective-permute-done((bf16[2,1,1,1,48,1536]{5,4,3,2,1,0:T(8,128)(2,1)S(1)}, bf16[2,1,1,1,48,1536]{5,4,3,2,1,0:T(8,128)(2,1)S(1)}, u32[]{:S(2)}, u32[]{:S(2)}) %collective-permute-start.21) | collective-permute-done | bytes 294944 | tf_op jit(solution)/shard_map/ppermute | solution.py:45
  78.6 2.5 collective-permute-start.24
  86.3 3.6 add_convert_fusion.qkv_ref
  91.7 10.0 %attn_fwd.1 = bf16[1024,384]{1,0:T(8,128)(2,1)} custom-call(s32[8]{0:T(128)} %fusion.71.count_ref, bf16[1024,1152]{1,0:T(8,128)(2,1)} %add_convert_fusion.qkv_ref), custom_call_target="tpu_custom_call" | custom-call | flops 1 | bytes 1 | tf_op jit(solution)/shard_map/attn_fwd/pallas_call | solution.py:229
  101.7 2.2 pad_maximum_fusion.12
  103.9 2.2 pad_maximum_fusion.13
  129.7 15.8 %collective-permute-done.31 = bf16[2,2,2,1,48,1536]{5,4,3,2,1,0:T(8,128)(2,1)S(1)} collective-permute-done((bf16[2,2,2,1,48,1536]{5,4,3,2,1,0:T(8,128)(2,1)}, bf16[2,2,2,1,48,1536]{5,4,3,2,1,0:T(8,128)(2,1)S(1)}, u32[]{:S(2)}, u32[]{:S(2)}) %collective-permute-start.31) | collective-permute-done | bytes 1179680 | tf_op jit(solution)/shard_map/ppermute | solution.py:45
  146.9 3.0 pad_maximum_fusion
  149.8 12.6 %up_gelu.1 = (bf16[1024,1536]{1,0:T(8,128)(2,1)}, bf16[1024,1536]{1,0:T(8,128)(2,1)}) custom-call(bf16[1024,768]{1,0:T(8,128)(2,1)} %pad_maximum_fusion.8.rows_ref, bf16[768,1536]{1,0:T(8,128)(2,1)} %bitcast.217, f32[1,1536]{1,0:T(1,128)} %get-tuple-element.572.bias_ref), custom_call_target="tpu_custom_call" | custom-call | flops 1 | bytes 1 | tf_op jit(solution)/shard_map/up_gelu/pallas_call | solution.py:277
  170.4 2.0 collective-permute-start.37
  173.0 2.6 convolution_convert_fusion.6
  176.4 3.0 pad_maximum_fusion.2
  180.6 3.8 collective-permute-done.37
  195.9 3.8 multiply_convert_fusion
  199.7 2.6 convolution_convert_fusion.5
  203.8 3.0 convolution_convert_fusion.1
  212.8 3.1 convolution_convert_fusion
  221.1 3.4 pad_maximum_fusion.3
  225.1 4.2 %cls_attn.1 = (bf16[16,1152]{1,0:T(8,128)(2,1)}, bf16[8,384]{1,0:T(8,128)(2,1)}, f32[16,768]{1,0:T(8,128)}) custom-call(s32[1]{0:T(128)S(6)} %select_n.201.count_ref, bf16[16,768]{1,0:T(8,128)(2,1)} %convert_element_type.459.rows_ref, bf16[768,1536]{1,0:T(8,128)(2,1)} %bitcast.199, bf16[768,1536]{1,0:T(8,128)(2,1)} %bitcast.200, ...), custom_call_target="tpu_custom_call" | custom-call | flops 1 | bytes 1 | tf_op jit(solution)/shard_map/cls_attn/pallas_call | solution.py:358
  231.3 3.0 pad_maximum_fusion.4
  238.8 4.3 %cls_up.1 = (bf16[8,1536]{1,0:T(8,128)(2,1)}, f32[16,1536]{1,0:T(8,128)}, f32[16,768]{1,0:T(8,128)}) custom-call(bf16[16,768]{1,0:T(8,128)(2,1)} %fusion.38.rows_ref, bf16[768,1536]{1,0:T(8,128)(2,1)} %bitcast.205, bf16[768,1536]{1,0:T(8,128)(2,1)} %bitcast.206, bf16[768,1536]{1,0:T(8,128)(2,1)} %bitcast.207, bf16[768,1536]{1,0:T(8,128)(2,1)} %bitcast.211, ...), custom_call_target="tpu_custom_call" | custom-call | flops 1 | bytes 1 | tf_op jit(solution)/shard_map/cls_up/pallas_call | solution.py:358
  249.2 4.1 cls_up_back.2
  259.8 4.3 %cls_attn_back.1 = (bf16[8,1152]{1,0:T(8,128)(2,1)}, f32[16,768]{1,0:T(8,128)}) custom-call(s32[1]{0:T(128)S(6)} %select_n.201.count_ref, bf16[16,768]{1,0:T(8,128)(2,1)} %get-tuple-element.468.grad_ref, bf16[768,1536]{1,0:T(8,128)(2,1)} %bitcast.202, bf16[768,1536]{1,0:T(8,128)(2,1)} %bitcast.203, bf16[768,1536]{1,0:T(8,128)(2,1)} %bitcast.204, ...), custom_call_target="tpu_custom_call" | custom-call | flops 1 | bytes 1 | tf_op jit(solution)/shard_map/cls_attn_back/pallas_call | solution.py:358
  272.0 2.9 add_convert_fusion.1
  274.9 2.4 add_convert_fusion.2
  278.9 4.1 cls_up_back.3
  288.4 2.2 fusion.32
  291.3 3.6 collective-permute-done.52
  305.9 3.9 collective-permute-done.56
  315.0 15.7 %attn_bwd.1 = (bf16[1024,1152]{1,0:T(8,128)(2,1)}, f32[1,1152]{1,0:T(1,128)}) custom-call(s32[8]{0:T(128)} %fusion.71.count_ref, bf16[1024,1152]{1,0:T(8,128)(2,1)} %add_convert_fusion.qkv_ref, bf16[1024,384]{1,0:T(8,128)(2,1)} %convolution_convert_fusion.7.grad_ref, f32[8,1,384]{2,1,0:T(1,128)} %reshape.553.first_ref), custom_call_target="tpu_custom_call" | custom-call | flops 1 | bytes 1 | tf_op jit(solution)/shard_map/attn_bwd/pallas_call | solution.py:246
  332.7 4.4 %convolution_convert_fusion.2 = bf16[768,1152]{1,0:T(8,128)(2,1)S(1)} fusion(bf16[1024,768]{1,0:T(8,128)(2,1)} %pad_maximum_fusion.7, bf16[1024,1152]{1,0:T(8,128)(2,1)} %get-tuple-element.335), kind=kOutput, calls=%fused_computation.4 | convolution fusion | flops 1812824064 | bytes 5701632 | tf_op jit(solution)/shard_map/dot_general | solution.py:35
  357.8 3.9 convolution_convert_fusion.4
  361.7 5.0 %collective-permute-done.63 = bf16[2,2,2,1,48,512]{5,4,3,2,1,0:T(8,128)(2,1)S(1)} collective-permute-done((bf16[2,2,2,1,48,512]{5,4,3,2,1,0:T(8,128)(2,1)}, bf16[2,2,2,1,48,512]{5,4,3,2,1,0:T(8,128)(2,1)S(1)}, u32[]{:S(2)}, u32[]{:S(2)}) %collective-permute-start.63) | collective-permute-done | bytes 393248 | tf_op jit(solution)/shard_map/ppermute | solution.py:45
  373.1 3.0 collective-permute-start.80
  379.3 3.6 collective-permute-done.80
  385.2 2.3 collective-permute-start.79
  400.6 5.2 %collective-permute-done.79 = bf16[2,2,1,2,8,7680]{5,4,3,2,1,0:T(8,128)(2,1)S(1)} collective-permute-done((bf16[2,2,1,2,8,7680]{5,4,3,2,1,0:T(8,128)(2,1)S(1)}, bf16[2,2,1,2,8,7680]{5,4,3,2,1,0:T(8,128)(2,1)S(1)}, u32[]{:S(2)}, u32[]{:S(2)}) %collective-permute-start.79) | collective-permute-done | bytes 983072 | tf_op jit(solution)/shard_map/ppermute | solution.py:45
  408.5 4.4 %owner_sums.1 = (f32[2,48,1152]{2,1,0:T(8,128)}, f32[2,48,384]{2,1,0:T(8,128)}, f32[2,48,1536]{2,1,0:T(8,128)}, f32[2,48,1536]{2,1,0:T(8,128)}, f32[48,128]{1,0:T(8,128)}) custom-call(bf16[128,7680]{1,0:T(8,128)(2,1)} %bitcast.229, bf16[128,5760]{1,0:T(8,128)(2,1)} %bitcast.230, bf16[768,48]{1,0:T(8,128)(2,1)} %constant.123.clone.pick_ref, ...), custom_call_target="tpu_custom_call" | custom-call | flops 1 | bytes 1 | tf_op jit(solution)/shard_map/owner_sums/pallas_call | solution.py:471
  (780 shorter events, 206.4 us)
Async XLA Ops:
  3.7 9.1 %collective-permute-start.1 = (f32[32,768]{1,0:T(8,128)S(1)}, f32[32,768]{1,0:T(8,128)S(1)}, u32[]{:S(2)}, u32[]{:S(2)}) collective-permute-start(f32[32,768]{1,0:T(8,128)S(1)} %pad_maximum_fusion.55), channel_id=1, source_target_pairs={{0,1},{1,0},{2,3},{3,2},{4,5},{5,4},{6,7},{7,6},{8,9},{9,8},{10,11... | collective-permute-start | bytes 294920 | tf_op jit(solution)/shard_map/ppermute | solution.py:49
  6.0 11.5 %collective-permute-start.3 = (bf16[1,1,1,1,48,512]{5,4,3,2,1,0:T(8,128)(2,1)S(1)}, bf16[1,1,1,1,48,512]{5,4,3,2,1,0:T(8,128)(2,1)S(1)}, u32[]{:S(2)}, u32[]{:S(2)}) collective-permute-start(bf16[1,1,1,1,48,512]{5,4,3,2,1,0:T(8,128)(2,1)S(1)} %maximum_bitcast_fusion), channel_id=1, source_target_pairs={{0,16},{2,18},{4,20},{6,22},{8,24},{10,26},{12,28},{14,30},{16,0},... | collective-permute-start | bytes 147464 | tf_op jit(solution)/shard_map/ppermute | solution.py:45
  24.4 15.3 %collective-permute-start.14 = (bf16[1,1,1,1,48,1536]{5,4,3,2,1,0:T(8,128)(2,1)S(1)}, bf16[1,1,1,1,48,1536]{5,4,3,2,1,0:T(8,128)(2,1)S(1)}, u32[]{:S(2)}, u32[]{:S(2)}) collective-permute-start(bf16[1,1,1,1,48,1536]{5,4,3,2,1,0:T(8,128)(2,1)S(1)} %get-tuple-element.210), channel_id=1, source_target_pairs={{0,16},{2,18},{4,20},{6,22},{8,24},{10,26},{12,28},{14,30},{16,0},... | collective-permute-start | bytes 442376 | tf_op jit(solution)/shard_map/ppermute | solution.py:45
  26.7 16.3 %collective-permute-start.15 = (bf16[1,1,1,1,48,1536]{5,4,3,2,1,0:T(8,128)(2,1)S(1)}, bf16[1,1,1,1,48,1536]{5,4,3,2,1,0:T(8,128)(2,1)S(1)}, u32[]{:S(2)}, u32[]{:S(2)}) collective-permute-start(bf16[1,1,1,1,48,1536]{5,4,3,2,1,0:T(8,128)(2,1)S(1)} %get-tuple-element.211), channel_id=1, source_target_pairs={{0,16},{2,18},{4,20},{6,22},{8,24},{10,26},{12,28},{14,30},{16,0},... | collective-permute-start | bytes 442376 | tf_op jit(solution)/shard_map/ppermute | solution.py:45
  27.4 18.0 %collective-permute-start.16 = (bf16[1,1,1,1,48,1536]{5,4,3,2,1,0:T(8,128)(2,1)S(1)}, bf16[1,1,1,1,48,1536]{5,4,3,2,1,0:T(8,128)(2,1)S(1)}, u32[]{:S(2)}, u32[]{:S(2)}) collective-permute-start(bf16[1,1,1,1,48,1536]{5,4,3,2,1,0:T(8,128)(2,1)S(1)} %bitcast.254), channel_id=1, source_target_pairs={{0,16},{2,18},{4,20},{6,22},{8,24},{10,26},{12,28},{14,30},{16,0},... | collective-permute-start | bytes 442376 | tf_op jit(solution)/shard_map/ppermute | solution.py:45
  29.7 15.7 %collective-permute-start.10 = (f32[32,768]{1,0:T(8,128)S(1)}, f32[32,768]{1,0:T(8,128)S(1)}, u32[]{:S(2)}, u32[]{:S(2)}) collective-permute-start(f32[32,768]{1,0:T(8,128)S(1)} %add.503), channel_id=1, source_target_pairs={{0,8},{2,10},{4,12},{6,14},{8,0},{10,2},{12,4},{14,6},{16,24},{18,... | collective-permute-start | bytes 294920 | tf_op jit(solution)/shard_map/ppermute | solution.py:45
  29.9 15.6 %collective-permute-start.13 = (bf16[2,1,1,2,48,512]{5,4,3,2,1,0:T(8,128)(2,1)S(1)}, bf16[2,1,1,2,48,512]{5,4,3,2,1,0:T(8,128)(2,1)S(1)}, u32[]{:S(2)}, u32[]{:S(2)}) collective-permute-start(bf16[2,1,1,2,48,512]{5,4,3,2,1,0:T(8,128)(2,1)S(1)} %pad_maximum_fusion.52), channel_id=1, source_target_pairs={{0,4},{2,6},{4,0},{6,2},{8,12},{10,14},{12,8},{14,10},{16,20},{18,... | collective-permute-start | bytes 589832 | tf_op jit(solution)/shard_map/ppermute | solution.py:45
  39.7 9.8 %collective-permute-start.12 = (bf16[2,1,2,1,48,512]{5,4,3,2,1,0:T(8,128)(2,1)S(1)}, bf16[2,1,2,1,48,512]{5,4,3,2,1,0:T(8,128)(2,1)S(1)}, u32[]{:S(2)}, u32[]{:S(2)}) collective-permute-start(bf16[2,1,2,1,48,512]{5,4,3,2,1,0:T(8,128)(2,1)S(1)} %pad_maximum_fusion.51), channel_id=1, source_target_pairs={{0,8},{2,10},{4,12},{6,14},{8,0},{10,2},{12,4},{14,6},{16,24},{18,... | collective-permute-start | bytes 589832 | tf_op jit(solution)/shard_map/ppermute | solution.py:45
  49.8 9.9 %collective-permute-start.20 = (bf16[2,1,1,1,48,1536]{5,4,3,2,1,0:T(8,128)(2,1)S(1)}, bf16[2,1,1,1,48,1536]{5,4,3,2,1,0:T(8,128)(2,1)S(1)}, u32[]{:S(2)}, u32[]{:S(2)}) collective-permute-start(bf16[2,1,1,1,48,1536]{5,4,3,2,1,0:T(8,128)(2,1)S(1)} %pad_maximum_fusion.43), channel_id=1, source_target_pairs={{0,4},{2,6},{4,0},{6,2},{8,12},{10,14},{12,8},{14,10},{16,20},{18,... | collective-permute-start | bytes 884744 | tf_op jit(solution)/shard_map/ppermute | solution.py:45
  51.3 18.0 %collective-permute-start.17 = (bf16[2,2,1,2,48,512]{5,4,3,2,1,0:T(8,128)(2,1)S(1)}, bf16[2,2,1,2,48,512]{5,4,3,2,1,0:T(8,128)(2,1)}, u32[]{:S(2)}, u32[]{:S(2)}) collective-permute-start(bf16[2,2,1,2,48,512]{5,4,3,2,1,0:T(8,128)(2,1)S(1)} %pad_maximum_fusion.37), channel_id=1, source_target_pairs={{0,4},{2,6},{4,0},{6,2},{8,12},{10,14},{12,8},{14,10},{16,20},{18,... | collective-permute-start | bytes 1179656 | tf_op jit(solution)/shard_map/ppermute | solution.py:45
  51.9 17.4 %collective-permute-start.18 = (bf16[2,2,2,1,48,512]{5,4,3,2,1,0:T(8,128)(2,1)S(1)}, bf16[2,2,2,1,48,512]{5,4,3,2,1,0:T(8,128)(2,1)}, u32[]{:S(2)}, u32[]{:S(2)}) collective-permute-start(bf16[2,2,2,1,48,512]{5,4,3,2,1,0:T(8,128)(2,1)S(1)} %pad_maximum_fusion.38), channel_id=1, source_target_pairs={{0,2},{2,0},{4,6},{6,4},{8,10},{10,8},{12,14},{14,12},{16,18},{18,... | collective-permute-start | bytes 1179656 | tf_op jit(solution)/shard_map/ppermute | solution.py:45
  52.5 16.9 %collective-permute-start.19 = (bf16[2,1,2,2,48,512]{5,4,3,2,1,0:T(8,128)(2,1)S(1)}, bf16[2,1,2,2,48,512]{5,4,3,2,1,0:T(8,128)(2,1)}, u32[]{:S(2)}, u32[]{:S(2)}) collective-permute-start(bf16[2,1,2,2,48,512]{5,4,3,2,1,0:T(8,128)(2,1)S(1)} %pad_maximum_fusion.39), channel_id=1, source_target_pairs={{0,8},{2,10},{4,12},{6,14},{8,0},{10,2},{12,4},{14,6},{16,24},{18,... | collective-permute-start | bytes 1179656 | tf_op jit(solution)/shard_map/ppermute | solution.py:45
  52.5 16.3 %collective-permute-start.21 = (bf16[2,1,1,1,48,1536]{5,4,3,2,1,0:T(8,128)(2,1)S(1)}, bf16[2,1,1,1,48,1536]{5,4,3,2,1,0:T(8,128)(2,1)S(1)}, u32[]{:S(2)}, u32[]{:S(2)}) collective-permute-start(bf16[2,1,1,1,48,1536]{5,4,3,2,1,0:T(8,128)(2,1)S(1)} %pad_maximum_fusion.44), channel_id=1, source_target_pairs={{0,2},{2,0},{4,6},{6,4},{8,10},{10,8},{12,14},{14,12},{16,18},{18,... | collective-permute-start | bytes 884744 | tf_op jit(solution)/shard_map/ppermute | solution.py:45
  59.8 9.5 %collective-permute-start.22 = (bf16[2,1,1,1,48,1536]{5,4,3,2,1,0:T(8,128)(2,1)S(1)}, bf16[2,1,1,1,48,1536]{5,4,3,2,1,0:T(8,128)(2,1)S(1)}, u32[]{:S(2)}, u32[]{:S(2)}) collective-permute-start(bf16[2,1,1,1,48,1536]{5,4,3,2,1,0:T(8,128)(2,1)S(1)} %pad_maximum_fusion.45), channel_id=1, source_target_pairs={{0,8},{2,10},{4,12},{6,14},{8,0},{10,2},{12,4},{14,6},{16,24},{18,... | collective-permute-start | bytes 884744 | tf_op jit(solution)/shard_map/ppermute | solution.py:45
  78.6 23.0 %collective-permute-start.24 = (bf16[2,1,2,1,48,1536]{5,4,3,2,1,0:T(8,128)(2,1)S(1)}, bf16[2,1,2,1,48,1536]{5,4,3,2,1,0:T(8,128)(2,1)}, u32[]{:S(2)}, u32[]{:S(2)}) collective-permute-start(bf16[2,1,2,1,48,1536]{5,4,3,2,1,0:T(8,128)(2,1)S(1)} %pad_maximum_fusion.28), channel_id=1, source_target_pairs={{0,8},{2,10},{4,12},{6,14},{8,0},{10,2},{12,4},{14,6},{16,24},{18,... | collective-permute-start | bytes 1769480 | tf_op jit(solution)/shard_map/ppermute | solution.py:45
  81.1 20.5 %collective-permute-start.25 = (bf16[2,1,1,2,48,1536]{5,4,3,2,1,0:T(8,128)(2,1)S(1)}, bf16[2,1,1,2,48,1536]{5,4,3,2,1,0:T(8,128)(2,1)}, u32[]{:S(2)}, u32[]{:S(2)}) collective-permute-start(bf16[2,1,1,2,48,1536]{5,4,3,2,1,0:T(8,128)(2,1)S(1)} %pad_maximum_fusion.29), channel_id=1, source_target_pairs={{0,4},{2,6},{4,0},{6,2},{8,12},{10,14},{12,8},{14,10},{16,20},{18,... | collective-permute-start | bytes 1769480 | tf_op jit(solution)/shard_map/ppermute | solution.py:45
  82.6 19.0 %collective-permute-start.26 = (bf16[2,2,1,1,48,1536]{5,4,3,2,1,0:T(8,128)(2,1)S(1)}, bf16[2,2,1,1,48,1536]{5,4,3,2,1,0:T(8,128)(2,1)}, u32[]{:S(2)}, u32[]{:S(2)}) collective-permute-start(bf16[2,2,1,1,48,1536]{5,4,3,2,1,0:T(8,128)(2,1)S(1)} %pad_maximum_fusion.30), channel_id=1, source_target_pairs={{0,2},{2,0},{4,6},{6,4},{8,10},{10,8},{12,14},{14,12},{16,18},{18,... | collective-permute-start | bytes 1769480 | tf_op jit(solution)/shard_map/ppermute | solution.py:45
  85.0 22.4 %collective-permute-start.27 = (bf16[1,1,1,1,48,1536]{5,4,3,2,1,0:T(8,128)(2,1)}, bf16[1,1,1,1,48,1536]{5,4,3,2,1,0:T(8,128)(2,1)}, u32[]{:S(2)}, u32[]{:S(2)}) collective-permute-start(bf16[1,1,1,1,48,1536]{5,4,3,2,1,0:T(8,128)(2,1)} %get-tuple-element.251), channel_id=1, source_target_pairs={{0,16},{2,18},{4,20},{6,22},{8,24},{10,26},{12,28},{14,30},{16,0},... | collective-permute-start | bytes 442376 | tf_op jit(solution)/shard_map/ppermute | solution.py:45
  89.9 17.5 %collective-permute-start.28 = (bf16[1,1,1,1,48,1536]{5,4,3,2,1,0:T(8,128)(2,1)}, bf16[1,1,1,1,48,1536]{5,4,3,2,1,0:T(8,128)(2,1)}, u32[]{:S(2)}, u32[]{:S(2)}) collective-permute-start(bf16[1,1,1,1,48,1536]{5,4,3,2,1,0:T(8,128)(2,1)} %get-tuple-element.252), channel_id=1, source_target_pairs={{0,16},{2,18},{4,20},{6,22},{8,24},{10,26},{12,28},{14,30},{16,0},... | collective-permute-start | bytes 442376 | tf_op jit(solution)/shard_map/ppermute | solution.py:45
  116.4 29.1 %collective-permute-start.31 = (bf16[2,2,2,1,48,1536]{5,4,3,2,1,0:T(8,128)(2,1)}, bf16[2,2,2,1,48,1536]{5,4,3,2,1,0:T(8,128)(2,1)S(1)}, u32[]{:S(2)}, u32[]{:S(2)}) collective-permute-start(bf16[2,2,2,1,48,1536]{5,4,3,2,1,0:T(8,128)(2,1)} %pad_maximum_fusion.12), channel_id=1, source_target_pairs={{0,2},{2,0},{4,6},{6,4},{8,10},{10,8},{12,14},{14,12},{16,18},{18,... | collective-permute-start | bytes 3538952 | tf_op jit(solution)/shard_map/ppermute | solution.py:45
  117.9 28.4 %collective-permute-start.32 = (bf16[2,1,2,2,48,1536]{5,4,3,2,1,0:T(8,128)(2,1)}, bf16[2,1,2,2,48,1536]{5,4,3,2,1,0:T(8,128)(2,1)}, u32[]{:S(2)}, u32[]{:S(2)}) collective-permute-start(bf16[2,1,2,2,48,1536]{5,4,3,2,1,0:T(8,128)(2,1)} %pad_maximum_fusion.13), channel_id=1, source_target_pairs={{0,8},{2,10},{4,12},{6,14},{8,0},{10,2},{12,4},{14,6},{16,24},{18,... | collective-permute-start | bytes 3538952 | tf_op jit(solution)/shard_map/ppermute | solution.py:45
  118.0 28.9 %collective-permute-start.33 = (bf16[2,2,1,2,48,1536]{5,4,3,2,1,0:T(8,128)(2,1)S(1)}, bf16[2,2,1,2,48,1536]{5,4,3,2,1,0:T(8,128)(2,1)}, u32[]{:S(2)}, u32[]{:S(2)}) collective-permute-start(bf16[2,2,1,2,48,1536]{5,4,3,2,1,0:T(8,128)(2,1)S(1)} %pad_maximum_fusion.14), channel_id=1, source_target_pairs={{0,4},{2,6},{4,0},{6,2},{8,12},{10,14},{12,8},{14,10},{16,20},{18,... | collective-permute-start | bytes 3538952 | tf_op jit(solution)/shard_map/ppermute | solution.py:45
  126.3 38.1 %collective-permute-start.34 = (bf16[2,1,1,1,48,1536]{5,4,3,2,1,0:T(8,128)(2,1)S(1)}, bf16[2,1,1,1,48,1536]{5,4,3,2,1,0:T(8,128)(2,1)}, u32[]{:S(2)}, u32[]{:S(2)}) collective-permute-start(bf16[2,1,1,1,48,1536]{5,4,3,2,1,0:T(8,128)(2,1)S(1)} %copy-done.18), channel_id=1, source_target_pairs={{0,4},{2,6},{4,0},{6,2},{8,12},{10,14},{12,8},{14,10},{16,20},{18,... | collective-permute-start | bytes 884744 | tf_op jit(solution)/shard_map/ppermute | solution.py:45
  127.8 36.5 %collective-permute-start.35 = (bf16[2,1,1,1,48,1536]{5,4,3,2,1,0:T(8,128)(2,1)S(1)}, bf16[2,1,1,1,48,1536]{5,4,3,2,1,0:T(8,128)(2,1)}, u32[]{:S(2)}, u32[]{:S(2)}) collective-permute-start(bf16[2,1,1,1,48,1536]{5,4,3,2,1,0:T(8,128)(2,1)S(1)} %copy-done.19), channel_id=1, source_target_pairs={{0,2},{2,0},{4,6},{6,4},{8,10},{10,8},{12,14},{14,12},{16,18},{18,... | collective-permute-start | bytes 884744 | tf_op jit(solution)/shard_map/ppermute | solution.py:45
  170.4 14.0 %collective-permute-start.37 = (bf16[2,1,2,1,48,1536]{5,4,3,2,1,0:T(8,128)(2,1)S(1)}, bf16[2,1,2,1,48,1536]{5,4,3,2,1,0:T(8,128)(2,1)S(1)}, u32[]{:S(2)}, u32[]{:S(2)}) collective-permute-start(bf16[2,1,2,1,48,1536]{5,4,3,2,1,0:T(8,128)(2,1)S(1)} %pad_maximum_fusion.32), channel_id=1, source_target_pairs={{0,8},{2,10},{4,12},{6,14},{8,0},{10,2},{12,4},{14,6},{16,24},{18,... | collective-permute-start | bytes 1769480 | tf_op jit(solution)/shard_map/ppermute | solution.py:45
  172.4 12.9 %collective-permute-start.38 = (bf16[2,1,1,2,48,1536]{5,4,3,2,1,0:T(8,128)(2,1)S(1)}, bf16[2,1,1,2,48,1536]{5,4,3,2,1,0:T(8,128)(2,1)S(1)}, u32[]{:S(2)}, u32[]{:S(2)}) collective-permute-start(bf16[2,1,1,2,48,1536]{5,4,3,2,1,0:T(8,128)(2,1)S(1)} %pad_maximum_fusion.33), channel_id=1, source_target_pairs={{0,4},{2,6},{4,0},{6,2},{8,12},{10,14},{12,8},{14,10},{16,20},{18,... | collective-permute-start | bytes 1769480 | tf_op jit(solution)/shard_map/ppermute | solution.py:45
  190.9 30.2 %collective-permute-start.43 = (bf16[2,2,2,1,48,1536]{5,4,3,2,1,0:T(8,128)(2,1)}, bf16[2,2,2,1,48,1536]{5,4,3,2,1,0:T(8,128)(2,1)S(1)}, u32[]{:S(2)}, u32[]{:S(2)}) collective-permute-start(bf16[2,2,2,1,48,1536]{5,4,3,2,1,0:T(8,128)(2,1)} %pad_maximum_fusion.15), channel_id=1, source_target_pairs={{0,2},{2,0},{4,6},{6,4},{8,10},{10,8},{12,14},{14,12},{16,18},{18,... | collective-permute-start | bytes 3538952 | tf_op jit(solution)/shard_map/ppermute | solution.py:45
  191.5 29.6 %collective-permute-start.44 = (bf16[2,1,2,2,48,1536]{5,4,3,2,1,0:T(8,128)(2,1)}, bf16[2,1,2,2,48,1536]{5,4,3,2,1,0:T(8,128)(2,1)S(1)}, u32[]{:S(2)}, u32[]{:S(2)}) collective-permute-start(bf16[2,1,2,2,48,1536]{5,4,3,2,1,0:T(8,128)(2,1)} %pad_maximum_fusion.16), channel_id=1, source_target_pairs={{0,8},{2,10},{4,12},{6,14},{8,0},{10,2},{12,4},{14,6},{16,24},{18,... | collective-permute-start | bytes 3538952 | tf_op jit(solution)/shard_map/ppermute | solution.py:45
  235.0 37.0 %collective-permute-start.50 = (bf16[2,2,2,1,48,1536]{5,4,3,2,1,0:T(8,128)(2,1)}, bf16[2,2,2,1,48,1536]{5,4,3,2,1,0:T(8,128)(2,1)}, u32[]{:S(2)}, u32[]{:S(2)}) collective-permute-start(bf16[2,2,2,1,48,1536]{5,4,3,2,1,0:T(8,128)(2,1)} %slice.999), channel_id=1, source_target_pairs={{0,2},{2,0},{4,6},{6,4},{8,10},{10,8},{12,14},{14,12},{16,18},{18,... | collective-permute-start | bytes 3538952 | tf_op jit(solution)/shard_map/ppermute | solution.py:45
  236.4 35.6 %collective-permute-start.51 = (bf16[2,1,2,2,48,1536]{5,4,3,2,1,0:T(8,128)(2,1)}, bf16[2,1,2,2,48,1536]{5,4,3,2,1,0:T(8,128)(2,1)}, u32[]{:S(2)}, u32[]{:S(2)}) collective-permute-start(bf16[2,1,2,2,48,1536]{5,4,3,2,1,0:T(8,128)(2,1)} %slice.1000), channel_id=1, source_target_pairs={{0,8},{2,10},{4,12},{6,14},{8,0},{10,2},{12,4},{14,6},{16,24},{18,... | collective-permute-start | bytes 3538952 | tf_op jit(solution)/shard_map/ppermute | solution.py:45
  285.3 9.6 %collective-permute-start.52 = (bf16[1,1,1,1,8,7680]{5,4,3,2,1,0:T(8,128)(2,1)}, bf16[1,1,1,1,8,7680]{5,4,3,2,1,0:T(8,128)(2,1)S(1)}, u32[]{:S(2)}, u32[]{:S(2)}) collective-permute-start(bf16[1,1,1,1,8,7680]{5,4,3,2,1,0:T(8,128)(2,1)} %bitcast.50), channel_id=1, source_target_pairs={{0,16},{2,18},{4,20},{6,22},{8,24},{10,26},{12,28},{14,30},{16,0},... | collective-permute-start | bytes 368648 | tf_op jit(solution)/shard_map/ppermute | solution.py:45
  286.2 23.5 %collective-permute-start.54 = (bf16[2,1,2,1,48,1536]{5,4,3,2,1,0:T(8,128)(2,1)}, bf16[2,1,2,1,48,1536]{5,4,3,2,1,0:T(8,128)(2,1)}, u32[]{:S(2)}, u32[]{:S(2)}) collective-permute-start(bf16[2,1,2,1,48,1536]{5,4,3,2,1,0:T(8,128)(2,1)} %get-tuple-element.308), channel_id=1, source_target_pairs={{0,8},{2,10},{4,12},{6,14},{8,0},{10,2},{12,4},{14,6},{16,24},{18,... | collective-permute-start | bytes 1769480 | tf_op jit(solution)/shard_map/ppermute | solution.py:45
  287.5 22.2 %collective-permute-start.55 = (bf16[2,1,1,2,48,1536]{5,4,3,2,1,0:T(8,128)(2,1)}, bf16[2,1,1,2,48,1536]{5,4,3,2,1,0:T(8,128)(2,1)}, u32[]{:S(2)}, u32[]{:S(2)}) collective-permute-start(bf16[2,1,1,2,48,1536]{5,4,3,2,1,0:T(8,128)(2,1)} %get-tuple-element.309), channel_id=1, source_target_pairs={{0,4},{2,6},{4,0},{6,2},{8,12},{10,14},{12,8},{14,10},{16,20},{18,... | collective-permute-start | bytes 1769480 | tf_op jit(solution)/shard_map/ppermute | solution.py:45
  299.0 10.8 %collective-permute-start.56 = (bf16[2,1,1,1,8,7680]{5,4,3,2,1,0:T(8,128)(2,1)S(1)}, bf16[2,1,1,1,8,7680]{5,4,3,2,1,0:T(8,128)(2,1)S(1)}, u32[]{:S(2)}, u32[]{:S(2)}) collective-permute-start(bf16[2,1,1,1,8,7680]{5,4,3,2,1,0:T(8,128)(2,1)S(1)} %pad_maximum_fusion.48), channel_id=1, source_target_pairs={{0,8},{2,10},{4,12},{6,14},{8,0},{10,2},{12,4},{14,6},{16,24},{18,... | collective-permute-start | bytes 737288 | tf_op jit(solution)/shard_map/ppermute | solution.py:45
  331.5 11.8 %collective-permute-start.58 = (f32[2,768]{1,0:T(2,128)S(1)}, f32[2,768]{1,0:T(2,128)S(1)}, u32[]{:S(2)}, u32[]{:S(2)}) collective-permute-start(f32[2,768]{1,0:T(2,128)S(1)} %pad_maximum_fusion.63), channel_id=1, source_target_pairs={{0,1},{1,0},{2,3},{3,2},{4,5},{5,4},{6,7},{7,6},{8,9},{9,8},{10,11... | collective-permute-start | bytes 18440 | tf_op jit(solution)/shard_map/ppermute | solution.py:49
  331.5 17.8 %collective-permute-start.61 = (bf16[1,1,1,1,8,5760]{5,4,3,2,1,0:T(8,128)(2,1)}, bf16[1,1,1,1,8,5760]{5,4,3,2,1,0:T(8,128)(2,1)}, u32[]{:S(2)}, u32[]{:S(2)}) collective-permute-start(bf16[1,1,1,1,8,5760]{5,4,3,2,1,0:T(8,128)(2,1)} %bitcast.63), channel_id=1, source_target_pairs={{0,16},{2,18},{4,20},{6,22},{8,24},{10,26},{12,28},{14,30},{16,0},... | collective-permute-start | bytes 276488 | tf_op jit(solution)/shard_map/ppermute | solution.py:45
  338.2 12.6 %collective-permute-start.59 = (bf16[2,1,1,1,48,1536]{5,4,3,2,1,0:T(8,128)(2,1)}, bf16[2,1,1,1,48,1536]{5,4,3,2,1,0:T(8,128)(2,1)}, u32[]{:S(2)}, u32[]{:S(2)}) collective-permute-start(bf16[2,1,1,1,48,1536]{5,4,3,2,1,0:T(8,128)(2,1)} %get-tuple-element.327), channel_id=1, source_target_pairs={{0,4},{2,6},{4,0},{6,2},{8,12},{10,14},{12,8},{14,10},{16,20},{18,... | collective-permute-start | bytes 884744 | tf_op jit(solution)/shard_map/ppermute | solution.py:45
  338.8 13.6 %collective-permute-start.60 = (bf16[2,1,1,1,48,1536]{5,4,3,2,1,0:T(8,128)(2,1)}, bf16[2,1,1,1,48,1536]{5,4,3,2,1,0:T(8,128)(2,1)}, u32[]{:S(2)}, u32[]{:S(2)}) collective-permute-start(bf16[2,1,1,1,48,1536]{5,4,3,2,1,0:T(8,128)(2,1)} %get-tuple-element.328), channel_id=1, source_target_pairs={{0,2},{2,0},{4,6},{6,4},{8,10},{10,8},{12,14},{14,12},{16,18},{18,... | collective-permute-start | bytes 884744 | tf_op jit(solution)/shard_map/ppermute | solution.py:45
  339.3 28.9 %collective-permute-start.65 = (bf16[2,2,1,1,8,7680]{5,4,3,2,1,0:T(8,128)(2,1)S(1)}, bf16[2,2,1,1,8,7680]{5,4,3,2,1,0:T(8,128)(2,1)}, u32[]{:S(2)}, u32[]{:S(2)}) collective-permute-start(bf16[2,2,1,1,8,7680]{5,4,3,2,1,0:T(8,128)(2,1)S(1)} %pad_maximum_fusion.34), channel_id=1, source_target_pairs={{0,2},{2,0},{4,6},{6,4},{8,10},{10,8},{12,14},{14,12},{16,18},{18,... | collective-permute-start | bytes 1474568 | tf_op jit(solution)/shard_map/ppermute | solution.py:45
  348.7 18.0 %collective-permute-start.63 = (bf16[2,2,2,1,48,512]{5,4,3,2,1,0:T(8,128)(2,1)}, bf16[2,2,2,1,48,512]{5,4,3,2,1,0:T(8,128)(2,1)S(1)}, u32[]{:S(2)}, u32[]{:S(2)}) collective-permute-start(bf16[2,2,2,1,48,512]{5,4,3,2,1,0:T(8,128)(2,1)} %pad_maximum_fusion.40), channel_id=1, source_target_pairs={{0,2},{2,0},{4,6},{6,4},{8,10},{10,8},{12,14},{14,12},{16,18},{18,... | collective-permute-start | bytes 1179656 | tf_op jit(solution)/shard_map/ppermute | solution.py:45
  349.4 18.8 %collective-permute-start.64 = (bf16[2,1,2,2,48,512]{5,4,3,2,1,0:T(8,128)(2,1)S(1)}, bf16[2,1,2,2,48,512]{5,4,3,2,1,0:T(8,128)(2,1)S(1)}, u32[]{:S(2)}, u32[]{:S(2)}) collective-permute-start(bf16[2,1,2,2,48,512]{5,4,3,2,1,0:T(8,128)(2,1)S(1)} %copy-done.36), channel_id=1, source_target_pairs={{0,8},{2,10},{4,12},{6,14},{8,0},{10,2},{12,4},{14,6},{16,24},{18,... | collective-permute-start | bytes 1179656 | tf_op jit(solution)/shard_map/ppermute | solution.py:45
  350.8 17.4 %collective-permute-start.62 = (bf16[2,2,1,2,48,640]{5,4,3,2,1,0:T(8,128)(2,1)S(1)}, bf16[2,2,1,2,48,640]{5,4,3,2,1,0:T(8,128)(2,1)S(1)}, u32[]{:S(2)}, u32[]{:S(2)}) collective-permute-start(bf16[2,2,1,2,48,640]{5,4,3,2,1,0:T(8,128)(2,1)S(1)} %pad_maximum_fusion.35), channel_id=1, source_target_pairs={{0,4},{2,6},{4,0},{6,2},{8,12},{10,14},{12,8},{14,10},{16,20},{18,... | collective-permute-start | bytes 1474568 | tf_op jit(solution)/shard_map/ppermute | solution.py:45
  356.7 37.6 %collective-permute-start.77 = (bf16[1,1,1,1,48,1536]{5,4,3,2,1,0:T(8,128)(2,1)S(1)}, bf16[1,1,1,1,48,1536]{5,4,3,2,1,0:T(8,128)(2,1)S(1)}, u32[]{:S(2)}, u32[]{:S(2)}) collective-permute-start(bf16[1,1,1,1,48,1536]{5,4,3,2,1,0:T(8,128)(2,1)S(1)} %get-tuple-element.367), channel_id=1, source_target_pairs={{0,16},{2,18},{4,20},{6,22},{8,24},{10,26},{12,28},{14,30},{16,0},... | collective-permute-start | bytes 442376 | tf_op jit(solution)/shard_map/ppermute | solution.py:45
  373.1 9.8 %collective-permute-start.80 = (bf16[2,1,2,1,8,5760]{5,4,3,2,1,0:T(8,128)(2,1)S(1)}, bf16[2,1,2,1,8,5760]{5,4,3,2,1,0:T(8,128)(2,1)S(1)}, u32[]{:S(2)}, u32[]{:S(2)}) collective-permute-start(bf16[2,1,2,1,8,5760]{5,4,3,2,1,0:T(8,128)(2,1)S(1)} %pad_maximum_fusion.42), channel_id=1, source_target_pairs={{0,8},{2,10},{4,12},{6,14},{8,0},{10,2},{12,4},{14,6},{16,24},{18,... | collective-permute-start | bytes 1105928 | tf_op jit(solution)/shard_map/ppermute | solution.py:45
  376.2 14.4 %collective-permute-start.67 = (bf16[512,768]{1,0:T(8,128)(2,1)S(1)}, bf16[512,768]{1,0:T(8,128)(2,1)S(1)}, u32[]{:S(2)}, u32[]{:S(2)}) collective-permute-start(bf16[512,768]{1,0:T(8,128)(2,1)S(1)} %slice.896), channel_id=1, source_target_pairs={{0,1},{1,0},{2,3},{3,2},{4,5},{5,4},{6,7},{7,6},{8,9},{9,8},{10,11... | collective-permute-start | bytes 2359304 | tf_op jit(solution)/shard_map/ppermute | solution.py:49
  385.0 10.3 %collective-permute-start.78 = (bf16[1,1,1,1,48,1536]{5,4,3,2,1,0:T(8,128)(2,1)S(1)}, bf16[1,1,1,1,48,1536]{5,4,3,2,1,0:T(8,128)(2,1)S(1)}, u32[]{:S(2)}, u32[]{:S(2)}) collective-permute-start(bf16[1,1,1,1,48,1536]{5,4,3,2,1,0:T(8,128)(2,1)S(1)} %get-tuple-element.368), channel_id=1, source_target_pairs={{0,16},{2,18},{4,20},{6,22},{8,24},{10,26},{12,28},{14,30},{16,0},... | collective-permute-start | bytes 442376 | tf_op jit(solution)/shard_map/ppermute | solution.py:45
  385.2 20.5 %collective-permute-start.79 = (bf16[2,2,1,2,8,7680]{5,4,3,2,1,0:T(8,128)(2,1)S(1)}, bf16[2,2,1,2,8,7680]{5,4,3,2,1,0:T(8,128)(2,1)S(1)}, u32[]{:S(2)}, u32[]{:S(2)}) collective-permute-start(bf16[2,2,1,2,8,7680]{5,4,3,2,1,0:T(8,128)(2,1)S(1)} %pad_maximum_fusion.21), channel_id=1, source_target_pairs={{0,4},{2,6},{4,0},{6,2},{8,12},{10,14},{12,8},{14,10},{16,20},{18,... | collective-permute-start | bytes 2949128 | tf_op jit(solution)/shard_map/ppermute | solution.py:45
  388.7 17.0 %collective-permute-start.81 = (bf16[2,2,2,1,8,5760]{5,4,3,2,1,0:T(8,128)(2,1)S(1)}, bf16[2,2,2,1,8,5760]{5,4,3,2,1,0:T(8,128)(2,1)S(1)}, u32[]{:S(2)}, u32[]{:S(2)}) collective-permute-start(bf16[2,2,2,1,8,5760]{5,4,3,2,1,0:T(8,128)(2,1)S(1)} %pad_maximum_fusion.25), channel_id=1, source_target_pairs={{0,2},{2,0},{4,6},{6,4},{8,10},{10,8},{12,14},{14,12},{16,18},{18,... | collective-permute-start | bytes 2211848 | tf_op jit(solution)/shard_map/ppermute | solution.py:45
  (190 other events, 1673.7 us)

commit v4 on v3

--- a/solution.py
+++ b/solution.py
@@ -576,25 +576,22 @@
     two = Gather([w_up[1], w_down[1].T], orders[1:], bits, count)
     got = swap_dp(small, bits - 3, count)
     one_q.send()
+    got = settle(got, one_q)
+    small = small + got
+    got = swap_dp(small, bits - 2, count)
+    one_q.send()
     one_q.state[0], *one_m.state = tie(one_q.state[0], *one_m.state)
     one_m.send()
     got = settle(got, one_q)
     small = small + got
-    got = swap_dp(small, bits - 2, count)
-    one_q.send()
-    got = settle(got, one_q, one_m)
-    small = small + got
     last = swap_dp(small, bits - 1, count)
     small = launch(small, one_q)
-    small = launch(small, one_m)
     while one_q.left() > 1:
         small = advance(small, one_q)
     x_own = dot_nn(layer_input[0], perm).astype(BF)
     x_full = jnp.concatenate([x_own, swap_half(x_own)], axis=0)
     x_full = settle(x_full, one_q, one_m)
-    x_full, *two.state = tie(x_full, *two.state)
     x_full = launch(x_full, one_m)
-    x_full = launch(x_full, two)
     x_full, last = tie(x_full, last)
     small = small + last
 
@@ -648,6 +645,9 @@
     w_qkv_r = jnp.concatenate([w[:, :three] for w in attn_r], axis=1)
     w_out_r = jnp.concatenate([w[:, three:] for w in attn_r], axis=1)
     qkv = (dot_nn(x_full, w_qkv_r) + v1["qkv"]).astype(BF)
+    qkv = advance(qkv, one_m)
+    qkv, *two.state = tie(qkv, *two.state)
+    qkv = launch(qkv, two)
     attended = attn_fwd(seg_counts, qkv)
     while one_m.left() > 1:
         attended = advance(attended, one_m)

time: 428 us -> 432 us (level)
    concatenate x39 -> x40, other arithmetic: 37.7 us -> 43.2 us  [join(): return jnp.concatenate([low, high], axis=bits - 1 - bit)]
    unnamed x345 -> x346, local copies, waits for them, and re-layouts: 19.2 us -> 21.8 us
  transfers between devices with their start and end apart: 82 -> 82, of which waited for: 27 -> 31; matrix products, arithmetic and copies ran while one was open for 34% -> 32% of each run, Pallas kernels for 8% -> 8%
where the time goes in v4:
time: 432 us; the launch traced here: 424 us
  other arithmetic  92.7 us (21%)
  starting transfers between devices  79.3 us (18%)
  waiting for transfers between devices  76.5 us (18%)
  Pallas kernels  65.2 us (15%)
  local copies, waits for them, and re-layouts  59.2 us (14%)
  matrix products  46 us (11%)
  between operations  4.57 us (1%)
    ppermute x64, waiting for transfers between devices, swap_dp(): return lax.ppermute(values, 'dp', [(i, i ^ 1 << bit) for i in range(count)])  76.1 us
    ppermute x64, starting transfers between devices, swap_dp(): return lax.ppermute(values, 'dp', [(i, i ^ 1 << bit) for i in range(count)])  75.2 us
    concatenate x40, other arithmetic, join(): return jnp.concatenate([low, high], axis=bits - 1 - bit)  43.2 us
    unnamed x346, local copies, waits for them, and re-layouts  21.8 us
    pallas_call x5, Pallas kernels, cls_call(): pl.pallas_call(kernel, grid_spec=pltpu.PrefetchScalarGridSpec(num_scalar_...  21.1 us
    dot_general x10, matrix products, dot_nn(): lax.dot_general(a, b, (((1,), (0,)), ((), ())), preferred_element_type=F32)  17.4 us
    pallas_call x1, Pallas kernels, attn_bwd(): pl.pallas_call(attn_bwd_kernel, grid_spec=pltpu.PrefetchScalarGridSpec(nu...  15.6 us
    pallas_call x1, Pallas kernels, up_gelu(): pl.pallas_call(up_kernel, grid=(hidden // tile_h, total // tile_r), in_sp...  12.5 us
  transfers between devices with their start and end apart: 82, of which 31 were waited for; matrix products, arithmetic and copies ran while one was open for 32% of the time, Pallas kernels for 8%

profile of v4, /device:TPU:0, one launch (start us, length us, event | category | flops | bytes accessed | tf_op | source)
XLA Modules:
  0.0 423.5 jit_solution(7616924882958764258)
XLA Ops:
  6.0 3.7 collective-permute-start.3
  9.7 3.0 collective-permute-start.5
  15.4 2.1 collective-permute-done.2
  35.5 2.2 collective-permute-start.14
  38.3 2.2 collective-permute-start.17
  40.5 7.1 %collective-permute-done.17 = bf16[1,1,1,1,48,1536]{5,4,3,2,1,0:T(8,128)(2,1)S(1)} collective-permute-done((bf16[1,1,1,1,48,1536]{5,4,3,2,1,0:T(8,128)(2,1)S(1)}, bf16[1,1,1,1,48,1536]{5,4,3,2,1,0:T(8,128)(2,1)S(1)}, u32[]{:S(2)}, u32[]{:S(2)}) %collective-permute-start.17) | collective-permute-done | bytes 147488 | tf_op jit(solution)/shard_map/ppermute | solution.py:45
  47.6 3.5 collective-permute-start.18
  52.4 9.3 %collective-permute-done.18 = bf16[1,1,1,1,48,1536]{5,4,3,2,1,0:T(8,128)(2,1)S(1)} collective-permute-done((bf16[1,1,1,1,48,1536]{5,4,3,2,1,0:T(8,128)(2,1)S(1)}, bf16[1,1,1,1,48,1536]{5,4,3,2,1,0:T(8,128)(2,1)S(1)}, u32[]{:S(2)}, u32[]{:S(2)}) %collective-permute-start.18) | collective-permute-done | bytes 147488 | tf_op jit(solution)/shard_map/ppermute | solution.py:45
  77.4 3.7 add_convert_fusion.qkv_ref
  86.6 2.0 collective-permute-start.24
  92.9 2.4 collective-permute-start.28
  95.4 10.0 %attn_fwd.1 = bf16[1024,384]{1,0:T(8,128)(2,1)} custom-call(s32[8]{0:T(128)} %fusion.71.count_ref, bf16[1024,1152]{1,0:T(8,128)(2,1)} %add_convert_fusion.qkv_ref), custom_call_target="tpu_custom_call" | custom-call | flops 1 | bytes 1 | tf_op jit(solution)/shard_map/attn_fwd/pallas_call | solution.py:229
  105.3 2.4 pad_maximum_fusion.12
  107.7 2.4 pad_maximum_fusion.13
  133.7 15.9 %collective-permute-done.31 = bf16[2,2,2,1,48,1536]{5,4,3,2,1,0:T(8,128)(2,1)S(1)} collective-permute-done((bf16[2,2,2,1,48,1536]{5,4,3,2,1,0:T(8,128)(2,1)}, bf16[2,2,2,1,48,1536]{5,4,3,2,1,0:T(8,128)(2,1)S(1)}, u32[]{:S(2)}, u32[]{:S(2)}) %collective-permute-start.31) | collective-permute-done | bytes 1179680 | tf_op jit(solution)/shard_map/ppermute | solution.py:45
  150.9 2.9 pad_maximum_fusion
  153.8 12.5 %up_gelu.1 = (bf16[1024,1536]{1,0:T(8,128)(2,1)}, bf16[1024,1536]{1,0:T(8,128)(2,1)}) custom-call(bf16[1024,768]{1,0:T(8,128)(2,1)} %pad_maximum_fusion.8.rows_ref, bf16[768,1536]{1,0:T(8,128)(2,1)} %bitcast.217, f32[1,1536]{1,0:T(1,128)} %get-tuple-element.568.bias_ref), custom_call_target="tpu_custom_call" | custom-call | flops 1 | bytes 1 | tf_op jit(solution)/shard_map/up_gelu/pallas_call | solution.py:277
  174.4 2.1 collective-permute-start.37
  177.4 2.6 convolution_convert_fusion.6
  180.8 2.9 pad_maximum_fusion.2
  184.9 3.5 collective-permute-done.37
  199.9 3.7 multiply_convert_fusion
  203.7 2.6 convolution_convert_fusion.5
  207.8 2.9 convolution_convert_fusion.1
  216.8 3.1 convolution_convert_fusion
  225.2 3.3 pad_maximum_fusion.3
  229.1 4.2 cls_attn.1
  235.2 3.0 pad_maximum_fusion.4
  242.7 4.3 %cls_up.1 = (bf16[8,1536]{1,0:T(8,128)(2,1)}, f32[16,1536]{1,0:T(8,128)}, f32[16,768]{1,0:T(8,128)}) custom-call(bf16[16,768]{1,0:T(8,128)(2,1)} %fusion.38.rows_ref, bf16[768,1536]{1,0:T(8,128)(2,1)} %bitcast.205, bf16[768,1536]{1,0:T(8,128)(2,1)} %bitcast.206, bf16[768,1536]{1,0:T(8,128)(2,1)} %bitcast.207, bf16[768,1536]{1,0:T(8,128)(2,1)} %bitcast.211, ...), custom_call_target="tpu_custom_call" | custom-call | flops 1 | bytes 1 | tf_op jit(solution)/shard_map/cls_up/pallas_call | solution.py:358
  253.1 4.1 cls_up_back.2
  263.7 4.3 %cls_attn_back.1 = (bf16[8,1152]{1,0:T(8,128)(2,1)}, f32[16,768]{1,0:T(8,128)}) custom-call(s32[1]{0:T(128)S(6)} %select_n.201.count_ref, bf16[16,768]{1,0:T(8,128)(2,1)} %get-tuple-element.464.grad_ref, bf16[768,1536]{1,0:T(8,128)(2,1)} %bitcast.202, bf16[768,1536]{1,0:T(8,128)(2,1)} %bitcast.203, bf16[768,1536]{1,0:T(8,128)(2,1)} %bitcast.204, ...), custom_call_target="tpu_custom_call" | custom-call | flops 1 | bytes 1 | tf_op jit(solution)/shard_map/cls_attn_back/pallas_call | solution.py:358
  275.9 2.9 add_convert_fusion.1
  278.8 2.4 add_convert_fusion.2
  282.8 4.1 cls_up_back.3
  293.4 2.2 fusion.32
  296.2 2.5 collective-permute-done.52
  305.5 2.0 concatenate.368
  309.8 4.4 %collective-permute-done.56 = bf16[2,1,1,1,8,7680]{5,4,3,2,1,0:T(8,128)(2,1)S(1)} collective-permute-done((bf16[2,1,1,1,8,7680]{5,4,3,2,1,0:T(8,128)(2,1)S(1)}, bf16[2,1,1,1,8,7680]{5,4,3,2,1,0:T(8,128)(2,1)S(1)}, u32[]{:S(2)}, u32[]{:S(2)}) %collective-permute-start.56) | collective-permute-done | bytes 245792 | tf_op jit(solution)/shard_map/ppermute | solution.py:45
  319.3 15.6 %attn_bwd.1 = (bf16[1024,1152]{1,0:T(8,128)(2,1)}, f32[1,1152]{1,0:T(1,128)}) custom-call(s32[8]{0:T(128)} %fusion.71.count_ref, bf16[1024,1152]{1,0:T(8,128)(2,1)} %add_convert_fusion.qkv_ref, bf16[1024,384]{1,0:T(8,128)(2,1)} %convolution_convert_fusion.7.grad_ref, f32[8,1,384]{2,1,0:T(1,128)} %reshape.553.first_ref), custom_call_target="tpu_custom_call" | custom-call | flops 1 | bytes 1 | tf_op jit(solution)/shard_map/attn_bwd/pallas_call | solution.py:246
  336.5 4.4 %convolution_convert_fusion.2 = bf16[768,1152]{1,0:T(8,128)(2,1)S(1)} fusion(bf16[1024,768]{1,0:T(8,128)(2,1)} %pad_maximum_fusion.7, bf16[1024,1152]{1,0:T(8,128)(2,1)} %get-tuple-element.331), kind=kOutput, calls=%fused_computation.4 | convolution fusion | flops 1812824064 | bytes 5701632 | tf_op jit(solution)/shard_map/dot_general | solution.py:35
  361.8 3.9 convolution_convert_fusion.4
  365.7 5.3 %collective-permute-done.63 = bf16[2,2,2,1,48,512]{5,4,3,2,1,0:T(8,128)(2,1)S(1)} collective-permute-done((bf16[2,2,2,1,48,512]{5,4,3,2,1,0:T(8,128)(2,1)}, bf16[2,2,2,1,48,512]{5,4,3,2,1,0:T(8,128)(2,1)S(1)}, u32[]{:S(2)}, u32[]{:S(2)}) %collective-permute-start.63) | collective-permute-done | bytes 393248 | tf_op jit(solution)/shard_map/ppermute | solution.py:45
  377.8 2.7 collective-permute-start.80
  383.3 3.8 collective-permute-done.80
  387.1 2.3 collective-permute-start.71
  402.0 2.0 add_bitcast_fusion
  405.3 4.2 %collective-permute-done.79 = bf16[2,2,1,2,8,7680]{5,4,3,2,1,0:T(8,128)(2,1)S(1)} collective-permute-done((bf16[2,2,1,2,8,7680]{5,4,3,2,1,0:T(8,128)(2,1)S(1)}, bf16[2,2,1,2,8,7680]{5,4,3,2,1,0:T(8,128)(2,1)S(1)}, u32[]{:S(2)}, u32[]{:S(2)}) %collective-permute-start.79) | collective-permute-done | bytes 983072 | tf_op jit(solution)/shard_map/ppermute | solution.py:45
  412.3 4.4 %owner_sums.1 = (f32[2,48,1152]{2,1,0:T(8,128)}, f32[2,48,384]{2,1,0:T(8,128)}, f32[2,48,1536]{2,1,0:T(8,128)}, f32[2,48,1536]{2,1,0:T(8,128)}, f32[48,128]{1,0:T(8,128)}) custom-call(bf16[128,7680]{1,0:T(8,128)(2,1)} %bitcast.229, bf16[128,5760]{1,0:T(8,128)(2,1)} %bitcast.230, bf16[768,48]{1,0:T(8,128)(2,1)} %constant.123.clone.pick_ref, ...), custom_call_target="tpu_custom_call" | custom-call | flops 1 | bytes 1 | tf_op jit(solution)/shard_map/owner_sums/pallas_call | solution.py:471
  (781 shorter events, 215.7 us)
Async XLA Ops:
  3.7 9.1 %collective-permute-start.1 = (f32[32,768]{1,0:T(8,128)S(1)}, f32[32,768]{1,0:T(8,128)S(1)}, u32[]{:S(2)}, u32[]{:S(2)}) collective-permute-start(f32[32,768]{1,0:T(8,128)S(1)} %pad_maximum_fusion.56), channel_id=1, source_target_pairs={{0,1},{1,0},{2,3},{3,2},{4,5},{5,4},{6,7},{7,6},{8,9},{9,8},{10,11... | collective-permute-start | bytes 294920 | tf_op jit(solution)/shard_map/ppermute | solution.py:49
  6.0 11.5 %collective-permute-start.3 = (bf16[1,1,1,1,48,512]{5,4,3,2,1,0:T(8,128)(2,1)S(1)}, bf16[1,1,1,1,48,512]{5,4,3,2,1,0:T(8,128)(2,1)S(1)}, u32[]{:S(2)}, u32[]{:S(2)}) collective-permute-start(bf16[1,1,1,1,48,512]{5,4,3,2,1,0:T(8,128)(2,1)S(1)} %maximum_bitcast_fusion), channel_id=1, source_target_pairs={{0,16},{2,18},{4,20},{6,22},{8,24},{10,26},{12,28},{14,30},{16,0},... | collective-permute-start | bytes 147464 | tf_op jit(solution)/shard_map/ppermute | solution.py:45
  15.3 35.8 %collective-permute-start = (bf16[512,768]{1,0:T(8,128)(2,1)S(1)}, bf16[512,768]{1,0:T(8,128)(2,1)S(1)}, u32[]{:S(2)}, u32[]{:S(2)}) collective-permute-start(bf16[512,768]{1,0:T(8,128)(2,1)S(1)} %fusion.8), channel_id=1, source_target_pairs={{0,1},{1,0},{2,3},{3,2},{4,5},{5,4},{6,7},{7,6},{8,9},{9,8},{10,11... | collective-permute-start | bytes 2359304 | tf_op jit(solution)/shard_map/ppermute | solution.py:49
  35.5 27.8 %collective-permute-start.14 = (bf16[2,2,1,2,48,512]{5,4,3,2,1,0:T(8,128)(2,1)S(1)}, bf16[2,2,1,2,48,512]{5,4,3,2,1,0:T(8,128)(2,1)S(1)}, u32[]{:S(2)}, u32[]{:S(2)}) collective-permute-start(bf16[2,2,1,2,48,512]{5,4,3,2,1,0:T(8,128)(2,1)S(1)} %pad_maximum_fusion.37), channel_id=1, source_target_pairs={{0,4},{2,6},{4,0},{6,2},{8,12},{10,14},{12,8},{14,10},{16,20},{18,... | collective-permute-start | bytes 1179656 | tf_op jit(solution)/shard_map/ppermute | solution.py:45
  37.7 25.6 %collective-permute-start.15 = (bf16[2,2,2,1,48,512]{5,4,3,2,1,0:T(8,128)(2,1)S(1)}, bf16[2,2,2,1,48,512]{5,4,3,2,1,0:T(8,128)(2,1)S(1)}, u32[]{:S(2)}, u32[]{:S(2)}) collective-permute-start(bf16[2,2,2,1,48,512]{5,4,3,2,1,0:T(8,128)(2,1)S(1)} %pad_maximum_fusion.38), channel_id=1, source_target_pairs={{0,2},{2,0},{4,6},{6,4},{8,10},{10,8},{12,14},{14,12},{16,18},{18,... | collective-permute-start | bytes 1179656 | tf_op jit(solution)/shard_map/ppermute | solution.py:45
  38.3 25.1 %collective-permute-start.16 = (bf16[2,1,2,2,48,512]{5,4,3,2,1,0:T(8,128)(2,1)S(1)}, bf16[2,1,2,2,48,512]{5,4,3,2,1,0:T(8,128)(2,1)S(1)}, u32[]{:S(2)}, u32[]{:S(2)}) collective-permute-start(bf16[2,1,2,2,48,512]{5,4,3,2,1,0:T(8,128)(2,1)S(1)} %pad_maximum_fusion.39), channel_id=1, source_target_pairs={{0,8},{2,10},{4,12},{6,14},{8,0},{10,2},{12,4},{14,6},{16,24},{18,... | collective-permute-start | bytes 1179656 | tf_op jit(solution)/shard_map/ppermute | solution.py:45
  38.3 9.4 %collective-permute-start.17 = (bf16[1,1,1,1,48,1536]{5,4,3,2,1,0:T(8,128)(2,1)S(1)}, bf16[1,1,1,1,48,1536]{5,4,3,2,1,0:T(8,128)(2,1)S(1)}, u32[]{:S(2)}, u32[]{:S(2)}) collective-permute-start(bf16[1,1,1,1,48,1536]{5,4,3,2,1,0:T(8,128)(2,1)S(1)} %get-tuple-element.215), channel_id=1, source_target_pairs={{0,16},{2,18},{4,20},{6,22},{8,24},{10,26},{12,28},{14,30},{16,0},... | collective-permute-start | bytes 442376 | tf_op jit(solution)/shard_map/ppermute | solution.py:45
  47.6 14.0 %collective-permute-start.18 = (bf16[1,1,1,1,48,1536]{5,4,3,2,1,0:T(8,128)(2,1)S(1)}, bf16[1,1,1,1,48,1536]{5,4,3,2,1,0:T(8,128)(2,1)S(1)}, u32[]{:S(2)}, u32[]{:S(2)}) collective-permute-start(bf16[1,1,1,1,48,1536]{5,4,3,2,1,0:T(8,128)(2,1)S(1)} %get-tuple-element.216), channel_id=1, source_target_pairs={{0,16},{2,18},{4,20},{6,22},{8,24},{10,26},{12,28},{14,30},{16,0},... | collective-permute-start | bytes 442376 | tf_op jit(solution)/shard_map/ppermute | solution.py:45
  51.1 12.2 %collective-permute-start.19 = (bf16[1,1,1,1,48,1536]{5,4,3,2,1,0:T(8,128)(2,1)S(1)}, bf16[1,1,1,1,48,1536]{5,4,3,2,1,0:T(8,128)(2,1)S(1)}, u32[]{:S(2)}, u32[]{:S(2)}) collective-permute-start(bf16[1,1,1,1,48,1536]{5,4,3,2,1,0:T(8,128)(2,1)S(1)} %bitcast.254), channel_id=1, source_target_pairs={{0,16},{2,18},{4,20},{6,22},{8,24},{10,26},{12,28},{14,30},{16,0},... | collective-permute-start | bytes 442376 | tf_op jit(solution)/shard_map/ppermute | solution.py:45
  70.7 10.3 %collective-permute-start.21 = (bf16[2,1,1,1,48,1536]{5,4,3,2,1,0:T(8,128)(2,1)}, bf16[2,1,1,1,48,1536]{5,4,3,2,1,0:T(8,128)(2,1)S(1)}, u32[]{:S(2)}, u32[]{:S(2)}) collective-permute-start(bf16[2,1,1,1,48,1536]{5,4,3,2,1,0:T(8,128)(2,1)} %pad_maximum_fusion.43), channel_id=1, source_target_pairs={{0,4},{2,6},{4,0},{6,2},{8,12},{10,14},{12,8},{14,10},{16,20},{18,... | collective-permute-start | bytes 884744 | tf_op jit(solution)/shard_map/ppermute | solution.py:45
  71.7 9.4 %collective-permute-start.22 = (bf16[2,1,1,1,48,1536]{5,4,3,2,1,0:T(8,128)(2,1)}, bf16[2,1,1,1,48,1536]{5,4,3,2,1,0:T(8,128)(2,1)S(1)}, u32[]{:S(2)}, u32[]{:S(2)}) collective-permute-start(bf16[2,1,1,1,48,1536]{5,4,3,2,1,0:T(8,128)(2,1)} %pad_maximum_fusion.44), channel_id=1, source_target_pairs={{0,2},{2,0},{4,6},{6,4},{8,10},{10,8},{12,14},{14,12},{16,18},{18,... | collective-permute-start | bytes 884744 | tf_op jit(solution)/shard_map/ppermute | solution.py:45
  86.6 18.7 %collective-permute-start.24 = (bf16[2,1,2,1,48,1536]{5,4,3,2,1,0:T(8,128)(2,1)}, bf16[2,1,2,1,48,1536]{5,4,3,2,1,0:T(8,128)(2,1)}, u32[]{:S(2)}, u32[]{:S(2)}) collective-permute-start(bf16[2,1,2,1,48,1536]{5,4,3,2,1,0:T(8,128)(2,1)} %pad_maximum_fusion.28), channel_id=1, source_target_pairs={{0,8},{2,10},{4,12},{6,14},{8,0},{10,2},{12,4},{14,6},{16,24},{18,... | collective-permute-start | bytes 1769480 | tf_op jit(solution)/shard_map/ppermute | solution.py:45
  88.6 16.7 %collective-permute-start.25 = (bf16[2,1,1,2,48,1536]{5,4,3,2,1,0:T(8,128)(2,1)}, bf16[2,1,1,2,48,1536]{5,4,3,2,1,0:T(8,128)(2,1)}, u32[]{:S(2)}, u32[]{:S(2)}) collective-permute-start(bf16[2,1,1,2,48,1536]{5,4,3,2,1,0:T(8,128)(2,1)} %pad_maximum_fusion.29), channel_id=1, source_target_pairs={{0,4},{2,6},{4,0},{6,2},{8,12},{10,14},{12,8},{14,10},{16,20},{18,... | collective-permute-start | bytes 1769480 | tf_op jit(solution)/shard_map/ppermute | solution.py:45
  89.7 15.6 %collective-permute-start.26 = (bf16[2,2,1,1,48,1536]{5,4,3,2,1,0:T(8,128)(2,1)}, bf16[2,2,1,1,48,1536]{5,4,3,2,1,0:T(8,128)(2,1)}, u32[]{:S(2)}, u32[]{:S(2)}) collective-permute-start(bf16[2,2,1,1,48,1536]{5,4,3,2,1,0:T(8,128)(2,1)} %pad_maximum_fusion.30), channel_id=1, source_target_pairs={{0,2},{2,0},{4,6},{6,4},{8,10},{10,8},{12,14},{14,12},{16,18},{18,... | collective-permute-start | bytes 1769480 | tf_op jit(solution)/shard_map/ppermute | solution.py:45
  92.4 19.2 %collective-permute-start.27 = (bf16[1,1,1,1,48,1536]{5,4,3,2,1,0:T(8,128)(2,1)}, bf16[1,1,1,1,48,1536]{5,4,3,2,1,0:T(8,128)(2,1)S(1)}, u32[]{:S(2)}, u32[]{:S(2)}) collective-permute-start(bf16[1,1,1,1,48,1536]{5,4,3,2,1,0:T(8,128)(2,1)} %get-tuple-element.247), channel_id=1, source_target_pairs={{0,16},{2,18},{4,20},{6,22},{8,24},{10,26},{12,28},{14,30},{16,0},... | collective-permute-start | bytes 442376 | tf_op jit(solution)/shard_map/ppermute | solution.py:45
  92.9 18.7 %collective-permute-start.28 = (bf16[1,1,1,1,48,1536]{5,4,3,2,1,0:T(8,128)(2,1)}, bf16[1,1,1,1,48,1536]{5,4,3,2,1,0:T(8,128)(2,1)S(1)}, u32[]{:S(2)}, u32[]{:S(2)}) collective-permute-start(bf16[1,1,1,1,48,1536]{5,4,3,2,1,0:T(8,128)(2,1)} %get-tuple-element.248), channel_id=1, source_target_pairs={{0,16},{2,18},{4,20},{6,22},{8,24},{10,26},{12,28},{14,30},{16,0},... | collective-permute-start | bytes 442376 | tf_op jit(solution)/shard_map/ppermute | solution.py:45
  120.5 29.1 %collective-permute-start.31 = (bf16[2,2,2,1,48,1536]{5,4,3,2,1,0:T(8,128)(2,1)}, bf16[2,2,2,1,48,1536]{5,4,3,2,1,0:T(8,128)(2,1)S(1)}, u32[]{:S(2)}, u32[]{:S(2)}) collective-permute-start(bf16[2,2,2,1,48,1536]{5,4,3,2,1,0:T(8,128)(2,1)} %pad_maximum_fusion.12), channel_id=1, source_target_pairs={{0,2},{2,0},{4,6},{6,4},{8,10},{10,8},{12,14},{14,12},{16,18},{18,... | collective-permute-start | bytes 3538952 | tf_op jit(solution)/shard_map/ppermute | solution.py:45
  121.9 28.4 %collective-permute-start.32 = (bf16[2,1,2,2,48,1536]{5,4,3,2,1,0:T(8,128)(2,1)}, bf16[2,1,2,2,48,1536]{5,4,3,2,1,0:T(8,128)(2,1)}, u32[]{:S(2)}, u32[]{:S(2)}) collective-permute-start(bf16[2,1,2,2,48,1536]{5,4,3,2,1,0:T(8,128)(2,1)} %pad_maximum_fusion.13), channel_id=1, source_target_pairs={{0,8},{2,10},{4,12},{6,14},{8,0},{10,2},{12,4},{14,6},{16,24},{18,... | collective-permute-start | bytes 3538952 | tf_op jit(solution)/shard_map/ppermute | solution.py:45
  122.0 28.9 %collective-permute-start.33 = (bf16[2,2,1,2,48,1536]{5,4,3,2,1,0:T(8,128)(2,1)S(1)}, bf16[2,2,1,2,48,1536]{5,4,3,2,1,0:T(8,128)(2,1)}, u32[]{:S(2)}, u32[]{:S(2)}) collective-permute-start(bf16[2,2,1,2,48,1536]{5,4,3,2,1,0:T(8,128)(2,1)S(1)} %pad_maximum_fusion.14), channel_id=1, source_target_pairs={{0,4},{2,6},{4,0},{6,2},{8,12},{10,14},{12,8},{14,10},{16,20},{18,... | collective-permute-start | bytes 3538952 | tf_op jit(solution)/shard_map/ppermute | solution.py:45
  130.7 37.6 %collective-permute-start.34 = (bf16[2,1,1,1,48,1536]{5,4,3,2,1,0:T(8,128)(2,1)S(1)}, bf16[2,1,1,1,48,1536]{5,4,3,2,1,0:T(8,128)(2,1)}, u32[]{:S(2)}, u32[]{:S(2)}) collective-permute-start(bf16[2,1,1,1,48,1536]{5,4,3,2,1,0:T(8,128)(2,1)S(1)} %copy-done.16), channel_id=1, source_target_pairs={{0,4},{2,6},{4,0},{6,2},{8,12},{10,14},{12,8},{14,10},{16,20},{18,... | collective-permute-start | bytes 884744 | tf_op jit(solution)/shard_map/ppermute | solution.py:45
  131.8 36.5 %collective-permute-start.35 = (bf16[2,1,1,1,48,1536]{5,4,3,2,1,0:T(8,128)(2,1)S(1)}, bf16[2,1,1,1,48,1536]{5,4,3,2,1,0:T(8,128)(2,1)}, u32[]{:S(2)}, u32[]{:S(2)}) collective-permute-start(bf16[2,1,1,1,48,1536]{5,4,3,2,1,0:T(8,128)(2,1)S(1)} %copy-done.17), channel_id=1, source_target_pairs={{0,2},{2,0},{4,6},{6,4},{8,10},{10,8},{12,14},{14,12},{16,18},{18,... | collective-permute-start | bytes 884744 | tf_op jit(solution)/shard_map/ppermute | solution.py:45
  174.4 14.1 %collective-permute-start.37 = (bf16[2,1,2,1,48,1536]{5,4,3,2,1,0:T(8,128)(2,1)S(1)}, bf16[2,1,2,1,48,1536]{5,4,3,2,1,0:T(8,128)(2,1)S(1)}, u32[]{:S(2)}, u32[]{:S(2)}) collective-permute-start(bf16[2,1,2,1,48,1536]{5,4,3,2,1,0:T(8,128)(2,1)S(1)} %pad_maximum_fusion.32), channel_id=1, source_target_pairs={{0,8},{2,10},{4,12},{6,14},{8,0},{10,2},{12,4},{14,6},{16,24},{18,... | collective-permute-start | bytes 1769480 | tf_op jit(solution)/shard_map/ppermute | solution.py:45
  176.4 12.9 %collective-permute-start.38 = (bf16[2,1,1,2,48,1536]{5,4,3,2,1,0:T(8,128)(2,1)S(1)}, bf16[2,1,1,2,48,1536]{5,4,3,2,1,0:T(8,128)(2,1)S(1)}, u32[]{:S(2)}, u32[]{:S(2)}) collective-permute-start(bf16[2,1,1,2,48,1536]{5,4,3,2,1,0:T(8,128)(2,1)S(1)} %pad_maximum_fusion.33), channel_id=1, source_target_pairs={{0,4},{2,6},{4,0},{6,2},{8,12},{10,14},{12,8},{14,10},{16,20},{18,... | collective-permute-start | bytes 1769480 | tf_op jit(solution)/shard_map/ppermute | solution.py:45
  194.9 30.3 %collective-permute-start.43 = (bf16[2,2,2,1,48,1536]{5,4,3,2,1,0:T(8,128)(2,1)}, bf16[2,2,2,1,48,1536]{5,4,3,2,1,0:T(8,128)(2,1)S(1)}, u32[]{:S(2)}, u32[]{:S(2)}) collective-permute-start(bf16[2,2,2,1,48,1536]{5,4,3,2,1,0:T(8,128)(2,1)} %pad_maximum_fusion.15), channel_id=1, source_target_pairs={{0,2},{2,0},{4,6},{6,4},{8,10},{10,8},{12,14},{14,12},{16,18},{18,... | collective-permute-start | bytes 3538952 | tf_op jit(solution)/shard_map/ppermute | solution.py:45
  195.5 29.7 %collective-permute-start.44 = (bf16[2,1,2,2,48,1536]{5,4,3,2,1,0:T(8,128)(2,1)}, bf16[2,1,2,2,48,1536]{5,4,3,2,1,0:T(8,128)(2,1)S(1)}, u32[]{:S(2)}, u32[]{:S(2)}) collective-permute-start(bf16[2,1,2,2,48,1536]{5,4,3,2,1,0:T(8,128)(2,1)} %pad_maximum_fusion.16), channel_id=1, source_target_pairs={{0,8},{2,10},{4,12},{6,14},{8,0},{10,2},{12,4},{14,6},{16,24},{18,... | collective-permute-start | bytes 3538952 | tf_op jit(solution)/shard_map/ppermute | solution.py:45
  233.3 8.3 %collective-permute-start.45 = (f32[16,768]{1,0:T(8,128)}, f32[16,768]{1,0:T(8,128)S(1)}, u32[]{:S(2)}, u32[]{:S(2)}) collective-permute-start(f32[16,768]{1,0:T(8,128)} %get-tuple-element.280), channel_id=1, source_target_pairs={{0,1},{1,0},{2,3},{3,2},{4,5},{5,4},{6,7},{7,6},{8,9},{9,8},{10,11... | collective-permute-start | bytes 147464 | tf_op jit(solution)/shard_map/ppermute | solution.py:49
  238.9 37.0 %collective-permute-start.50 = (bf16[2,2,2,1,48,1536]{5,4,3,2,1,0:T(8,128)(2,1)}, bf16[2,2,2,1,48,1536]{5,4,3,2,1,0:T(8,128)(2,1)}, u32[]{:S(2)}, u32[]{:S(2)}) collective-permute-start(bf16[2,2,2,1,48,1536]{5,4,3,2,1,0:T(8,128)(2,1)} %slice.999), channel_id=1, source_target_pairs={{0,2},{2,0},{4,6},{6,4},{8,10},{10,8},{12,14},{14,12},{16,18},{18,... | collective-permute-start | bytes 3538952 | tf_op jit(solution)/shard_map/ppermute | solution.py:45
  240.4 35.6 %collective-permute-start.51 = (bf16[2,1,2,2,48,1536]{5,4,3,2,1,0:T(8,128)(2,1)}, bf16[2,1,2,2,48,1536]{5,4,3,2,1,0:T(8,128)(2,1)}, u32[]{:S(2)}, u32[]{:S(2)}) collective-permute-start(bf16[2,1,2,2,48,1536]{5,4,3,2,1,0:T(8,128)(2,1)} %slice.1000), channel_id=1, source_target_pairs={{0,8},{2,10},{4,12},{6,14},{8,0},{10,2},{12,4},{14,6},{16,24},{18,... | collective-permute-start | bytes 3538952 | tf_op jit(solution)/shard_map/ppermute | solution.py:45
  289.2 9.6 %collective-permute-start.52 = (bf16[1,1,1,1,8,7680]{5,4,3,2,1,0:T(8,128)(2,1)}, bf16[1,1,1,1,8,7680]{5,4,3,2,1,0:T(8,128)(2,1)S(1)}, u32[]{:S(2)}, u32[]{:S(2)}) collective-permute-start(bf16[1,1,1,1,8,7680]{5,4,3,2,1,0:T(8,128)(2,1)} %bitcast.50), channel_id=1, source_target_pairs={{0,16},{2,18},{4,20},{6,22},{8,24},{10,26},{12,28},{14,30},{16,0},... | collective-permute-start | bytes 368648 | tf_op jit(solution)/shard_map/ppermute | solution.py:45
  290.9 23.2 %collective-permute-start.54 = (bf16[2,1,2,1,48,1536]{5,4,3,2,1,0:T(8,128)(2,1)}, bf16[2,1,2,1,48,1536]{5,4,3,2,1,0:T(8,128)(2,1)}, u32[]{:S(2)}, u32[]{:S(2)}) collective-permute-start(bf16[2,1,2,1,48,1536]{5,4,3,2,1,0:T(8,128)(2,1)} %get-tuple-element.304), channel_id=1, source_target_pairs={{0,8},{2,10},{4,12},{6,14},{8,0},{10,2},{12,4},{14,6},{16,24},{18,... | collective-permute-start | bytes 1769480 | tf_op jit(solution)/shard_map/ppermute | solution.py:45
  292.2 21.9 %collective-permute-start.55 = (bf16[2,1,1,2,48,1536]{5,4,3,2,1,0:T(8,128)(2,1)}, bf16[2,1,1,2,48,1536]{5,4,3,2,1,0:T(8,128)(2,1)}, u32[]{:S(2)}, u32[]{:S(2)}) collective-permute-start(bf16[2,1,1,2,48,1536]{5,4,3,2,1,0:T(8,128)(2,1)} %get-tuple-element.305), channel_id=1, source_target_pairs={{0,4},{2,6},{4,0},{6,2},{8,12},{10,14},{12,8},{14,10},{16,20},{18,... | collective-permute-start | bytes 1769480 | tf_op jit(solution)/shard_map/ppermute | solution.py:45
  302.9 11.3 %collective-permute-start.56 = (bf16[2,1,1,1,8,7680]{5,4,3,2,1,0:T(8,128)(2,1)S(1)}, bf16[2,1,1,1,8,7680]{5,4,3,2,1,0:T(8,128)(2,1)S(1)}, u32[]{:S(2)}, u32[]{:S(2)}) collective-permute-start(bf16[2,1,1,1,8,7680]{5,4,3,2,1,0:T(8,128)(2,1)S(1)} %pad_maximum_fusion.48), channel_id=1, source_target_pairs={{0,8},{2,10},{4,12},{6,14},{8,0},{10,2},{12,4},{14,6},{16,24},{18,... | collective-permute-start | bytes 737288 | tf_op jit(solution)/shard_map/ppermute | solution.py:45
  335.8 11.8 %collective-permute-start.58 = (f32[2,768]{1,0:T(2,128)S(1)}, f32[2,768]{1,0:T(2,128)S(1)}, u32[]{:S(2)}, u32[]{:S(2)}) collective-permute-start(f32[2,768]{1,0:T(2,128)S(1)} %pad_maximum_fusion.64), channel_id=1, source_target_pairs={{0,1},{1,0},{2,3},{3,2},{4,5},{5,4},{6,7},{7,6},{8,9},{9,8},{10,11... | collective-permute-start | bytes 18440 | tf_op jit(solution)/shard_map/ppermute | solution.py:49
  335.9 17.8 %collective-permute-start.61 = (bf16[1,1,1,1,8,5760]{5,4,3,2,1,0:T(8,128)(2,1)}, bf16[1,1,1,1,8,5760]{5,4,3,2,1,0:T(8,128)(2,1)}, u32[]{:S(2)}, u32[]{:S(2)}) collective-permute-start(bf16[1,1,1,1,8,5760]{5,4,3,2,1,0:T(8,128)(2,1)} %bitcast.63), channel_id=1, source_target_pairs={{0,16},{2,18},{4,20},{6,22},{8,24},{10,26},{12,28},{14,30},{16,0},... | collective-permute-start | bytes 276488 | tf_op jit(solution)/shard_map/ppermute | solution.py:45
  342.0 13.5 %collective-permute-start.59 = (bf16[2,1,1,1,48,1536]{5,4,3,2,1,0:T(8,128)(2,1)}, bf16[2,1,1,1,48,1536]{5,4,3,2,1,0:T(8,128)(2,1)}, u32[]{:S(2)}, u32[]{:S(2)}) collective-permute-start(bf16[2,1,1,1,48,1536]{5,4,3,2,1,0:T(8,128)(2,1)} %get-tuple-element.323), channel_id=1, source_target_pairs={{0,4},{2,6},{4,0},{6,2},{8,12},{10,14},{12,8},{14,10},{16,20},{18,... | collective-permute-start | bytes 884744 | tf_op jit(solution)/shard_map/ppermute | solution.py:45
  343.0 13.6 %collective-permute-start.60 = (bf16[2,1,1,1,48,1536]{5,4,3,2,1,0:T(8,128)(2,1)}, bf16[2,1,1,1,48,1536]{5,4,3,2,1,0:T(8,128)(2,1)}, u32[]{:S(2)}, u32[]{:S(2)}) collective-permute-start(bf16[2,1,1,1,48,1536]{5,4,3,2,1,0:T(8,128)(2,1)} %get-tuple-element.324), channel_id=1, source_target_pairs={{0,2},{2,0},{4,6},{6,4},{8,10},{10,8},{12,14},{14,12},{16,18},{18,... | collective-permute-start | bytes 884744 | tf_op jit(solution)/shard_map/ppermute | solution.py:45
  343.6 28.5 %collective-permute-start.65 = (bf16[2,2,1,1,8,7680]{5,4,3,2,1,0:T(8,128)(2,1)S(1)}, bf16[2,2,1,1,8,7680]{5,4,3,2,1,0:T(8,128)(2,1)}, u32[]{:S(2)}, u32[]{:S(2)}) collective-permute-start(bf16[2,2,1,1,8,7680]{5,4,3,2,1,0:T(8,128)(2,1)S(1)} %pad_maximum_fusion.34), channel_id=1, source_target_pairs={{0,2},{2,0},{4,6},{6,4},{8,10},{10,8},{12,14},{14,12},{16,18},{18,... | collective-permute-start | bytes 1474568 | tf_op jit(solution)/shard_map/ppermute | solution.py:45
  353.0 18.0 %collective-permute-start.63 = (bf16[2,2,2,1,48,512]{5,4,3,2,1,0:T(8,128)(2,1)}, bf16[2,2,2,1,48,512]{5,4,3,2,1,0:T(8,128)(2,1)S(1)}, u32[]{:S(2)}, u32[]{:S(2)}) collective-permute-start(bf16[2,2,2,1,48,512]{5,4,3,2,1,0:T(8,128)(2,1)} %pad_maximum_fusion.40), channel_id=1, source_target_pairs={{0,2},{2,0},{4,6},{6,4},{8,10},{10,8},{12,14},{14,12},{16,18},{18,... | collective-permute-start | bytes 1179656 | tf_op jit(solution)/shard_map/ppermute | solution.py:45
  353.7 18.4 %collective-permute-start.64 = (bf16[2,1,2,2,48,512]{5,4,3,2,1,0:T(8,128)(2,1)S(1)}, bf16[2,1,2,2,48,512]{5,4,3,2,1,0:T(8,128)(2,1)S(1)}, u32[]{:S(2)}, u32[]{:S(2)}) collective-permute-start(bf16[2,1,2,2,48,512]{5,4,3,2,1,0:T(8,128)(2,1)S(1)} %copy-done.32), channel_id=1, source_target_pairs={{0,8},{2,10},{4,12},{6,14},{8,0},{10,2},{12,4},{14,6},{16,24},{18,... | collective-permute-start | bytes 1179656 | tf_op jit(solution)/shard_map/ppermute | solution.py:45
  355.5 16.6 %collective-permute-start.62 = (bf16[2,2,1,2,48,640]{5,4,3,2,1,0:T(8,128)(2,1)S(1)}, bf16[2,2,1,2,48,640]{5,4,3,2,1,0:T(8,128)(2,1)S(1)}, u32[]{:S(2)}, u32[]{:S(2)}) collective-permute-start(bf16[2,2,1,2,48,640]{5,4,3,2,1,0:T(8,128)(2,1)S(1)} %pad_maximum_fusion.35), channel_id=1, source_target_pairs={{0,4},{2,6},{4,0},{6,2},{8,12},{10,14},{12,8},{14,10},{16,20},{18,... | collective-permute-start | bytes 1474568 | tf_op jit(solution)/shard_map/ppermute | solution.py:45
  361.0 38.0 %collective-permute-start.77 = (bf16[1,1,1,1,48,1536]{5,4,3,2,1,0:T(8,128)(2,1)S(1)}, bf16[1,1,1,1,48,1536]{5,4,3,2,1,0:T(8,128)(2,1)S(1)}, u32[]{:S(2)}, u32[]{:S(2)}) collective-permute-start(bf16[1,1,1,1,48,1536]{5,4,3,2,1,0:T(8,128)(2,1)S(1)} %get-tuple-element.363), channel_id=1, source_target_pairs={{0,16},{2,18},{4,20},{6,22},{8,24},{10,26},{12,28},{14,30},{16,0},... | collective-permute-start | bytes 442376 | tf_op jit(solution)/shard_map/ppermute | solution.py:45
  372.5 8.0 %collective-permute-start.69 = (bf16[2,1,2,1,48,512]{5,4,3,2,1,0:T(8,128)(2,1)S(1)}, bf16[2,1,2,1,48,512]{5,4,3,2,1,0:T(8,128)(2,1)S(1)}, u32[]{:S(2)}, u32[]{:S(2)}) collective-permute-start(bf16[2,1,2,1,48,512]{5,4,3,2,1,0:T(8,128)(2,1)S(1)} %get-tuple-element.349), channel_id=1, source_target_pairs={{0,8},{2,10},{4,12},{6,14},{8,0},{10,2},{12,4},{14,6},{16,24},{18,... | collective-permute-start | bytes 589832 | tf_op jit(solution)/shard_map/ppermute | solution.py:45
  377.8 9.4 %collective-permute-start.80 = (bf16[2,1,2,1,8,5760]{5,4,3,2,1,0:T(8,128)(2,1)S(1)}, bf16[2,1,2,1,8,5760]{5,4,3,2,1,0:T(8,128)(2,1)S(1)}, u32[]{:S(2)}, u32[]{:S(2)}) collective-permute-start(bf16[2,1,2,1,8,5760]{5,4,3,2,1,0:T(8,128)(2,1)S(1)} %pad_maximum_fusion.42), channel_id=1, source_target_pairs={{0,8},{2,10},{4,12},{6,14},{8,0},{10,2},{12,4},{14,6},{16,24},{18,... | collective-permute-start | bytes 1105928 | tf_op jit(solution)/shard_map/ppermute | solution.py:45
  380.5 15.0 %collective-permute-start.67 = (bf16[512,768]{1,0:T(8,128)(2,1)S(1)}, bf16[512,768]{1,0:T(8,128)(2,1)S(1)}, u32[]{:S(2)}, u32[]{:S(2)}) collective-permute-start(bf16[512,768]{1,0:T(8,128)(2,1)S(1)} %slice.896), channel_id=1, source_target_pairs={{0,1},{1,0},{2,3},{3,2},{4,5},{5,4},{6,7},{7,6},{8,9},{9,8},{10,11... | collective-permute-start | bytes 2359304 | tf_op jit(solution)/shard_map/ppermute | solution.py:49
  389.6 10.6 %collective-permute-start.78 = (bf16[1,1,1,1,48,1536]{5,4,3,2,1,0:T(8,128)(2,1)S(1)}, bf16[1,1,1,1,48,1536]{5,4,3,2,1,0:T(8,128)(2,1)S(1)}, u32[]{:S(2)}, u32[]{:S(2)}) collective-permute-start(bf16[1,1,1,1,48,1536]{5,4,3,2,1,0:T(8,128)(2,1)S(1)} %get-tuple-element.364), channel_id=1, source_target_pairs={{0,16},{2,18},{4,20},{6,22},{8,24},{10,26},{12,28},{14,30},{16,0},... | collective-permute-start | bytes 442376 | tf_op jit(solution)/shard_map/ppermute | solution.py:45
  390.1 19.4 %collective-permute-start.79 = (bf16[2,2,1,2,8,7680]{5,4,3,2,1,0:T(8,128)(2,1)S(1)}, bf16[2,2,1,2,8,7680]{5,4,3,2,1,0:T(8,128)(2,1)S(1)}, u32[]{:S(2)}, u32[]{:S(2)}) collective-permute-start(bf16[2,2,1,2,8,7680]{5,4,3,2,1,0:T(8,128)(2,1)S(1)} %pad_maximum_fusion.21), channel_id=1, source_target_pairs={{0,4},{2,6},{4,0},{6,2},{8,12},{10,14},{12,8},{14,10},{16,20},{18,... | collective-permute-start | bytes 2949128 | tf_op jit(solution)/shard_map/ppermute | solution.py:45
  393.1 16.5 %collective-permute-start.81 = (bf16[2,2,2,1,8,5760]{5,4,3,2,1,0:T(8,128)(2,1)S(1)}, bf16[2,2,2,1,8,5760]{5,4,3,2,1,0:T(8,128)(2,1)S(1)}, u32[]{:S(2)}, u32[]{:S(2)}) collective-permute-start(bf16[2,2,2,1,8,5760]{5,4,3,2,1,0:T(8,128)(2,1)S(1)} %pad_maximum_fusion.25), channel_id=1, source_target_pairs={{0,2},{2,0},{4,6},{6,4},{8,10},{10,8},{12,14},{14,12},{16,18},{18,... | collective-permute-start | bytes 2211848 | tf_op jit(solution)/shard_map/ppermute | solution.py:45
  395.5 8.5 %collective-permute-start.75 = (bf16[1,1,1,1,48,512]{5,4,3,2,1,0:T(8,128)(2,1)S(1)}, bf16[1,1,1,1,48,512]{5,4,3,2,1,0:T(8,128)(2,1)S(1)}, u32[]{:S(2)}, u32[]{:S(2)}) collective-permute-start(bf16[1,1,1,1,48,512]{5,4,3,2,1,0:T(8,128)(2,1)S(1)} %get-tuple-element.361), channel_id=1, source_target_pairs={{0,16},{2,18},{4,20},{6,22},{8,24},{10,26},{12,28},{14,30},{16,0},... | collective-permute-start | bytes 147464 | tf_op jit(solution)/shard_map/ppermute | solution.py:45
  (191 other events, 1543.6 us)
